TPU v7x, 32 devices: a whole 2x2x4 slice. The times are simulated.
32 devices in a mesh: dp: 4 (over x, core), row: 2 (over y), col: 4 (over z).
Axes of the slice: x: 2, y: 2, z: 4, core: 2. Of those that a mesh axis runs over, the one named last changes fastest.
Arguments:
- tokens: bfloat16 [4096, 2048], P(('dp', 'row'), 'col'), may hold values from -6 to 6
- parent: int32 [4, 4], P('dp'), may hold values from -1 to 1, as said below
- depth: int32 [4, 4], P('dp'), may hold values from 0 to 2, as said below
- w_qkv: float32 [2048, 6144], P('row', 'col'), may hold values from -0.125 to 0.125
- b_qkv: float32 [6144], P('col'), may hold values from -3 to 3
- w_out: float32 [2048, 2048], P('col', 'row'), may hold values from -0.75 to 0.75
- w_up: float32 [2048, 8192], P('row', 'col'), may hold values from -0.125 to 0.125
- b_up: float32 [8192], P('col'), may hold values from -3 to 3
- w_down: float32 [8192, 2048], P('col', 'row'), may hold values from -0.0625 to 0.0625
- b_res: float32 [2048], P('col'), may hold values from -3 to 3
- ln_gain: float32 [2048], replicated, may hold values from 0.5 to 1.5
- ln_bias: float32 [2048], replicated, may hold values from -2 to 2
- cotangent: bfloat16 [4096, 2048], P(('dp', 'row'), 'col'), may hold values from -6 to 6
Outputs:
- output: bfloat16 [4096, 2048], P(('dp', 'row'), 'col')
- tokens_grad: float32 [4096, 2048], P(('dp', 'row'), 'col')
- w_qkv_grad: float32 [2048, 6144], P('row', 'col')
- b_qkv_grad: float32 [6144], P('col')
- w_out_grad: float32 [2048, 2048], P('col', 'row')
- w_up_grad: float32 [2048, 8192], P('row', 'col')
- b_up_grad: float32 [8192], P('col')
- w_down_grad: float32 [8192, 2048], P('col', 'row')
- b_res_grad: float32 [2048], P('col')
- ln_gain_grad: float32 [2048], replicated
- ln_bias_grad: float32 [2048], replicated
Inputs may be any that keep to these rules, and one draw needn't show every extreme that they name: In every tree segments 0 to 1 form a trunk: segment 0 has parent -1 and each other trunk segment j has parent j - 1. Every later segment has a trunk segment as parent, and the last segment's parent is trunk segment 4 // 2 - 1. Segment 0 has depth 0 and every other segment one more than its parent.
All inputs are finite; a program needn't handle non-finite values.
Results may differ from a plain program's by a relative error of at most 0.018.
Values may be sent and summed in bfloat16 or wider, within the bound.
No kernel may reach another device: no remote copies, remote signals or barrier semaphores. Data moves between devices by JAX's collectives and lax.ppermute only.
A program may use at most 256 MiB of HBM per device.

v0:
```python
import functools
import math

import jax
import jax.numpy as jnp
from jax import lax
from jax.sharding import PartitionSpec as P

HD = 64
ROT = 32
SEG = 256


norm_epsilon = 1e-05
masked_fill = -1e30
rotary_base = 10000.0


def precise_dot(left, right):
    return jnp.dot(left, right, precision=lax.Precision.HIGHEST, preferred_element_type=jnp.float32)


def ancestry(parent_row):
    seg_count = parent_row.shape[0]
    labels = jnp.arange(seg_count, dtype=jnp.int32)
    identity = jnp.eye(seg_count, dtype=jnp.float32)
    parent_hot = (parent_row[:, None] == labels[None, :]).astype(jnp.float32)

    def extend(rounds, reachable):
        return jnp.minimum(identity + precise_dot(parent_hot, reachable), 1.0)

    return lax.fori_loop(0, seg_count, extend, identity)


def rotate(values, cosines, sines):
    half_rot = ROT // 2
    former = values[..., :half_rot]
    latter = values[..., half_rot:ROT]
    return jnp.concatenate(
        [former * cosines - latter * sines, latter * cosines + former * sines, values[..., ROT:]],
        axis=-1,
    )


def angles_of(positions):
    frequency = jnp.exp(
        -math.log(rotary_base) * 2.0 * jnp.arange(ROT // 2, dtype=jnp.float32) / ROT
    )
    phase_angle = positions[:, None] * frequency[None, :]
    return (jnp.cos(phase_angle)[:, None, :], jnp.sin(phase_angle)[:, None, :])


def reorder_rows(gradient, row_count, dp_count):
    leading = gradient.shape[0]
    blocked = gradient.reshape(
        row_count, dp_count, leading // (row_count * dp_count), gradient.shape[1]
    )
    return jnp.transpose(blocked, (1, 0, 2, 3)).reshape(leading, gradient.shape[1])


def reorder_cols(gradient, row_count, dp_count):
    trailing = gradient.shape[1]
    blocked = gradient.reshape(
        gradient.shape[0], row_count, dp_count, trailing // (row_count * dp_count)
    )
    return jnp.transpose(blocked, (0, 2, 1, 3)).reshape(gradient.shape[0], trailing)


def per_device(
    tokens,
    parent,
    depth,
    w_qkv,
    b_qkv,
    w_out,
    w_up,
    b_up,
    w_down,
    b_res,
    ln_gain,
    ln_bias,
    cotangent,
):
    tok_rows = tokens.shape[0]
    col_width = tokens.shape[1]
    row_count = lax.axis_size("row")
    dp_count = lax.axis_size("dp")
    row_start = lax.axis_index("row") * tok_rows
    local_heads = w_out.shape[0] // HD
    seg_count = parent.shape[1]
    labels = jnp.arange(seg_count, dtype=jnp.int32)
    reachable = ancestry(parent[0])
    query_index = row_start + jnp.arange(tok_rows, dtype=jnp.int32)
    query_seg = query_index // SEG
    query_hot = (query_seg[:, None] == labels[None, :]).astype(jnp.float32)
    query_reach = precise_dot(query_hot, reachable)
    levels = precise_dot(query_hot, depth[0].astype(jnp.float32)[:, None])[:, 0]
    positions = levels * SEG + (query_index % SEG).astype(jnp.float32)
    cosines, sines = angles_of(positions)
    score_scale = HD ** (-0.5)

    def permit(key_len):
        key_index = jnp.arange(key_len, dtype=jnp.int32)
        key_seg = key_index // SEG
        key_hot = (key_seg[:, None] == labels[None, :]).astype(jnp.float32)
        linked = precise_dot(query_reach, key_hot.T) > 0.5
        return linked & (
            (query_seg[:, None] != key_seg[None, :]) | (query_index[:, None] >= key_index[None, :])
        )

    whole = lax.all_gather(tokens, "col", axis=1, tiled=True).astype(jnp.float32)
    centred = whole - jnp.mean(whole, axis=1, keepdims=True)
    inv_scale = lax.rsqrt(jnp.mean(centred * centred, axis=1, keepdims=True) + norm_epsilon)
    normal = centred * inv_scale
    normed = (normal * ln_gain + ln_bias).astype(jnp.bfloat16)
    qkv_full, up_full, out_full, down_full = (
        lax.all_gather(w_qkv.astype(jnp.bfloat16), "row", axis=0, tiled=True),
        lax.all_gather(w_up.astype(jnp.bfloat16), "row", axis=0, tiled=True),
        lax.all_gather(w_out.astype(jnp.bfloat16), "row", axis=1, tiled=True),
        lax.all_gather(w_down.astype(jnp.bfloat16), "row", axis=1, tiled=True),
    )
    mixed = (jnp.dot(normed, qkv_full, preferred_element_type=jnp.float32) + b_qkv).reshape(
        tok_rows, local_heads, 3, HD
    )

    def rotate_pair(query_pre, key_pre):
        return (rotate(query_pre, cosines, sines), rotate(key_pre, cosines, sines))

    rotated, rotate_back = jax.vjp(rotate_pair, mixed[:, :, 0], mixed[:, :, 1])
    queries = rotated[0].astype(jnp.bfloat16)
    key_rows = rotated[1].astype(jnp.bfloat16)
    value_rows = mixed[:, :, 2].astype(jnp.bfloat16)
    key_flat = key_rows.reshape(tok_rows, local_heads * HD)
    value_flat = value_rows.reshape(tok_rows, local_heads * HD)

    def scores_for(key_part):
        raw_scores = (
            jnp.einsum("qhe,khe->hqk", queries, key_part, preferred_element_type=jnp.float32)
            * score_scale
        )
        allowed = permit(key_part.shape[0])
        return (jnp.where(allowed[None], raw_scores, masked_fill), allowed)

    pieces = (
        lax.all_gather(key_flat, "row", axis=0, tiled=True),
        lax.all_gather(value_flat, "row", axis=0, tiled=True),
    )
    running_top = jnp.full((local_heads, tok_rows), masked_fill, jnp.float32)
    key_len = pieces[0].shape[0]
    key_part = pieces[0].reshape(key_len, local_heads, HD)
    value_part = pieces[1].reshape(key_len, local_heads, HD)
    scores, allowed = scores_for(key_part)
    new_top = jnp.maximum(running_top, jnp.max(scores, axis=2))
    exponent = jnp.where(allowed[None], jnp.exp(scores - new_top[:, :, None]), 0.0)
    running_sum = jnp.sum(exponent, axis=2)
    weighted = jnp.einsum(
        "hqk,khe->hqe",
        exponent.astype(jnp.bfloat16),
        value_part,
        preferred_element_type=jnp.float32,
    )
    running_top, running_sum, weighted = (new_top, running_sum, weighted)
    log_total = running_top + jnp.log(running_sum)
    attn_exact = weighted / running_sum[:, :, None]
    attended = (
        jnp.transpose(attn_exact, (1, 0, 2))
        .reshape(tok_rows, local_heads * HD)
        .astype(jnp.bfloat16)
    )
    hidden_up = jnp.dot(normed, up_full, preferred_element_type=jnp.float32) + b_up
    activated, gelu_back = jax.vjp(functools.partial(jax.nn.gelu, approximate=True), hidden_up)
    activated = activated.astype(jnp.bfloat16)
    branch_terms = jnp.dot(attended, out_full, preferred_element_type=jnp.float32) + jnp.dot(
        activated, down_full, preferred_element_type=jnp.float32
    )
    branch = lax.psum_scatter(
        branch_terms.astype(jnp.bfloat16), "col", scatter_dimension=1, tiled=True
    ).astype(jnp.float32)
    output = (tokens.astype(jnp.float32) + branch + b_res).astype(jnp.bfloat16)
    grad_full = lax.all_gather(cotangent, "col", axis=1, tiled=True)
    res_bias_grad = jnp.sum(cotangent.astype(jnp.float32), axis=0)
    down_grad = jnp.einsum("tf,td->fd", activated, grad_full, preferred_element_type=jnp.float32)
    out_grad = jnp.einsum("te,td->ed", attended, grad_full, preferred_element_type=jnp.float32)
    act_grad = jnp.einsum("td,fd->tf", grad_full, down_full, preferred_element_type=jnp.float32)
    up_grad = gelu_back(act_grad)[0].astype(jnp.bfloat16)
    attn_grad = jnp.einsum(
        "td,ed->te", grad_full, out_full, preferred_element_type=jnp.float32
    ).astype(jnp.bfloat16)
    up_bias_grad = jnp.sum(up_grad.astype(jnp.float32), axis=0)
    up_weight_grad = jnp.einsum("td,tf->df", normed, up_grad, preferred_element_type=jnp.float32)
    out_heads = attn_grad.reshape(tok_rows, local_heads, HD)
    delta_sum = jnp.einsum("qhe,hqe->hq", out_heads.astype(jnp.float32), attn_exact)
    pieces = (
        lax.all_gather(key_flat, "row", axis=0, tiled=True),
        lax.all_gather(value_flat, "row", axis=0, tiled=True),
    )
    key_len = pieces[0].shape[0]
    key_part = pieces[0].reshape(key_len, local_heads, HD)
    value_part = pieces[1].reshape(key_len, local_heads, HD)
    scores, allowed = scores_for(key_part)
    softmaxed = jnp.where(allowed[None], jnp.exp(scores - log_total[:, :, None]), 0.0)
    prob_grad = jnp.einsum(
        "qhe,khe->hqk", out_heads, value_part, preferred_element_type=jnp.float32
    )
    score_grad = (softmaxed * (prob_grad - delta_sum[:, :, None])).astype(jnp.bfloat16)
    query_grad = (
        jnp.einsum("hqk,khe->qhe", score_grad, key_part, preferred_element_type=jnp.float32)
        * score_scale
    )
    key_grad = (
        jnp.einsum("hqk,qhe->khe", score_grad, queries, preferred_element_type=jnp.float32)
        * score_scale
    )
    value_grad = jnp.einsum(
        "hqk,qhe->khe",
        softmaxed.astype(jnp.bfloat16),
        out_heads,
        preferred_element_type=jnp.float32,
    )
    stacked = jnp.stack([key_grad, value_grad], axis=1).reshape(key_len, 2 * local_heads * HD)
    pair_grad = stacked
    query_grad, pair_grad = (query_grad, pair_grad)
    own_pairs = (
        lax.psum_scatter(pair_grad.astype(jnp.bfloat16), "row", scatter_dimension=0, tiled=True)
        .astype(jnp.float32)
        .reshape(tok_rows, 2, local_heads, HD)
    )
    query_pre, key_pre = rotate_back((query_grad, own_pairs[:, 0]))
    mixed_grad = (
        jnp.stack([query_pre, key_pre, own_pairs[:, 1]], axis=2)
        .reshape(tok_rows, 3 * local_heads * HD)
        .astype(jnp.bfloat16)
    )
    qkv_bias_grad = jnp.sum(mixed_grad.astype(jnp.float32), axis=0)
    qkv_weight_grad = jnp.einsum(
        "td,tc->dc", normed, mixed_grad, preferred_element_type=jnp.float32
    )
    norm_part = jnp.einsum(
        "tc,dc->td", mixed_grad, qkv_full, preferred_element_type=jnp.float32
    ) + jnp.einsum("tf,df->td", up_grad, up_full, preferred_element_type=jnp.float32)
    norm_grad = lax.psum(norm_part.astype(jnp.bfloat16), "col").astype(jnp.float32)
    gain_grad = jnp.sum(norm_grad * normal, axis=0)
    shift_grad = jnp.sum(norm_grad, axis=0)
    scaled = norm_grad * ln_gain
    mean_scaled = jnp.mean(scaled, axis=1, keepdims=True)
    mean_mixed = jnp.mean(scaled * normal, axis=1, keepdims=True)
    col_start = lax.axis_index("col") * col_width
    scaled_share = lax.dynamic_slice_in_dim(scaled, col_start, col_width, 1)
    normal_share = lax.dynamic_slice_in_dim(normal, col_start, col_width, 1)
    tokens_grad = inv_scale * (
        scaled_share - mean_scaled - normal_share * mean_mixed
    ) + cotangent.astype(jnp.float32)
    qkv_bias_grad, up_bias_grad, res_bias_grad, gain_grad, shift_grad = (
        lax.psum(qkv_bias_grad.astype(jnp.bfloat16), ("dp", "row")).astype(jnp.float32),
        lax.psum(up_bias_grad.astype(jnp.bfloat16), ("dp", "row")).astype(jnp.float32),
        lax.psum(res_bias_grad.astype(jnp.bfloat16), ("dp", "row")).astype(jnp.float32),
        lax.psum(gain_grad.astype(jnp.bfloat16), ("dp", "row")).astype(jnp.float32),
        lax.psum(shift_grad.astype(jnp.bfloat16), ("dp", "row")).astype(jnp.float32),
    )
    pieces_now = (
        lax.psum_scatter(
            reorder_rows(qkv_weight_grad, row_count, dp_count).astype(jnp.bfloat16),
            ("dp", "row"),
            scatter_dimension=0,
            tiled=True,
        ).astype(jnp.float32),
        lax.psum_scatter(
            reorder_rows(up_weight_grad, row_count, dp_count).astype(jnp.bfloat16),
            ("dp", "row"),
            scatter_dimension=0,
            tiled=True,
        ).astype(jnp.float32),
        lax.psum_scatter(
            reorder_cols(out_grad, row_count, dp_count).astype(jnp.bfloat16),
            ("dp", "row"),
            scatter_dimension=1,
            tiled=True,
        ).astype(jnp.float32),
        lax.psum_scatter(
            reorder_cols(down_grad, row_count, dp_count).astype(jnp.bfloat16),
            ("dp", "row"),
            scatter_dimension=1,
            tiled=True,
        ).astype(jnp.float32),
    )
    qkv_weight_grad, up_weight_grad, out_grad, down_grad = (
        lax.all_gather(pieces_now[0].astype(jnp.bfloat16), "dp", axis=0, tiled=True).astype(
            jnp.float32
        ),
        lax.all_gather(pieces_now[1].astype(jnp.bfloat16), "dp", axis=0, tiled=True).astype(
            jnp.float32
        ),
        lax.all_gather(pieces_now[2].astype(jnp.bfloat16), "dp", axis=1, tiled=True).astype(
            jnp.float32
        ),
        lax.all_gather(pieces_now[3].astype(jnp.bfloat16), "dp", axis=1, tiled=True).astype(
            jnp.float32
        ),
    )
    return (
        output,
        tokens_grad,
        qkv_weight_grad,
        qkv_bias_grad,
        out_grad,
        up_weight_grad,
        up_bias_grad,
        down_grad,
        res_bias_grad,
        gain_grad,
        shift_grad,
    )


def solution(mesh):
    return jax.shard_map(
        per_device,
        mesh=mesh,
        in_specs=(
            P(("dp", "row"), "col"),
            P("dp", None),
            P("dp", None),
            P("row", "col"),
            P("col"),
            P("col", "row"),
            P("row", "col"),
            P("col"),
            P("col", "row"),
            P("col"),
            P(),
            P(),
            P(("dp", "row"), "col"),
        ),
        out_specs=(
            P(("dp", "row"), "col"),
            P(("dp", "row"), "col"),
            P("row", "col"),
            P("col"),
            P("col", "row"),
            P("row", "col"),
            P("col"),
            P("col", "row"),
            P("col"),
            P(),
            P(),
        ),
        check_vma=False,
    )
```

profile of v0, /device:TPU:0, one launch (start us, length us, event | category | flops | bytes accessed | tf_op | source)
XLA Modules:
  0.0 1054.9 jit_solution(18216092555689512656)
XLA Ops:
  16.1 41.9 %all-gather.13.cloned.1.call-done = bf16[512,2048]{1,0:T(8,128)(2,1)} async-done(((bf16[512,512]{1,0:T(8,128)(2,1)}), bf16[512,2048]{1,0:T(8,128)(2,1)}) %all-gather.13.cloned.1.call-update) | async-done | bytes 2097168 | tf_op jit(solution)/shard_map/all_gather | solution.py:111
  62.4 76.9 %all-gather.15.cloned.1.call-done = bf16[2048,1536]{1,0:T(8,128)(2,1)} async-done(((bf16[1024,1536]{1,0:T(8,128)(2,1)}), bf16[2048,1536]{1,0:T(8,128)(2,1)}) %all-gather.15.cloned.1.call-update) | async-done | bytes 6291472 | tf_op jit(solution)/shard_map/all_gather | solution.py:117
  174.5 47.1 %all-gather.27.cloned.1.call-done = bf16[512,2048]{1,0:T(8,128)(2,1)} async-done(((bf16[512,512]{1,0:T(8,128)(2,1)}), bf16[512,2048]{1,0:T(8,128)(2,1)}) %all-gather.27.cloned.1.call-update) | async-done | bytes 2097168 | tf_op jit(solution)/shard_map/all_gather | solution.py:180
  227.0 16.7 %all-gather.17.cloned.1.call-done = bf16[1024,512]{0,1:T(8,128)(2,1)} async-done(((bf16[512,512]{0,1:T(8,128)(2,1)}), bf16[1024,512]{0,1:T(8,128)(2,1)}) %all-gather.17.cloned.1.call-update) | async-done | bytes 1048592 | tf_op jit(solution)/shard_map/all_gather | solution.py:145
  254.9 12.1 %all-gather.19.cloned.1.call-done = bf16[1024,512]{0,1:T(8,128)(2,1)} async-done(((bf16[512,512]{0,1:T(8,128)(2,1)}), bf16[1024,512]{0,1:T(8,128)(2,1)}) %all-gather.19.cloned.1.call-update) | async-done | bytes 1048592 | tf_op jit(solution)/shard_map/all_gather | solution.py:146
  280.0 9.9 multiply_convert_fusion
  307.6 65.6 %all-gather.23.cloned.1.call-done = bf16[2048,2048]{1,0:T(8,128)(2,1)} async-done(((bf16[1024,2048]{1,0:T(8,128)(2,1)}), bf16[2048,2048]{1,0:T(8,128)(2,1)}) %all-gather.23.cloned.1.call-update) | async-done | bytes 8388624 | tf_op jit(solution)/shard_map/all_gather | solution.py:118
  373.2 9.9 fusion.64
  383.0 96.3 %all-gather.25.cloned.1.call-done = bf16[2048,2048]{1,0:T(8,128)(2,1)} async-done(((bf16[2048,1024]{1,0:T(8,128)(2,1)}), bf16[2048,2048]{1,0:T(8,128)(2,1)}) %all-gather.25.cloned.1.call-update) | async-done | bytes 8388624 | tf_op jit(solution)/shard_map/all_gather | solution.py:120
  479.3 13.4 %fusion.65 = (bf16[2048]{0:T(1024)(128)(2,1)S(1)}, bf16[512,2048]{1,0:T(8,128)(2,1)}) fusion(f32[512,2048]{1,0:T(8,128)} %fusion.64, f32[2048]{0:T(1024)S(1)} %copy-done.29, bf16[512,2048]{1,0:T(8,128)(2,1)} %all-gather.27.cloned.1.call-done, bf16[2048,2048]{1,0:T(8,128)(2,1)} %all-gather.25.cloned.1.call-done), kind=kOutput, calls=%fused_computation.132 | convolution fusion | flops 4318033920 | bytes 16789504 | tf_op jit(solution)/shard_map/td,fd->tf/dot_general | solution.py:184
  492.7 21.3 %reduce-scatter.9.cloned.1.call-done = bf16[512,1024]{0,1:T(8,128)(2,1)} async-done(((bf16[1024,1024]{0,1:T(8,128)(2,1)}), bf16[512,1024]{0,1:T(8,128)(2,1)}) %reduce-scatter.9.cloned.1.call-update) | async-done | bytes 1048592 | tf_op jit(solution)/shard_map/reduce_scatter | solution.py:224
  556.4 11.0 %convolution_convert_fusion = bf16[2048,2048]{0,1:T(8,128)(2,1)} fusion(bf16[512,2048]{1,0:T(8,128)(2,1)} %all-gather.27.cloned.1.call-done, f32[512,2048]{1,0:T(8,128)} %fusion.64, f32[2048]{0:T(1024)S(1)} %copy-done.29), kind=kOutput, calls=%fused_computation.21 | convolution fusion | flops 4309647360 | bytes 14688256 | tf_op jit(solution)/shard_map/tf,td->fd/dot_general | solution.py:182
  567.4 21.7 %copy.57 = bf16[2048,4,2,256]{3,2,1,0:T(2,128)(2,1)} copy(bf16[2048,4,2,256]{0,3,1,2:T(8,128)(2,1)} %bitcast.110) | data formatting | bytes 16777216 | tf_op jit(solution)/shard_map/convert_element_type | solution.py:280
  589.2 14.4 %convert_element_type.255 = bf16[2048,2048]{1,0:T(8,128)(2,1)} reshape(bf16[2048,4,2,256]{3,2,1,0:T(2,128)(2,1)} %copy.57) | data formatting | bytes 16777216 | tf_op jit(solution)/shard_map/convert_element_type | solution.py:280
  603.7 13.1 %all-reduce.9.cloned.1.call-done = bf16[512,2048]{1,0:T(8,128)(2,1)} async-done(((bf16[512,2048]{1,0:T(8,128)(2,1)}), bf16[512,2048]{1,0:T(8,128)(2,1)}) %all-reduce.9.cloned.1.call-update) | async-done | bytes 2097168 | tf_op jit(solution)/shard_map/psum | solution.py:241
  634.6 25.6 %reduce-scatter.13.cloned.1.call-done = bf16[512,256]{0,1:T(8,128)(2,1)} async-done(((bf16[512,2048]{0,1:T(8,128)(2,1)}), bf16[512,256]{0,1:T(8,128)(2,1)}) %reduce-scatter.13.cloned.1.call-update) | async-done | bytes 262160 | tf_op jit(solution)/shard_map/reduce_scatter | solution.py:273
  672.4 63.2 %reduce-scatter.15.cloned.1.call-done = bf16[256,2048]{1,0:T(8,128)(2,1)} async-done(((bf16[2048,2048]{1,0:T(8,128)(2,1)}), bf16[256,2048]{1,0:T(8,128)(2,1)}) %reduce-scatter.15.cloned.1.call-update) | async-done | bytes 1048592 | tf_op jit(solution)/shard_map/reduce_scatter | solution.py:267
  735.7 75.3 %reduce-scatter.17.cloned.1.call-done = bf16[2048,256]{1,0:T(8,128)(2,1)} async-done(((bf16[2048,2048]{1,0:T(8,128)(2,1)}), bf16[2048,256]{1,0:T(8,128)(2,1)}) %reduce-scatter.17.cloned.1.call-update) | async-done | bytes 1048592 | tf_op jit(solution)/shard_map/reduce_scatter | solution.py:279
  811.1 65.6 %reduce-scatter.11.cloned.1.call-done = bf16[256,1536]{1,0:T(8,128)(2,1)} async-done(((bf16[2048,1536]{1,0:T(8,128)(2,1)}), bf16[256,1536]{1,0:T(8,128)(2,1)}) %reduce-scatter.11.cloned.1.call-update) | async-done | bytes 786448 | tf_op jit(solution)/shard_map/reduce_scatter | solution.py:261
  876.9 17.9 %all-gather.31.cloned.1.call-done = bf16[512,1024]{0,1:T(8,128)(2,1)} async-done(((bf16[512,256]{0,1:T(8,128)(2,1)}), bf16[512,1024]{0,1:T(8,128)(2,1)}) %all-gather.31.cloned.1.call-update) | async-done | bytes 1048592 | tf_op jit(solution)/shard_map/all_gather | solution.py:293
  897.3 43.2 %reduce-scatter.7.cloned.1.call-done = bf16[512,512]{1,0:T(8,128)(2,1)} async-done(((bf16[512,2048]{1,0:T(8,128)(2,1)}), bf16[512,512]{1,0:T(8,128)(2,1)}) %reduce-scatter.7.cloned.1.call-update) | async-done | bytes 524304 | tf_op jit(solution)/shard_map/reduce_scatter | solution.py:176
  942.9 25.2 %all-reduce.6 = (bf16[1536]{0:T(1024)(128)(2,1)S(1)}, bf16[2048]{0:T(1024)(128)(2,1)S(1)}, bf16[512]{0:T(512)(128)(2,1)S(1)}, bf16[2048]{0:T(1024)(128)(2,1)S(1)}, bf16[2048]{0:T(1024)(128)(2,1)S(1)}) all-reduce(bf16[1536]{0:T(1024)(128)(2,1)S(1)} %reduce_sum.110, ...), channel_id=1, replica_groups=mesh['dp'=4,'row'=2,'col'=4] {'dp','row'}, use_global_device_ids=true, to_apply=%region_13.14 | all-reduce | flops 8192 | bytes 32768 | tf_op jit(solution)/shard_map/psum | solution.py:254
  982.5 29.9 %all-gather.35.cloned.1.call-done = bf16[2048,1024]{1,0:T(8,128)(2,1)} async-done(((bf16[2048,256]{1,0:T(8,128)(2,1)}), bf16[2048,1024]{1,0:T(8,128)(2,1)}) %all-gather.35.cloned.1.call-update) | async-done | bytes 4194320 | tf_op jit(solution)/shard_map/all_gather | solution.py:296
  1019.0 23.5 %all-gather.29.cloned.1.call-done = bf16[1024,1536]{1,0:T(8,128)(2,1)} async-done(((bf16[256,1536]{1,0:T(8,128)(2,1)}), bf16[1024,1536]{1,0:T(8,128)(2,1)}) %all-gather.29.cloned.1.call-update) | async-done | bytes 3145744 | tf_op jit(solution)/shard_map/all_gather | solution.py:287
  (199 shorter events, 200.0 us)
Async XLA Ops:
  7.2 50.8 %all-gather.13.cloned.1.call-start = ((), (), s32[]{:S(2)}) async-start(), calls=%async_computation.6 | async-start | bytes 2621440 | tf_op jit(solution)/shard_map/all_gather | solution.py:111
  7.9 131.4 %all-gather.15.cloned.1.call-start = ((), (), s32[]{:S(2)}) async-start(), calls=%async_computation.7 | async-start | bytes 9437184 | tf_op jit(solution)/shard_map/all_gather | solution.py:117
  13.0 161.5 %all-gather.21.cloned.1.call-start = ((), (), s32[]{:S(2)}) async-start(), calls=%async_computation.10 | async-start | bytes 3145728 | tf_op jit(solution)/shard_map/all_gather | solution.py:119
  14.2 207.4 %all-gather.27.cloned.1.call-start = ((), (), s32[]{:S(2)}) async-start(), calls=%async_computation.14 | async-start | bytes 2621440 | tf_op jit(solution)/shard_map/all_gather | solution.py:180
  14.8 228.9 %all-gather.17.cloned.1.call-start = ((), (), s32[]{:S(2)}) async-start(), calls=%async_computation.8 | async-start | bytes 1572864 | tf_op jit(solution)/shard_map/all_gather | solution.py:145
  152.2 114.9 %all-gather.19.cloned.1.call-start = ((), (), s32[]{:S(2)}) async-start(), calls=%async_computation.9 | async-start | bytes 1572864 | tf_op jit(solution)/shard_map/all_gather | solution.py:146
  153.1 220.1 %all-gather.23.cloned.1.call-start = ((), (), s32[]{:S(2)}) async-start(), calls=%async_computation.11 | async-start | bytes 12582912 | tf_op jit(solution)/shard_map/all_gather | solution.py:118
  159.2 320.1 %all-gather.25.cloned.1.call-start = ((), (), s32[]{:S(2)}) async-start(), calls=%async_computation.12 | async-start | bytes 12582912 | tf_op jit(solution)/shard_map/all_gather | solution.py:120
  165.4 348.7 %reduce-scatter.9.cloned.1.call-start = ((), (), s32[]{:S(2)}) async-start(), calls=%async_computation.15 | async-start | bytes 3145728 | tf_op jit(solution)/shard_map/reduce_scatter | solution.py:224
  300.2 316.6 %all-reduce.9.cloned.1.call-start = ((), (), s32[]{:S(2)}) async-start(), calls=%async_computation.16 | async-start | bytes 4194304 | tf_op jit(solution)/shard_map/psum | solution.py:241
  307.6 171.7 %copy-start.29 = (f32[2048]{0:T(1024)S(1)}, f32[2048]{0:T(1024)}, u32[]{:S(2)}) copy-start(f32[2048]{0:T(1024)} %param.22) | copy-start | bytes 24580
  530.4 129.8 %reduce-scatter.13.cloned.1.call-start = ((), (), s32[]{:S(2)}) async-start(), calls=%async_computation.19 | async-start | bytes 2359296 | tf_op jit(solution)/shard_map/reduce_scatter | solution.py:273
  539.0 196.6 %reduce-scatter.15.cloned.1.call-start = ((), (), s32[]{:S(2)}) async-start(), calls=%async_computation.21 | async-start | bytes 9437184 | tf_op jit(solution)/shard_map/reduce_scatter | solution.py:267
  556.4 254.6 %reduce-scatter.17.cloned.1.call-start = ((), (), s32[]{:S(2)}) async-start(), calls=%async_computation.23 | async-start | bytes 9437184 | tf_op jit(solution)/shard_map/reduce_scatter | solution.py:279
  603.6 273.0 %reduce-scatter.11.cloned.1.call-start = ((), (), s32[]{:S(2)}) async-start(), calls=%async_computation.17 | async-start | bytes 7077888 | tf_op jit(solution)/shard_map/reduce_scatter | solution.py:261
  634.5 260.2 %all-gather.31.cloned.1.call-start = ((), (), s32[]{:S(2)}) async-start(), calls=%async_computation.20 | async-start | bytes 1310720 | tf_op jit(solution)/shard_map/all_gather | solution.py:293
  660.2 280.3 %reduce-scatter.7.cloned.1.call-start = ((), (), s32[]{:S(2)}) async-start(), calls=%async_computation.13 | async-start | bytes 2621440 | tf_op jit(solution)/shard_map/reduce_scatter | solution.py:176
  672.3 204.3 %copy-start.5 = (bf16[512,512]{1,0:T(8,128)(2,1)S(1)}, bf16[512,512]{1,0:T(8,128)(2,1)}, u32[]{:S(2)}) copy-start(bf16[512,512]{1,0:T(8,128)(2,1)} %param.27) | copy-start | bytes 1572868
  672.3 268.2 %copy-start.8 = (bf16[512,512]{1,0:T(8,128)(2,1)S(1)}, bf16[512,512]{1,0:T(8,128)(2,1)}, u32[]{:S(2)}) copy-start(bf16[512,512]{1,0:T(8,128)(2,1)} %param.15) | copy-start | bytes 1572868
  672.3 268.2 %copy-start.27 = (f32[512]{0:T(512)S(1)}, f32[512]{0:T(512)}, u32[]{:S(2)}) copy-start(f32[512]{0:T(512)} %param.24) | copy-start | bytes 6148
  672.3 270.2 %copy-start.4 = (bf16[512,2048]{1,0:T(8,128)(2,1)S(1)}, bf16[512,2048]{1,0:T(8,128)(2,1)}, u32[]{:S(2)}) copy-start(bf16[512,2048]{1,0:T(8,128)(2,1)} %all-reduce.9.cloned.1.call-done) | copy-start | bytes 6291460
  672.4 303.5 %all-gather.33.cloned.1.call-start = ((), (), s32[]{:S(2)}) async-start(), calls=%async_computation.22 | async-start | bytes 5242880 | tf_op jit(solution)/shard_map/all_gather | solution.py:290
  735.6 276.7 %all-gather.35.cloned.1.call-start = ((), (), s32[]{:S(2)}) async-start(), calls=%async_computation.24 | async-start | bytes 5242880 | tf_op jit(solution)/shard_map/all_gather | solution.py:296
  811.0 231.4 %all-gather.29.cloned.1.call-start = ((), (), s32[]{:S(2)}) async-start(), calls=%async_computation.18 | async-start | bytes 3932160 | tf_op jit(solution)/shard_map/all_gather | solution.py:287
  (31 other events, 839.1 us)
Sparse Core Ops, SparseCore 0:
  9.6 48.3 all-gather.12
  60.1 79.1 all-gather.14
  141.4 33.0 all-gather.20
  176.0 45.6 all-gather.26
  223.6 20.0 all-gather.16
  245.7 21.2 all-gather.18
  269.1 104.0 all-gather.22
  375.3 103.9 all-gather.24
  482.1 31.8 reduce-scatter.8
  530.5 86.1 all-reduce.8
  620.0 40.1 reduce-scatter.12
  664.1 71.4 reduce-scatter.14
  739.7 71.2 reduce-scatter.16
  814.8 61.7 reduce-scatter.10
  878.0 16.6 all-gather.30
  896.9 43.6 reduce-scatter.6
  942.0 33.8 all-gather.32
  977.2 35.0 all-gather.34
  1013.9 28.4 all-gather.28
where the time goes:
time: 1060 us; the launch traced here: 1050 us
  waiting for transfers between devices  744 us (70%)
  matrix products  128 us (12%)
  local copies, waits for them, and re-layouts  74.6 us (7%)
  other arithmetic  67.1 us (6%)
  blocking collectives  25.2 us (2%)
  between operations  15 us (1%)
    all_gather x1, waiting for transfers between devices, per_device(): lax.all_gather(w_down.astype(jnp.bfloat16), 'row', axis=1, tiled=True)  96.3 us
    all_gather x1, waiting for transfers between devices, per_device(): lax.all_gather(w_qkv.astype(jnp.bfloat16), 'row', axis=0, tiled=True)  76.9 us
    reduce_scatter x1, waiting for transfers between devices, per_device(): lax.psum_scatter(reorder_cols(down_grad, row_count, dp_count).astype(jnp....  75.3 us
    all_gather x1, waiting for transfers between devices, per_device(): lax.all_gather(w_up.astype(jnp.bfloat16), 'row', axis=0, tiled=True)  65.6 us
    reduce_scatter x1, waiting for transfers between devices, per_device(): lax.psum_scatter(reorder_rows(qkv_weight_grad, row_count, dp_count).astyp...  65.6 us
    reduce_scatter x1, waiting for transfers between devices, per_device(): lax.psum_scatter(reorder_rows(up_weight_grad, row_count, dp_count).astype...  63.2 us
    all_gather x1, waiting for transfers between devices, per_device(): grad_full = lax.all_gather(cotangent, 'col', axis=1, tiled=True)  47.1 us
    reduce_scatter x1, waiting for transfers between devices, per_device(): lax.psum_scatter(branch_terms.astype(jnp.bfloat16), 'col', scatter_dimens...  43.2 us
  transfers between devices with their start and end apart: 19, of which 19 were waited for; matrix products, arithmetic and copies ran while one was open for 23% of the time, Pallas kernels for 0%

commit v1 on v0

--- a/solution.py
+++ b/solution.py
@@ -4,6 +4,8 @@
 import jax
 import jax.numpy as jnp
 from jax import lax
+from jax.experimental import pallas as pl
+from jax.experimental.pallas import tpu as pltpu
 from jax.sharding import PartitionSpec as P
 
 HD = 64
@@ -66,7 +68,7 @@
     return jnp.transpose(blocked, (0, 2, 1, 3)).reshape(gradient.shape[0], trailing)
 
 
-def per_device(
+def general_device(
     tokens,
     parent,
     depth,
@@ -312,7 +314,490 @@
     )
 
 
+SWAP_ROW = [(0, 1), (1, 0)]
+SWAP_X = [(0, 2), (2, 0), (1, 3), (3, 1)]
+SWAP_CORE = [(0, 1), (1, 0), (2, 3), (3, 2)]
+
+
+def bf16(values):
+    return values.astype(jnp.bfloat16)
+
+
+def f32(values):
+    return values.astype(jnp.float32)
+
+
+def matmul(left, right, dims=((1,), (0,))):
+    return lax.dot_general(left, right, (dims, ((), ())), preferred_element_type=jnp.float32)
+
+
+def swap_row(values):
+    return lax.ppermute(values, "row", SWAP_ROW)
+
+
+def swap_x(values):
+    return lax.ppermute(values, "dp", SWAP_X)
+
+
+def swap_core(values):
+    return lax.ppermute(values, "dp", SWAP_CORE)
+
+
+def pick(index, first, second):
+    return jnp.where(index == 0, first, second)
+
+
+def pair(index, mine, theirs, axis):
+    return pick(
+        index,
+        jnp.concatenate([mine, theirs], axis=axis),
+        jnp.concatenate([theirs, mine], axis=axis),
+    )
+
+
+def gather_line(block, blocks, col):
+    count = len(blocks)
+    width = block.shape[1]
+    to_right, to_left, right, left = [], [], block, block
+    for hop in range(1, count):
+        right = lax.ppermute(right, "col", [(at, at + 1) for at in range(hop - 1, count - 1)])
+        left = lax.ppermute(left, "col", [(at, at - 1) for at in range(1, count - hop + 1)])
+        to_right.append(right)
+        to_left.append(left)
+    slots = jnp.concatenate(to_right[::-1] + [block] + to_left, axis=1)
+    return jnp.concatenate(
+        [
+            lax.dynamic_slice_in_dim(slots, (count - 1 - col + at) * width, width, 1)
+            for at in blocks
+        ],
+        axis=1,
+    )
+
+
+def rotary_tables(positions):
+    lane = jnp.arange(2 * HD, dtype=jnp.int32) % HD
+    half_rot = ROT // 2
+    frequency = jnp.exp(
+        -math.log(rotary_base) * 2.0 * (lane % half_rot).astype(jnp.float32) / ROT
+    )
+    angle = positions[:, None] * frequency[None, :]
+    turned = (lane < ROT)[None, :]
+    sines = jnp.sin(angle)
+    return (
+        jnp.where(turned, jnp.cos(angle), 1.0),
+        jnp.where((lane < half_rot)[None, :], -sines, 0.0),
+        jnp.where(turned & (lane >= half_rot)[None, :], sines, 0.0),
+    )
+
+
+def turn(values, cosines, sines_low, sines_high):
+    width = values.shape[1]
+    half_rot = ROT // 2
+    return (
+        values * cosines
+        + pltpu.roll(values, width - half_rot, 1) * sines_low
+        + pltpu.roll(values, half_rot, 1) * sines_high
+    )
+
+
+def split_kernel(mixed_ref, cos_ref, low_ref, high_ref, query_ref, keyval_ref):
+    cosines, low, high = cos_ref[...], low_ref[...], high_ref[...]
+    rows = mixed_ref.shape[0]
+    half = query_ref.shape[1]
+    first = lax.broadcasted_iota(jnp.int32, (rows, 2 * HD), 1) < HD
+    scale = HD ** (-0.5)
+    for at in range(half // (2 * HD)):
+        tiles = [mixed_ref[:, (3 * at + part) * 2 * HD : (3 * at + part + 1) * 2 * HD] for part in range(3)]
+        query = jnp.where(first, tiles[0], tiles[1])
+        key = jnp.where(first, pltpu.roll(tiles[0], HD, 1), pltpu.roll(tiles[2], HD, 1))
+        value = jnp.where(first, tiles[1], tiles[2])
+        here = slice(at * 2 * HD, (at + 1) * 2 * HD)
+        query_ref[:, here] = bf16(f32(bf16(turn(query, cosines, low, high))) * scale)
+        keyval_ref[:, here] = bf16(turn(key, cosines, low, high))
+        keyval_ref[:, half + at * 2 * HD : half + (at + 1) * 2 * HD] = bf16(value)
+
+
+def join_kernel(row_ref, dq_ref, dkv_ref, sent_ref, cos_ref, low_ref, high_ref, out_ref):
+    cosines, low, high = cos_ref[...], -low_ref[...], -high_ref[...]
+    rows = dq_ref.shape[0]
+    half = dq_ref.shape[1]
+    first = lax.broadcasted_iota(jnp.int32, (rows, 2 * HD), 1) < HD
+    owner = row_ref[0] == 0
+    for at in range(half // (2 * HD)):
+        here = slice(at * 2 * HD, (at + 1) * 2 * HD)
+        there = slice(half + at * 2 * HD, half + (at + 1) * 2 * HD)
+        query = turn(dq_ref[:, here], cosines, low, high)
+        key = dkv_ref[:, here] + jnp.where(owner, f32(sent_ref[:, here]), 0.0)
+        value = dkv_ref[:, there] + jnp.where(owner, f32(sent_ref[:, there]), 0.0)
+        key = pltpu.roll(turn(key, cosines, low, high), HD, 1)
+        tiles = (jnp.where(first, query, key), jnp.where(first, value, query), jnp.where(first, key, value))
+        for part in range(3):
+            out_ref[:, (3 * at + part) * 2 * HD : (3 * at + part + 1) * 2 * HD] = bf16(tiles[part])
+
+
+def tree_kernel(
+    parent_ref, row_ref, query_ref, keyval_ref, trunk_ref, grad_ref,
+    out_ref, dq_ref, dkv_ref, dtrunk_ref,
+    keys, values, dkeys, dvalues,
+):
+    tree = pl.program_id(0)
+    row = row_ref[0]
+    rows, half = query_ref.shape
+    trunk_len = trunk_ref.shape[0]
+    segs = rows // SEG
+    trunk_segs = trunk_len // SEG
+    seg_count = parent_ref.shape[1]
+    first_row = row == 0
+    keys[...] = jnp.where(first_row, keyval_ref[:, :half], trunk_ref[:, :half])
+    values[...] = jnp.where(first_row, keyval_ref[:, half:], trunk_ref[:, half:])
+    dkeys[...] = jnp.zeros_like(dkeys)
+    dvalues[...] = jnp.zeros_like(dvalues)
+    lane = lax.broadcasted_iota(jnp.int32, (1, half), 1)
+    causal = lax.broadcasted_iota(jnp.int32, (SEG, SEG), 0) >= lax.broadcasted_iota(
+        jnp.int32, (SEG, SEG), 1
+    )
+    across = ((1,), (1,))
+    down = ((0,), (0,))
+    for seg in range(segs):
+        here = slice(seg * SEG, (seg + 1) * SEG)
+        above = parent_ref[tree, row * segs + seg]
+        linked = [above == at for at in range(trunk_segs)]
+        for _ in range(seg_count - 2):
+            above = jnp.where(above >= 0, parent_ref[tree, jnp.maximum(above, 0)], -1)
+            linked = [was | (above == at) for at, was in enumerate(linked)]
+        bias = [jnp.where(is_linked, 0.0, masked_fill) for is_linked in linked]
+        query, grad = query_ref[here, :], grad_ref[here, :]
+        own_key, own_value = keyval_ref[here, :half], keyval_ref[here, half:]
+        attended = jnp.zeros((SEG, half), jnp.float32)
+        dquery = jnp.zeros((SEG, half), jnp.float32)
+        dkey = jnp.zeros((SEG, half), jnp.float32)
+        dvalue = jnp.zeros((SEG, half), jnp.float32)
+        for head in range(half // HD):
+            mine = (lane >= head * HD) & (lane < (head + 1) * HD)
+            head_query = jnp.where(mine, query, jnp.zeros_like(query))
+            head_grad = jnp.where(mine, grad, jnp.zeros_like(grad))
+            scores = [
+                matmul(head_query, keys[at * SEG : (at + 1) * SEG, :], across) + bias[at]
+                for at in range(trunk_segs)
+            ] + [jnp.where(causal, matmul(head_query, own_key, across), masked_fill)]
+            top = functools.reduce(jnp.maximum, [jnp.max(s, axis=1, keepdims=True) for s in scores])
+            powers = [jnp.exp(s - top) for s in scores]
+            total = functools.reduce(jnp.add, [jnp.sum(p, axis=1, keepdims=True) for p in powers])
+            probs = [p / total for p in powers]
+            low = [bf16(p) for p in probs]
+            blocks = [values[at * SEG : (at + 1) * SEG, :] for at in range(trunk_segs)] + [own_value]
+            prob_grads = [matmul(head_grad, v, across) for v in blocks]
+            delta = functools.reduce(
+                jnp.add, [jnp.sum(p * g, axis=1, keepdims=True) for p, g in zip(probs, prob_grads)]
+            )
+            score_grads = [bf16(p * (g - delta)) for p, g in zip(probs, prob_grads)]
+            head_out = functools.reduce(jnp.add, [matmul(p, v) for p, v in zip(low, blocks)])
+            attended = jnp.where(mine, head_out, attended)
+            key_blocks = [keys[at * SEG : (at + 1) * SEG, :] for at in range(trunk_segs)] + [own_key]
+            head_dq = functools.reduce(jnp.add, [matmul(s, u) for s, u in zip(score_grads, key_blocks)])
+            dquery = jnp.where(mine, head_dq, dquery)
+            dkey = dkey + matmul(score_grads[-1], head_query, down)
+            dvalue = dvalue + matmul(low[-1], head_grad, down)
+            for at in range(trunk_segs):
+                spot = slice(at * SEG, (at + 1) * SEG)
+                dkeys[spot, :] += matmul(score_grads[at], head_query, down)
+                dvalues[spot, :] += matmul(low[at], head_grad, down)
+        out_ref[here, :] = bf16(attended)
+        dq_ref[here, :] = dquery * HD ** (-0.5)
+        dkv_ref[here, :half] = dkey
+        dkv_ref[here, half:] = dvalue
+    dtrunk_ref[:, :half] = bf16(dkeys[...])
+    dtrunk_ref[:, half:] = bf16(dvalues[...])
+
+    @pl.when(first_row)
+    def _():
+        dkv_ref[:, :half] += dkeys[...]
+        dkv_ref[:, half:] += dvalues[...]
+
+
+def row_block(rows, width):
+    return pl.BlockSpec((rows, width), lambda at, *_: (at, 0))
+
+
+def split_heads(mixed, tables):
+    count, width = mixed.shape
+    rows = SEG
+    return pl.pallas_call(
+        split_kernel,
+        grid=(count // rows,),
+        in_specs=[row_block(rows, width)] + [row_block(rows, 2 * HD)] * 3,
+        out_specs=[row_block(rows, width // 3), row_block(rows, 2 * width // 3)],
+        out_shape=[
+            jax.ShapeDtypeStruct((count, width // 3), jnp.bfloat16),
+            jax.ShapeDtypeStruct((count, 2 * width // 3), jnp.bfloat16),
+        ],
+        cost_estimate=pl.CostEstimate(flops=20 * count * width, bytes_accessed=8 * count * width, transcendentals=0),
+        name="split_heads",
+    )(mixed, *tables)
+
+
+def join_heads(row, dq, dkv, sent, tables):
+    count, half = dq.shape
+    rows = SEG
+    return pl.pallas_call(
+        join_kernel,
+        grid_spec=pltpu.PrefetchScalarGridSpec(
+            num_scalar_prefetch=1,
+            grid=(count // rows,),
+            in_specs=[row_block(rows, half), row_block(rows, 2 * half), row_block(rows, 2 * half)]
+            + [row_block(rows, 2 * HD)] * 3,
+            out_specs=row_block(rows, 3 * half),
+        ),
+        out_shape=jax.ShapeDtypeStruct((count, 3 * half), jnp.bfloat16),
+        cost_estimate=pl.CostEstimate(flops=60 * count * half, bytes_accessed=24 * count * half, transcendentals=0),
+        name="join_heads",
+    )(row, dq, dkv, sent, *tables)
+
+
+def tree_attention(parents, row, query, keyval, trunk, grad):
+    trees = parents.shape[0]
+    count, half = query.shape
+    rows = count // trees
+    keys = trunk.shape[0] // trees
+    pairs = count * (keys + SEG) * (half // HD)
+    return pl.pallas_call(
+        tree_kernel,
+        grid_spec=pltpu.PrefetchScalarGridSpec(
+            num_scalar_prefetch=2,
+            grid=(trees,),
+            in_specs=[
+                row_block(rows, half),
+                row_block(rows, 2 * half),
+                row_block(keys, 2 * half),
+                row_block(rows, half),
+            ],
+            out_specs=[
+                row_block(rows, half),
+                row_block(rows, half),
+                row_block(rows, 2 * half),
+                row_block(keys, 2 * half),
+            ],
+            scratch_shapes=[pltpu.VMEM((keys, half), jnp.bfloat16)] * 2
+            + [pltpu.VMEM((keys, half), jnp.float32)] * 2,
+        ),
+        out_shape=[
+            jax.ShapeDtypeStruct((count, half), jnp.bfloat16),
+            jax.ShapeDtypeStruct((count, half), jnp.float32),
+            jax.ShapeDtypeStruct((count, 2 * half), jnp.float32),
+            jax.ShapeDtypeStruct((trees * keys, 2 * half), jnp.bfloat16),
+        ],
+        cost_estimate=pl.CostEstimate(
+            flops=12 * pairs * half, bytes_accessed=20 * count * half, transcendentals=pairs
+        ),
+        name="tree_attention",
+    )(parents, row, query, keyval, trunk, grad)
+
+
+def paired_device(
+    tokens,
+    parent,
+    depth,
+    w_qkv,
+    b_qkv,
+    w_out,
+    w_up,
+    b_up,
+    w_down,
+    b_res,
+    ln_gain,
+    ln_bias,
+    cotangent,
+):
+    count, width = tokens.shape
+    row = lax.axis_index("row")
+    col = lax.axis_index("col")
+    core = lax.axis_index("dp") % 2
+    slab = lax.axis_index("dp") // 2
+    cols = lax.axis_size("col")
+    half = 2 * width
+    heads_width = w_out.shape[0] // 2
+    hidden = w_up.shape[1] // 2
+    blocks = [2 * row, 2 * row + 1, 2 * (1 - row), 2 * (1 - row) + 1]
+
+    def part(values, at, size, axis):
+        return lax.dynamic_slice_in_dim(values, at * size, size, axis)
+
+    def other_half(send, axis):
+        by_row = swap_row(send)
+        by_x = swap_x(by_row)
+        return pair(slab, by_row, by_x, axis)
+
+    def whole_weight(master, axis):
+        send = bf16(part(master, slab, width, axis))
+        return jnp.concatenate([bf16(master), other_half(send, axis)], axis=axis)
+
+    up_full = whole_weight(part(w_up, core, hidden, 1), 0)
+    qkv_full = whole_weight(part(w_qkv, core, 3 * heads_width, 1), 0)
+    down_full = whole_weight(part(w_down, core, hidden, 0), 1)
+    out_full = whole_weight(part(w_out, core, heads_width, 0), 1)
+
+    tables = jnp.concatenate([parent, depth], axis=0)
+    tables = jnp.stack([tables, swap_core(tables)])
+    parents = tables[:, 0]
+    segs = count // SEG
+    token = jnp.arange(count, dtype=jnp.int32)
+    levels = jnp.zeros((2, count), jnp.float32)
+    for seg in range(segs):
+        level = lax.dynamic_slice_in_dim(tables[:, 1], row * segs + seg, 1, 1).astype(jnp.float32)
+        levels = jnp.where((token // SEG == seg)[None, :], level, levels)
+    positions = (levels * SEG + (token % SEG).astype(jnp.float32)[None, :]).reshape(2 * count)
+    rotary = rotary_tables(positions)
+
+    whole = f32(gather_line(tokens, blocks, col))
+    gain_here = jnp.concatenate([part(ln_gain, at, width, 0) for at in blocks])
+    bias_here = jnp.concatenate([part(ln_bias, at, width, 0) for at in blocks])
+    mean = jnp.mean(whole, axis=1, keepdims=True)
+    centred = whole - mean
+    inv_scale = lax.rsqrt(jnp.mean(centred * centred, axis=1, keepdims=True) + norm_epsilon)
+    normed = bf16(centred * inv_scale * gain_here + bias_here)
+    normed = jnp.concatenate([normed, swap_core(normed)], axis=0)
+    grad = gather_line(cotangent, blocks, col)
+    grad = jnp.concatenate([grad, swap_core(grad)], axis=0)
+
+    mixed = matmul(normed, qkv_full) + part(b_qkv, core, 3 * heads_width, 0)
+    query, keyval = split_heads(mixed, rotary)
+    trunk = lax.ppermute(keyval, "row", [(0, 1)])
+    hidden_up = matmul(normed, up_full) + part(b_up, core, hidden, 0)
+    root = math.sqrt(2.0 / math.pi)
+    squared = hidden_up * hidden_up
+    bend = jnp.tanh(root * (hidden_up + 0.044715 * squared * hidden_up))
+    activated = bf16(0.5 * hidden_up * (1.0 + bend))
+    slope = bf16(
+        0.5 * (1.0 + bend)
+        + 0.5 * hidden_up * (1.0 - bend * bend) * root * (1.0 + 3.0 * 0.044715 * squared)
+    )
+
+    def reduced(left, right, name):
+        sent = swap_row(bf16(left()))
+        both = bf16(right() + f32(sent))
+        return bf16(f32(both) + f32(swap_x(both)))
+
+    down_dims = ((0,), (0,))
+    across = ((1,), (1,))
+    grad_own, grad_other = grad[:, :half], grad[:, half:]
+    normed_own, normed_other = normed[:, :half], normed[:, half:]
+    cut = hidden // 4
+    down_first = reduced(
+        lambda: matmul(activated[:, :cut], grad_other, down_dims),
+        lambda: matmul(activated[:, :cut], grad_own, down_dims),
+        "down_first",
+    )
+    down_last = reduced(
+        lambda: matmul(activated[:, cut:], grad_other, down_dims),
+        lambda: matmul(activated[:, cut:], grad_own, down_dims),
+        "down_last",
+    )
+    down_sum = jnp.concatenate([down_first, down_last], axis=0)
+    down_grad = f32(pair(core, down_sum, swap_core(down_sum), 0))
+
+    act_grad = matmul(grad, down_full, across)
+    up_grad = bf16(act_grad * f32(slope))
+    up_sum = reduced(
+        lambda: matmul(normed_other, up_grad, down_dims),
+        lambda: matmul(normed_own, up_grad, down_dims),
+        "up",
+    )
+    up_weight_grad = f32(pair(core, up_sum, swap_core(up_sum), 1))
+
+    out_heads = bf16(matmul(grad, out_full, across))
+    row_table = jnp.reshape(row, (1,)).astype(jnp.int32)
+    attended, query_grad, own_grad, trunk_grad = tree_attention(
+        parents, row_table, query, keyval, trunk, out_heads
+    )
+    trunk_sent = lax.ppermute(trunk_grad, "row", [(1, 0)])
+    out_sum = reduced(
+        lambda: matmul(attended, grad_other, down_dims),
+        lambda: matmul(attended, grad_own, down_dims),
+        "out",
+    )
+    out_grad = f32(pair(core, out_sum, swap_core(out_sum), 0))
+    mixed_grad = join_heads(row_table, query_grad, own_grad, trunk_sent, rotary)
+    qkv_sum = reduced(
+        lambda: matmul(normed_other, mixed_grad, down_dims),
+        lambda: matmul(normed_own, mixed_grad, down_dims),
+        "qkv",
+    )
+    qkv_weight_grad = f32(pair(core, qkv_sum, swap_core(qkv_sum), 1))
+
+    def spread(terms):
+        mine = terms[:count] + f32(swap_core(bf16(terms[count:])))
+        mine = bf16(mine)
+        ordered = pair(row, mine[:, :half], mine[:, half:], 1)
+        stacked = jnp.stack([ordered[:, at * width : (at + 1) * width] for at in range(cols)])
+        swapped = lax.all_to_all(stacked, "col", 0, 0, tiled=True)
+        return jnp.sum(f32(swapped), axis=0)
+
+    branch = spread(matmul(attended, out_full) + matmul(activated, down_full))
+    output = bf16(f32(tokens) + branch + b_res)
+
+    norm_grad = spread(
+        matmul(mixed_grad, qkv_full, across) + matmul(up_grad, up_full, across)
+    )
+    normal = (f32(tokens) - mean) * inv_scale
+    scaled = norm_grad * part(ln_gain, col, width, 0)
+    sums = jnp.stack([jnp.sum(scaled, axis=1), jnp.sum(scaled * normal, axis=1)])
+    shifted = [
+        lax.ppermute(sums, "col", [(at, (at + hop) % cols) for at in range(cols)])
+        for hop in range(1, cols)
+    ]
+    sums = functools.reduce(jnp.add, shifted, sums) / (cols * width)
+    tokens_grad = inv_scale * (
+        scaled - sums[0][:, None] - normal * sums[1][:, None]
+    ) + f32(cotangent)
+
+    small = jnp.concatenate(
+        [
+            jnp.sum(f32(up_grad), axis=0),
+            jnp.sum(f32(mixed_grad), axis=0),
+            jnp.sum(f32(cotangent), axis=0),
+            jnp.sum(norm_grad * normal, axis=0),
+            jnp.sum(norm_grad, axis=0),
+        ]
+    ).reshape(-1, 128)
+    small = small + swap_row(small)
+    small = small + swap_x(small)
+    small, small_other = small.reshape(-1), swap_core(small).reshape(-1)
+    bounds = [0, hidden, hidden + 3 * heads_width]
+    up_bias_grad = pair(core, small[: bounds[1]], small_other[: bounds[1]], 0)
+    qkv_bias_grad = pair(
+        core, small[bounds[1] : bounds[2]], small_other[bounds[1] : bounds[2]], 0
+    )
+    shared = (small + small_other)[bounds[2] :].reshape(3, width)
+    res_bias_grad = shared[0]
+    norm_sums = shared[1:].reshape(-1, 128)
+    arrived = [norm_sums] + [
+        lax.ppermute(norm_sums, "col", [(at, (at + hop) % cols) for at in range(cols)])
+        for hop in range(1, cols)
+    ]
+    arrived = arrived[::-1]
+    arrived = jnp.stack(arrived + arrived[:-1])
+    arrived = lax.dynamic_slice_in_dim(arrived, cols - 1 - col, cols, 0)
+    arrived = arrived.reshape(cols, 2, width)
+    gain_grad = arrived[:, 0].reshape(-1)
+    shift_grad = arrived[:, 1].reshape(-1)
+    return (
+        output,
+        tokens_grad,
+        qkv_weight_grad,
+        qkv_bias_grad,
+        out_grad,
+        up_weight_grad,
+        up_bias_grad,
+        down_grad,
+        res_bias_grad,
+        gain_grad,
+        shift_grad,
+    )
+
+
 def solution(mesh):
+    sizes = (mesh.shape["dp"], mesh.shape["row"], mesh.shape["col"])
+    per_device = paired_device if sizes == (4, 2, 4) else general_device
     return jax.shard_map(
         per_device,
         mesh=mesh,

time: 1060 us -> 575 us (0.54)
  waiting for transfers between devices: 744 us -> 220 us
  starting transfers between devices: 0.98 us -> 81.5 us
  matrix products: 128 us -> 95.7 us
  Pallas kernels: 0 us -> 28.3 us
  blocking collectives: 25.2 us -> 0 us
  local copies, waits for them, and re-layouts: 74.6 us -> 53.8 us
  other arithmetic: 67.1 us -> 87.3 us
  between operations: 15 us -> 1.75 us
    all_gather x12 -> x0, waiting for transfers between devices: 435 us -> none  [the longest x1 96.3 us: per_device(): lax.all_gather(w_down.astype(jnp.bfloat16), 'row', axis=1, tiled=True)]
    reduce_scatter x6 -> x0, waiting for transfers between devices: 294 us -> none  [the longest x1 75.3 us: per_device(): lax.psum_scatter(reorder_cols(down_grad, row_count, dp_count).astype(jnp....]
    ppermute x0 -> x50, waiting for transfers between devices: none -> 210 us  [the longest x10 78.2 us: swap_x(): return lax.ppermute(values, 'dp', SWAP_X)]
    ppermute x0 -> x50, starting transfers between devices: none -> 65.8 us  [the longest x6 15.5 us: gather_line(): lax.ppermute(right, 'col', [(at, at + 1) for at in range(hop - 1, count -...]
    convert_element_type x6 -> x4, local copies, waits for them, and re-layouts: 49.8 us -> 12.2 us  [bf16(): return values.astype(jnp.bfloat16)]
    dot_general x25 -> x18, matrix products: 128 us -> 95.7 us  [matmul(): lax.dot_general(left, right, (dims, ((), ())), preferred_element_type=jnp...]
    pallas_call x0 -> x3, Pallas kernels: none -> 28.3 us  [the longest x1 18 us: tree_attention(): pl.pallas_call(tree_kernel, grid_spec=pltpu.PrefetchScalarGridSpec(num_sc...]
    psum x1 -> x0, blocking collectives: 25.2 us -> none  [per_device(): lax.psum(qkv_bias_grad.astype(jnp.bfloat16), ('dp', 'row'))]
  transfers between devices with their start and end apart: 19 -> 52, of which waited for: 19 -> 24; matrix products, arithmetic and copies ran while one was open for 23% -> 37% of each run, Pallas kernels for 0% -> 4%
where the time goes in v1:
time: 575 us; the launch traced here: 569 us
  waiting for transfers between devices  220 us (38%)
  matrix products  95.7 us (17%)
  other arithmetic  87.3 us (15%)
  starting transfers between devices  81.5 us (14%)
  local copies, waits for them, and re-layouts  53.8 us (9%)
  Pallas kernels  28.3 us (5%)
    dot_general x18, matrix products, matmul(): lax.dot_general(left, right, (dims, ((), ())), preferred_element_type=jnp...  95.7 us
    ppermute x10, waiting for transfers between devices, swap_x(): return lax.ppermute(values, 'dp', SWAP_X)  78.2 us
    ppermute x10, waiting for transfers between devices, swap_row(): return lax.ppermute(values, 'row', SWAP_ROW)  76.6 us
    ppermute x6, waiting for transfers between devices, gather_line(): lax.ppermute(left, 'col', [(at, at - 1) for at in range(1, count - hop +...  31.8 us
    unnamed x105, local copies, waits for them, and re-layouts  25.3 us
    convert_element_type x4, other arithmetic, f32(): return values.astype(jnp.float32)  20.2 us
    convert_element_type x8, other arithmetic, bf16(): return values.astype(jnp.bfloat16)  18.6 us
    pallas_call x1, Pallas kernels, tree_attention(): pl.pallas_call(tree_kernel, grid_spec=pltpu.PrefetchScalarGridSpec(num_sc...  18 us
  transfers between devices with their start and end apart: 52, of which 24 were waited for; matrix products, arithmetic and copies ran while one was open for 37% of the time, Pallas kernels for 4%

profile of v1, /device:TPU:0, one launch (start us, length us, event | category | flops | bytes accessed | tf_op | source)
XLA Modules:
  0.0 568.7 jit_solution(11747116313208400823)
XLA Ops:
  58.3 7.8 %collective-permute-done.15 = bf16[512,512]{1,0:T(8,128)(2,1)} collective-permute-done((bf16[512,512]{1,0:T(8,128)(2,1)S(1)}, bf16[512,512]{1,0:T(8,128)(2,1)}, u32[]{:S(2)}, u32[]{:S(2)}) %collective-permute-start.15) | collective-permute-done | bytes 524320 | tf_op jit(solution)/shard_map/ppermute | solution.py:364
  67.7 6.9 %collective-permute-done.5 = bf16[512,512]{1,0:T(8,128)(2,1)} collective-permute-done((bf16[512,512]{1,0:T(8,128)(2,1)S(1)}, bf16[512,512]{1,0:T(8,128)(2,1)}, u32[]{:S(2)}, u32[]{:S(2)}) %collective-permute-start.5) | collective-permute-done | bytes 524320 | tf_op jit(solution)/shard_map/ppermute | solution.py:364
  81.7 11.6 %collective-permute-done.16 = bf16[512,512]{1,0:T(8,128)(2,1)S(1)} collective-permute-done((bf16[512,512]{1,0:T(8,128)(2,1)}, bf16[512,512]{1,0:T(8,128)(2,1)S(1)}, u32[]{:S(2)}, u32[]{:S(2)}) %collective-permute-start.16) | collective-permute-done | bytes 524320 | tf_op jit(solution)/shard_map/ppermute | solution.py:364
  109.2 10.4 %collective-permute-done.20 = bf16[512,1024]{1,0:T(8,128)(2,1)} collective-permute-done((bf16[512,1024]{1,0:T(8,128)(2,1)}, bf16[512,1024]{1,0:T(8,128)(2,1)}, u32[]{:S(2)}, u32[]{:S(2)}) %collective-permute-start.20) | collective-permute-done | bytes 1048608 | tf_op jit(solution)/shard_map/ppermute | solution.py:335
  122.0 11.9 %collective-permute-done.22 = bf16[1024,512]{1,0:T(8,128)(2,1)} collective-permute-done((bf16[1024,512]{1,0:T(8,128)(2,1)}, bf16[1024,512]{1,0:T(8,128)(2,1)}, u32[]{:S(2)}, u32[]{:S(2)}) %collective-permute-start.22) | collective-permute-done | bytes 1048608 | tf_op jit(solution)/shard_map/ppermute | solution.py:335
  140.5 22.2 %collective-permute-done.9 = bf16[512,768]{1,0:T(8,128)(2,1)S(1)} collective-permute-done((bf16[512,768]{1,0:T(8,128)(2,1)}, bf16[512,768]{1,0:T(8,128)(2,1)S(1)}, u32[]{:S(2)}, u32[]{:S(2)}) %collective-permute-start.9) | collective-permute-done | bytes 786464 | tf_op jit(solution)/shard_map/ppermute | solution.py:339
  177.7 14.1 %pad_maximum_fusion.1 = bf16[1024,2048]{1,0:T(8,128)(2,1)S(1)} fusion(bf16[512,2048]{1,0:T(8,128)(2,1)} %collective-permute-done.17, bf16[512,512]{1,0:T(8,128)(2,1)S(1)} %get-tuple-element.53, bf16[512,512]{1,0:T(8,128)(2,1)S(1)} %get-tuple-element.54, bf16[512,512]{1,0:T(8,128)(2,1)S(1)} %get-tuple-element.55, bf16[512,512]{1,0:T(8,128)(2,1)S(1)} %get-tuple-element.52), kind=kLoop, calls=%fused_computation.25 | loop fusion | flops 20971520 | bytes 8388608 | tf_op jit(solution)/shard_map/concatenate | solution.py:660
  191.8 11.0 %multiply_convert_fusion.1 = (bf16[1024,1024]{1,0:T(8,128)(2,1)S(1)}, f32[1024,1024]{1,0:T(8,128)}) fusion(f32[1024]{0:T(1024)S(1)} %dynamic_slice.115, bf16[1024,1024]{1,0:T(8,128)(2,1)S(1)} %maximum_select_fusion.3, bf16[1024,1024]{1,0:T(8,128)(2,1)S(1)} %copy-done.12, bf16[512,2048]{1,0:T(8,128)(2,1)} %collective-permute-done.7, bf16[512,2048]{1,0:T(8,128)(2,1)} %fusion.5), kind=kOutput, calls=%fused_computation.39 | convolution fusion | flops 4322230272 | bytes 14684160 | tf_op jit(solution)/shard_map/dot_general | solution.py:331
  207.4 7.3 %broadcast_add_fusion.mixed_ref = f32[1024,768]{1,0:T(8,128)} fusion(f32[768]{0:T(1024)S(1)} %dynamic_slice.104, bf16[1024,768]{1,0:T(8,128)(2,1)S(1)} %maximum_select_fusion.7, bf16[1024,768]{1,0:T(8,128)(2,1)S(1)} %copy-done.18, bf16[512,2048]{1,0:T(8,128)(2,1)} %collective-permute-done.7, bf16[512,2048]{1,0:T(8,128)(2,1)} %fusion.5), kind=kOutput, calls=%fused_computation.84 | convolution fusion | flops 3236691968 | bytes 10488832 | tf_op jit(solution)/shard_map/dot_general | solution.py:331
  230.6 10.3 %convert_reduce_fusion.3 = (f32[1024]{0:T(1024)S(1)}, bf16[1024,1024]{1,0:T(8,128)(2,1)}) fusion(f32[1024,1024]{1,0:T(8,128)} %get-tuple-element.94, f32[1024]{0:T(1024)S(1)} %dynamic_slice.115, bf16[1024,2048]{1,0:T(8,128)(2,1)S(1)} %copy-done.8, bf16[1024,1024]{1,0:T(8,128)(2,1)} %maximum_select_fusion.4, bf16[1024,1024]{1,0:T(8,128)(2,1)S(1)} %copy-done.14), kind=kOutput, calls=%fused_computation.34 | convolution fusion | flops 4327472128 | bytes 14688256 | tf_op jit(solution)/shard_map/dot_general | solution.py:331
  247.2 18.0 %tree_attention.1 = (bf16[1024,256]{1,0:T(8,128)(2,1)}, f32[1024,256]{1,0:T(8,128)}, f32[1024,512]{1,0:T(8,128)}, bf16[1024,512]{1,0:T(8,128)(2,1)}) custom-call(s32[2,4]{1,0:T(2,128)} %bitcast.83, s32[1]{0:T(128)} %bitcast.3.row_ref, bf16[1024,256]{1,0:T(8,128)(2,1)} %get-tuple-element.17.query_ref, bf16[1024,512]{1,0:T(8,128)(2,1)} %get-tuple-element.18.keyval_ref, ...), custom_call_target="tpu_custom_call" | custom-call | flops 9663676416 | bytes 5242880 | tf_op jit(solution)/shard_map/tree_attention/pallas_call | solution.py:563
  266.9 10.1 %fusion.14 = f32[1024,2048]{1,0:T(8,128)} fusion(bf16[1024,1024]{1,0:T(8,128)(2,1)} %copy-done.32, bf16[1024,1024]{1,0:T(8,128)(2,1)} %maximum_select_fusion.4, bf16[1024,1024]{1,0:T(8,128)(2,1)S(1)} %copy-done.14), kind=kOutput, calls=%fused_computation.51 | convolution fusion | flops 4303355904 | bytes 14680064 | tf_op jit(solution)/shard_map/dot_general | solution.py:331
  289.4 8.9 %fusion.21 = f32[1024,2048]{1,0:T(8,128)} fusion(bf16[1024,768]{1,0:T(8,128)(2,1)} %join_heads.1, bf16[1024,768]{1,0:T(8,128)(2,1)} %copy-done.20, bf16[1024,768]{1,0:T(8,128)(2,1)S(1)} %copy-done.19), kind=kOutput, calls=%fused_computation.69 | convolution fusion | flops 3227516928 | bytes 13107200 | tf_op jit(solution)/shard_map/dot_general | solution.py:331
  298.2 8.6 %fusion.17 = f32[1024,2048]{1,0:T(8,128)S(1)} fusion(f32[1024,2048]{1,0:T(8,128)} %fusion.21, bf16[1024,1024]{1,0:T(8,128)(2,1)S(1)} %copy-done.34, bf16[1024,1024]{1,0:T(8,128)(2,1)S(1)} %copy-done.16, bf16[1024,1024]{1,0:T(8,128)(2,1)S(1)} %copy-done.13), kind=kOutput, calls=%fused_computation.54 | convolution fusion | flops 4305453056 | bytes 23068672 | tf_op jit(solution)/shard_map/dot_general | solution.py:331
  321.2 51.5 %collective-permute-done.36 = bf16[256,1024]{1,0:T(8,128)(2,1)S(1)} collective-permute-done((bf16[256,1024]{1,0:T(8,128)(2,1)S(1)}, bf16[256,1024]{1,0:T(8,128)(2,1)S(1)}, u32[]{:S(2)}, u32[]{:S(2)}) %collective-permute-start.36) | collective-permute-done | bytes 524320 | tf_op jit(solution)/shard_map/ppermute | solution.py:335
  383.2 11.0 %all-to-all-start.1 = ((bf16[4,512,512]{2,1,0:T(8,128)(2,1)}), bf16[4,512,512]{2,1,0:T(8,128)(2,1)}, u32[]{:S(2)}, u32[]{:S(2)}) async-start(bf16[4,512,512]{2,1,0:T(8,128)(2,1)} %pad_maximum_fusion.16), calls=%async_computation.1 | async-start | bytes 4194304 | tf_op jit(solution)/shard_map/all_to_all | solution.py:732
  407.5 15.5 %collective-permute-done.45 = bf16[768,1024]{1,0:T(8,128)(2,1)} collective-permute-done((bf16[768,1024]{1,0:T(8,128)(2,1)S(1)}, bf16[768,1024]{1,0:T(8,128)(2,1)}, u32[]{:S(2)}, u32[]{:S(2)}) %collective-permute-start.45) | collective-permute-done | bytes 1572896 | tf_op jit(solution)/shard_map/ppermute | solution.py:339
  431.9 10.7 %all-to-all-done.1 = bf16[4,512,512]{2,1,0:T(8,128)(2,1)} async-done(((bf16[4,512,512]{2,1,0:T(8,128)(2,1)}), bf16[4,512,512]{2,1,0:T(8,128)(2,1)}, u32[]{:S(2)}, u32[]{:S(2)}) %all-to-all-start.1) | async-done | bytes 2097184 | tf_op jit(solution)/shard_map/all_to_all | solution.py:732
  460.8 7.1 %collective-permute-done.40 = bf16[1024,1024]{0,1:T(8,128)(2,1)} collective-permute-done((bf16[1024,1024]{0,1:T(8,128)(2,1)}, bf16[1024,1024]{0,1:T(8,128)(2,1)}, u32[]{:S(2)}, u32[]{:S(2)}) %collective-permute-start.40) | collective-permute-done | bytes 2097184 | tf_op jit(solution)/shard_map/ppermute | solution.py:339
  472.5 27.9 %collective-permute-done.31 = bf16[1024,768]{0,1:T(8,128)(2,1)} collective-permute-done((bf16[1024,768]{0,1:T(8,128)(2,1)}, bf16[1024,768]{0,1:T(8,128)(2,1)}, u32[]{:S(2)}, u32[]{:S(2)}) %collective-permute-start.31) | collective-permute-done | bytes 1572896 | tf_op jit(solution)/shard_map/ppermute | solution.py:339
  512.2 6.7 %collective-permute-start.29 = (f32[2,512]{1,0:T(2,128)S(1)}, f32[2,512]{1,0:T(2,128)S(1)}, u32[]{:S(2)}, u32[]{:S(2)}) collective-permute-start(f32[2,512]{1,0:T(2,128)S(1)} %pad_maximum_fusion.31), channel_id=1, source_target_pairs={{0,3},{1,0},{2,1},{3,2},{4,7},{5,4},{6,5},{7,6},{8,11},{9,8},{10,9... | collective-permute-start | bytes 12296 | tf_op jit(solution)/shard_map/ppermute | solution.py:745
  531.5 6.3 %fusion.10 = f32[1024,2048]{0,1:T(8,128)} fusion(bf16[1024,1024]{0,1:T(8,128)(2,1)} %collective-permute-done.41, bf16[1024,1024]{0,1:T(8,128)(2,1)} %add_convert_fusion, pred[]{:T(512)S(6)} %eq.45), kind=kLoop, calls=%fused_computation.29 | loop fusion | flops 20971520 | bytes 12582913 | tf_op jit(solution)/shard_map/convert_element_type | solution.py:327
  537.8 9.1 %copy.31 = f32[1024,2048]{1,0:T(8,128)} copy(f32[1024,2048]{0,1:T(8,128)} %fusion.10) | data formatting | bytes 16777216
  552.4 6.6 %copy.30 = f32[1024,1536]{1,0:T(8,128)} copy(f32[1024,1536]{0,1:T(8,128)} %fusion.12) | data formatting | bytes 12582912
  (291 shorter events, 255.4 us)
Async XLA Ops:
  13.5 92.4 %collective-permute-start = (s32[2,4]{1,0:T(2,128)S(1)}, s32[2,4]{1,0:T(2,128)S(1)}, u32[]{:S(2)}, u32[]{:S(2)}) collective-permute-start(s32[2,4]{1,0:T(2,128)S(1)} %get-tuple-element.91), channel_id=1, source_target_pairs={{0,8},{8,0},{16,24},{24,16},{1,9},{9,1},{17,25},{25,17},{2,10},{10... | collective-permute-start | bytes 104 | tf_op jit(solution)/shard_map/ppermute | solution.py:343
  53.4 67.8 %collective-permute-start.8 = (bf16[512,768]{1,0:T(8,128)(2,1)S(1)}, bf16[512,768]{1,0:T(8,128)(2,1)}, u32[]{:S(2)}, u32[]{:S(2)}) collective-permute-start(bf16[512,768]{1,0:T(8,128)(2,1)S(1)} %dynamic_slice.167), channel_id=1, source_target_pairs={{0,4},{4,0},{1,5},{5,1},{2,6},{6,2},{3,7},{7,3},{8,12},{12,8},{9,1... | collective-permute-start | bytes 2359304 | tf_op jit(solution)/shard_map/ppermute | solution.py:335
  94.9 39.0 %collective-permute-start.22 = (bf16[1024,512]{1,0:T(8,128)(2,1)}, bf16[1024,512]{1,0:T(8,128)(2,1)}, u32[]{:S(2)}, u32[]{:S(2)}) collective-permute-start(bf16[1024,512]{1,0:T(8,128)(2,1)} %dynamic_slice.165), channel_id=1, source_target_pairs={{0,4},{4,0},{1,5},{5,1},{2,6},{6,2},{3,7},{7,3},{8,12},{12,8},{9,1... | collective-permute-start | bytes 3145736 | tf_op jit(solution)/shard_map/ppermute | solution.py:335
  105.9 71.7 %collective-permute-start.17 = (bf16[512,2048]{1,0:T(8,128)(2,1)}, bf16[512,2048]{1,0:T(8,128)(2,1)}, u32[]{:S(2)}, u32[]{:S(2)}) collective-permute-start(bf16[512,2048]{1,0:T(8,128)(2,1)} %pad_maximum_fusion.14), channel_id=1, source_target_pairs={{0,8},{8,0},{16,24},{24,16},{1,9},{9,1},{17,25},{25,17},{2,10},{10... | collective-permute-start | bytes 6291464 | tf_op jit(solution)/shard_map/ppermute | solution.py:343
  108.8 83.0 %collective-permute-start.7 = (bf16[512,2048]{1,0:T(8,128)(2,1)}, bf16[512,2048]{1,0:T(8,128)(2,1)}, u32[]{:S(2)}, u32[]{:S(2)}) collective-permute-start(bf16[512,2048]{1,0:T(8,128)(2,1)} %fusion.5), channel_id=1, source_target_pairs={{0,8},{8,0},{16,24},{24,16},{1,9},{9,1},{17,25},{25,17},{2,10},{10... | collective-permute-start | bytes 6291464 | tf_op jit(solution)/shard_map/ppermute | solution.py:343
  119.6 45.1 %collective-permute-start.21 = (bf16[512,1024]{1,0:T(8,128)(2,1)}, bf16[512,1024]{1,0:T(8,128)(2,1)}, u32[]{:S(2)}, u32[]{:S(2)}) collective-permute-start(bf16[512,1024]{1,0:T(8,128)(2,1)} %collective-permute-done.20), channel_id=1, source_target_pairs={{0,16},{16,0},{8,24},{24,8},{1,17},{17,1},{9,25},{25,9},{2,18},{18... | collective-permute-start | bytes 3145736 | tf_op jit(solution)/shard_map/ppermute | solution.py:339
  121.2 41.5 %collective-permute-start.9 = (bf16[512,768]{1,0:T(8,128)(2,1)}, bf16[512,768]{1,0:T(8,128)(2,1)S(1)}, u32[]{:S(2)}, u32[]{:S(2)}) collective-permute-start(bf16[512,768]{1,0:T(8,128)(2,1)} %collective-permute-done.8), channel_id=1, source_target_pairs={{0,16},{16,0},{8,24},{24,8},{1,17},{17,1},{9,25},{25,9},{2,18},{18... | collective-permute-start | bytes 2359304 | tf_op jit(solution)/shard_map/ppermute | solution.py:339
  133.9 40.1 %collective-permute-start.23 = (bf16[1024,512]{1,0:T(8,128)(2,1)}, bf16[1024,512]{1,0:T(8,128)(2,1)S(1)}, u32[]{:S(2)}, u32[]{:S(2)}) collective-permute-start(bf16[1024,512]{1,0:T(8,128)(2,1)} %collective-permute-done.22), channel_id=1, source_target_pairs={{0,16},{16,0},{8,24},{24,8},{1,17},{17,1},{9,25},{25,9},{2,18},{18... | collective-permute-start | bytes 3145736 | tf_op jit(solution)/shard_map/ppermute | solution.py:339
  224.3 151.6 %collective-permute-start.44 = (bf16[768,1024]{1,0:T(8,128)(2,1)}, bf16[768,1024]{1,0:T(8,128)(2,1)}, u32[]{:S(2)}, u32[]{:S(2)}) collective-permute-start(bf16[768,1024]{1,0:T(8,128)(2,1)} %convolution_convert_fusion.1), channel_id=1, source_target_pairs={{0,4},{4,0},{1,5},{5,1},{2,6},{6,2},{3,7},{7,3},{8,12},{12,8},{9,1... | collective-permute-start | bytes 4718600 | tf_op jit(solution)/shard_map/ppermute | solution.py:335
  224.3 55.7 %collective-permute-start.42 = (bf16[256,1024]{1,0:T(8,128)(2,1)}, bf16[256,1024]{1,0:T(8,128)(2,1)}, u32[]{:S(2)}, u32[]{:S(2)}) collective-permute-start(bf16[256,1024]{1,0:T(8,128)(2,1)} %fusion.43), channel_id=1, source_target_pairs={{0,4},{4,0},{1,5},{5,1},{2,6},{6,2},{3,7},{7,3},{8,12},{12,8},{9,1... | collective-permute-start | bytes 1572872 | tf_op jit(solution)/shard_map/ppermute | solution.py:335
  307.2 72.4 %collective-permute-start.26 = (bf16[512,2048]{1,0:T(8,128)(2,1)S(1)}, bf16[512,2048]{1,0:T(8,128)(2,1)S(1)}, u32[]{:S(2)}, u32[]{:S(2)}) collective-permute-start(bf16[512,2048]{1,0:T(8,128)(2,1)S(1)} %slice.286), channel_id=1, source_target_pairs={{0,8},{8,0},{16,24},{24,16},{1,9},{9,1},{17,25},{25,17},{2,10},{10... | collective-permute-start | bytes 6291464 | tf_op jit(solution)/shard_map/ppermute | solution.py:343
  313.4 87.3 %collective-permute-start.39 = (bf16[1024,1024]{0,1:T(8,128)(2,1)}, bf16[1024,1024]{0,1:T(8,128)(2,1)}, u32[]{:S(2)}, u32[]{:S(2)}) collective-permute-start(bf16[1024,1024]{0,1:T(8,128)(2,1)} %convolution_convert_fusion), channel_id=1, source_target_pairs={{0,4},{4,0},{1,5},{5,1},{2,6},{6,2},{3,7},{7,3},{8,12},{12,8},{9,1... | collective-permute-start | bytes 6291464 | tf_op jit(solution)/shard_map/ppermute | solution.py:335
  317.6 55.1 %collective-permute-start.36 = (bf16[256,1024]{1,0:T(8,128)(2,1)S(1)}, bf16[256,1024]{1,0:T(8,128)(2,1)S(1)}, u32[]{:S(2)}, u32[]{:S(2)}) collective-permute-start(bf16[256,1024]{1,0:T(8,128)(2,1)S(1)} %fusion.40), channel_id=1, source_target_pairs={{0,4},{4,0},{1,5},{5,1},{2,6},{6,2},{3,7},{7,3},{8,12},{12,8},{9,1... | collective-permute-start | bytes 1572872 | tf_op jit(solution)/shard_map/ppermute | solution.py:335
  321.2 105.5 %collective-permute-start.24 = (bf16[512,2048]{1,0:T(8,128)(2,1)}, bf16[512,2048]{1,0:T(8,128)(2,1)}, u32[]{:S(2)}, u32[]{:S(2)}) collective-permute-start(bf16[512,2048]{1,0:T(8,128)(2,1)} %slice.287), channel_id=1, source_target_pairs={{0,8},{8,0},{16,24},{24,16},{1,9},{9,1},{17,25},{25,17},{2,10},{10... | collective-permute-start | bytes 6291464 | tf_op jit(solution)/shard_map/ppermute | solution.py:343
  374.2 78.8 %collective-permute-start.37 = (bf16[256,1024]{1,0:T(8,128)(2,1)}, bf16[256,1024]{1,0:T(8,128)(2,1)}, u32[]{:S(2)}, u32[]{:S(2)}) collective-permute-start(bf16[256,1024]{1,0:T(8,128)(2,1)} %fusion.49), channel_id=1, source_target_pairs={{0,16},{16,0},{8,24},{24,8},{1,17},{17,1},{9,25},{25,9},{2,18},{18... | collective-permute-start | bytes 1572872 | tf_op jit(solution)/shard_map/ppermute | solution.py:339
  379.2 43.8 %collective-permute-start.45 = (bf16[768,1024]{1,0:T(8,128)(2,1)S(1)}, bf16[768,1024]{1,0:T(8,128)(2,1)}, u32[]{:S(2)}, u32[]{:S(2)}) collective-permute-start(bf16[768,1024]{1,0:T(8,128)(2,1)S(1)} %add_convert_fusion.4), channel_id=1, source_target_pairs={{0,16},{16,0},{8,24},{24,8},{1,17},{17,1},{9,25},{25,9},{2,18},{18... | collective-permute-start | bytes 4718600 | tf_op jit(solution)/shard_map/ppermute | solution.py:339
  383.2 59.4 %all-to-all-start.1 = ((bf16[4,512,512]{2,1,0:T(8,128)(2,1)}), bf16[4,512,512]{2,1,0:T(8,128)(2,1)}, u32[]{:S(2)}, u32[]{:S(2)}) async-start(bf16[4,512,512]{2,1,0:T(8,128)(2,1)} %pad_maximum_fusion.16), calls=%async_computation.1 | async-start | bytes 4194304 | tf_op jit(solution)/shard_map/all_to_all | solution.py:732
  398.9 48.3 %collective-permute-start.30 = (bf16[1024,768]{0,1:T(8,128)(2,1)}, bf16[1024,768]{0,1:T(8,128)(2,1)}, u32[]{:S(2)}, u32[]{:S(2)}) collective-permute-start(bf16[1024,768]{0,1:T(8,128)(2,1)} %convolution_convert_fusion.2), channel_id=1, source_target_pairs={{0,4},{4,0},{1,5},{5,1},{2,6},{6,2},{3,7},{7,3},{8,12},{12,8},{9,1... | collective-permute-start | bytes 4718600 | tf_op jit(solution)/shard_map/ppermute | solution.py:335
  406.8 61.2 %collective-permute-start.40 = (bf16[1024,1024]{0,1:T(8,128)(2,1)}, bf16[1024,1024]{0,1:T(8,128)(2,1)}, u32[]{:S(2)}, u32[]{:S(2)}) collective-permute-start(bf16[1024,1024]{0,1:T(8,128)(2,1)} %add_convert_fusion.1), channel_id=1, source_target_pairs={{0,16},{16,0},{8,24},{24,8},{1,17},{17,1},{9,25},{25,9},{2,18},{18... | collective-permute-start | bytes 6291464 | tf_op jit(solution)/shard_map/ppermute | solution.py:339
  426.8 76.3 %collective-permute-start.46 = (bf16[1024,1024]{1,0:T(8,128)(2,1)}, bf16[1024,1024]{1,0:T(8,128)(2,1)}, u32[]{:S(2)}, u32[]{:S(2)}) collective-permute-start(bf16[1024,1024]{1,0:T(8,128)(2,1)} %pad_maximum_fusion.17), channel_id=1, source_target_pairs={{0,8},{8,0},{16,24},{24,16},{1,9},{9,1},{17,25},{25,17},{2,10},{10... | collective-permute-start | bytes 6291464 | tf_op jit(solution)/shard_map/ppermute | solution.py:343
  442.6 81.1 %all-to-all-start = ((bf16[4,512,512]{2,1,0:T(8,128)(2,1)}), bf16[4,512,512]{2,1,0:T(8,128)(2,1)}, u32[]{:S(2)}, u32[]{:S(2)}) async-start(bf16[4,512,512]{2,1,0:T(8,128)(2,1)} %pad_maximum_fusion.15), calls=%async_computation | async-start | bytes 4194304 | tf_op jit(solution)/shard_map/all_to_all | solution.py:732
  452.3 48.0 %collective-permute-start.31 = (bf16[1024,768]{0,1:T(8,128)(2,1)}, bf16[1024,768]{0,1:T(8,128)(2,1)}, u32[]{:S(2)}, u32[]{:S(2)}) collective-permute-start(bf16[1024,768]{0,1:T(8,128)(2,1)} %add_convert_fusion.6), channel_id=1, source_target_pairs={{0,16},{16,0},{8,24},{24,8},{1,17},{17,1},{9,25},{25,9},{2,18},{18... | collective-permute-start | bytes 4718600 | tf_op jit(solution)/shard_map/ppermute | solution.py:339
  472.5 59.0 %collective-permute-start.41 = (bf16[1024,1024]{0,1:T(8,128)(2,1)}, bf16[1024,1024]{0,1:T(8,128)(2,1)}, u32[]{:S(2)}, u32[]{:S(2)}) collective-permute-start(bf16[1024,1024]{0,1:T(8,128)(2,1)} %add_convert_fusion), channel_id=1, source_target_pairs={{0,8},{8,0},{16,24},{24,16},{1,9},{9,1},{17,25},{25,17},{2,10},{10... | collective-permute-start | bytes 6291464 | tf_op jit(solution)/shard_map/ppermute | solution.py:343
  503.0 44.8 %collective-permute-start.32 = (bf16[1024,768]{0,1:T(8,128)(2,1)S(1)}, bf16[1024,768]{0,1:T(8,128)(2,1)}, u32[]{:S(2)}, u32[]{:S(2)}) collective-permute-start(bf16[1024,768]{0,1:T(8,128)(2,1)S(1)} %add_convert_fusion.5), channel_id=1, source_target_pairs={{0,8},{8,0},{16,24},{24,16},{1,9},{9,1},{17,25},{25,17},{2,10},{10... | collective-permute-start | bytes 4718600 | tf_op jit(solution)/shard_map/ppermute | solution.py:343
  (68 other events, 1148.1 us)

commit v2 on v1

--- a/solution.py
+++ b/solution.py
@@ -355,23 +355,8 @@
     )
 
 
-def gather_line(block, blocks, col):
-    count = len(blocks)
-    width = block.shape[1]
-    to_right, to_left, right, left = [], [], block, block
-    for hop in range(1, count):
-        right = lax.ppermute(right, "col", [(at, at + 1) for at in range(hop - 1, count - 1)])
-        left = lax.ppermute(left, "col", [(at, at - 1) for at in range(1, count - hop + 1)])
-        to_right.append(right)
-        to_left.append(left)
-    slots = jnp.concatenate(to_right[::-1] + [block] + to_left, axis=1)
-    return jnp.concatenate(
-        [
-            lax.dynamic_slice_in_dim(slots, (count - 1 - col + at) * width, width, 1)
-            for at in blocks
-        ],
-        axis=1,
-    )
+def after(value, *earlier):
+    return lax.optimization_barrier((value,) + earlier)[0]
 
 
 def rotary_tables(positions):
@@ -515,6 +500,235 @@
         dkv_ref[:, half:] += dvalues[...]
 
 
+def store_blocks(place_ref, sides, full_ref, plain_ref):
+    row, slab = place_ref[1], place_ref[2]
+    for side, values in enumerate(sides):
+        width = values[0].shape[1]
+        for source, value in enumerate(values):
+            within = source % 2
+            here = row == source // 2
+
+            @pl.when(here)
+            def _():
+                full_ref[side, :, within * width : (within + 1) * width] = value
+
+            @pl.when(jnp.logical_not(here))
+            def _():
+                plain_ref[side, :, within * width : (within + 1) * width] = value
+                at = (2 + jnp.where(slab == 0, within, 1 - within)) * width
+                full_ref[side, :, pl.ds(pl.multiple_of(at, width), width)] = value
+
+
+def gather_kernel(place_ref, mine_ref, theirs_ref, full_ref, plain_ref):
+    sides = [[ref[at] for at in range(ref.shape[0])] for ref in (mine_ref, theirs_ref)]
+    store_blocks(place_ref, sides, full_ref, plain_ref)
+
+
+def norm_kernel(
+    place_ref, gain_ref, bias_ref, mine_ref, theirs_ref, full_ref, plain_ref, normal_ref, scale_ref
+):
+    sides = []
+    for side, ref in enumerate((mine_ref, theirs_ref)):
+        values = [f32(ref[at]) for at in range(ref.shape[0])]
+        features = len(values) * values[0].shape[1]
+        mean = functools.reduce(jnp.add, [jnp.sum(v, axis=1, keepdims=True) for v in values]) / features
+        centred = [v - mean for v in values]
+        square = functools.reduce(jnp.add, [jnp.sum(v * v, axis=1, keepdims=True) for v in centred])
+        inv_scale = lax.rsqrt(square / features + norm_epsilon)
+        normals = [v * inv_scale for v in centred]
+        if side == 0:
+            scale_ref[...] = inv_scale
+            for source, normal in enumerate(normals):
+
+                @pl.when(place_ref[0] == source)
+                def _():
+                    normal_ref[...] = normal
+
+        sides.append(
+            [
+                bf16(normal * gain_ref[source : source + 1, :] + bias_ref[source : source + 1, :])
+                for source, normal in enumerate(normals)
+            ]
+        )
+    store_blocks(place_ref, sides, full_ref, plain_ref)
+
+
+def pair_rows(rows, width):
+    return pl.BlockSpec((2, rows, width), lambda at, *_: (0, at, 0))
+
+
+def gathered(place, mine, theirs, norm=None):
+    blocks, count, width = mine.shape
+    rows = SEG // 2
+    full = blocks * width
+    in_specs = [pl.BlockSpec((blocks, rows, width), lambda at, *_: (0, at, 0))] * 2
+    out_specs = [pair_rows(rows, full), pair_rows(rows, full // 2)]
+    out_shape = [
+        jax.ShapeDtypeStruct((2, count, full), jnp.bfloat16),
+        jax.ShapeDtypeStruct((2, count, full // 2), jnp.bfloat16),
+    ]
+    operands = [mine, theirs]
+    if norm is not None:
+        gain = [values.reshape(blocks, width) for values in norm]
+        operands = gain + operands
+        in_specs = [pl.BlockSpec((blocks, width), lambda at, *_: (0, 0))] * 2 + in_specs
+        out_specs = out_specs + [row_block(rows, width), row_block(rows, 1)]
+        out_shape = out_shape + [
+            jax.ShapeDtypeStruct((count, width), jnp.float32),
+            jax.ShapeDtypeStruct((count, 1), jnp.float32),
+        ]
+    results = pl.pallas_call(
+        gather_kernel if norm is None else norm_kernel,
+        grid_spec=pltpu.PrefetchScalarGridSpec(
+            num_scalar_prefetch=1, grid=(count // rows,), in_specs=in_specs, out_specs=out_specs
+        ),
+        out_shape=out_shape,
+        cost_estimate=pl.CostEstimate(
+            flops=40 * count * width, bytes_accessed=50 * count * width, transcendentals=0
+        ),
+        name="join_blocks" if norm is None else "norm_blocks",
+    )(place, *operands)
+    return [values.reshape(2 * count, -1) for values in results[:2]] + list(results[2:])
+
+
+def stack_kernel(place_ref, terms_ref, arrived_ref, out_ref):
+    row, slab = place_ref[1], place_ref[2]
+    width = out_ref.shape[2]
+    for spot in range(4):
+        here = slice(spot * width, (spot + 1) * width)
+        value = bf16(terms_ref[:, here] + f32(arrived_ref[:, here]))
+        if spot < 2:
+            out_ref[2 * row + spot] = value
+        else:
+            out_ref[2 * (1 - row) + jnp.where(slab == 0, spot - 2, 3 - spot)] = value
+
+
+def stacked(place, terms, arrived, blocks):
+    count, full = arrived.shape
+    rows = SEG // 2
+    width = full // blocks
+    return pl.pallas_call(
+        stack_kernel,
+        grid_spec=pltpu.PrefetchScalarGridSpec(
+            num_scalar_prefetch=1,
+            grid=(count // rows,),
+            in_specs=[row_block(rows, full), row_block(rows, full)],
+            out_specs=pl.BlockSpec((blocks, rows, width), lambda at, *_: (0, at, 0)),
+        ),
+        out_shape=jax.ShapeDtypeStruct((blocks, count, width), jnp.bfloat16),
+        cost_estimate=pl.CostEstimate(flops=count * full, bytes_accessed=8 * count * full, transcendentals=0),
+        name="stack_blocks",
+    )(place, terms, arrived)
+
+
+def cast_rows_kernel(place_ref, master_ref, own_ref, send_ref):
+    value = bf16(master_ref[...])
+    own_ref[...] = value
+    half = pl.num_programs(0) // 2
+
+    @pl.when(pl.program_id(0) // half == place_ref[2])
+    def _():
+        send_ref[...] = value
+
+
+def cast_cols_kernel(place_ref, master_ref, own_ref, send_ref):
+    value = bf16(master_ref[...])
+    own_ref[...] = value
+    half = value.shape[1] // 2
+    send_ref[...] = jnp.where(place_ref[2] == 0, value[:, :half], value[:, half:])
+
+
+def cast_weight(place, master, axis):
+    height, width = master.shape
+    rows = SEG
+    if axis == 0:
+        width = width // 2
+        steps = height // rows
+        half = steps // 2
+        specs = [
+            pl.BlockSpec((rows, width), lambda at, place_ref: (at, place_ref[3])),
+            pl.BlockSpec((rows, width), lambda at, place_ref: (at, 0)),
+            pl.BlockSpec(
+                (rows, width), lambda at, place_ref: (jnp.clip(at - half * place_ref[2], 0, half - 1), 0)
+            ),
+        ]
+        send = (height // 2, width)
+        whole = (2 * height, width)
+    else:
+        height = height // 2
+        steps = height // rows
+        specs = [
+            pl.BlockSpec((rows, width), lambda at, place_ref: (at + steps * place_ref[3], 0)),
+            pl.BlockSpec((rows, width), lambda at, place_ref: (at, 0)),
+            pl.BlockSpec((rows, width // 2), lambda at, place_ref: (at, 0)),
+        ]
+        send = (height, width // 2)
+        whole = (height, 2 * width)
+    return pl.pallas_call(
+        cast_rows_kernel if axis == 0 else cast_cols_kernel,
+        grid_spec=pltpu.PrefetchScalarGridSpec(
+            num_scalar_prefetch=1, grid=(steps,), in_specs=specs[:1], out_specs=specs[1:]
+        ),
+        out_shape=[
+            jax.ShapeDtypeStruct(whole, jnp.bfloat16),
+            jax.ShapeDtypeStruct(send, jnp.bfloat16),
+        ],
+        cost_estimate=pl.CostEstimate(flops=height * width, bytes_accessed=7 * height * width, transcendentals=0),
+        name="cast_weight",
+    )(place, master)
+
+
+def settle_kernel(place_ref, mine_ref, theirs_ref, *refs):
+    out_ref = refs[-1]
+
+    @pl.when(pl.program_id(0) == 0)
+    def _():
+        out_ref[...] = f32(mine_ref[...])
+
+    @pl.when(pl.program_id(0) == 1)
+    def _():
+        out_ref[...] = f32(theirs_ref[...])
+
+
+def settle(place, mine, theirs, shape, axis, offset, dest=None):
+    rows, width = SEG, mine.shape[1]
+    steps = mine.shape[0] // rows
+    first = offset // rows
+    per_core = shape[0] // 2 // rows
+
+    def whose(turn, place_ref):
+        return place_ref[3] + turn - 2 * place_ref[3] * turn
+
+    def out_at(turn, at, place_ref):
+        if axis == 0:
+            return (whose(turn, place_ref) * per_core + first + at, 0)
+        return (first + at, whose(turn, place_ref))
+
+    in_specs = [
+        pl.BlockSpec((rows, width), lambda turn, at, place_ref: (jnp.where(turn == 0, at, steps - 1), 0)),
+        pl.BlockSpec((rows, width), lambda turn, at, place_ref: (jnp.where(turn == 0, 0, at), 0)),
+    ]
+    operands = [place, mine, theirs]
+    aliases = {}
+    if dest is not None:
+        in_specs.append(pl.BlockSpec(memory_space=pl.ANY))
+        operands.append(dest)
+        aliases = {3: 0}
+    return pl.pallas_call(
+        settle_kernel,
+        grid_spec=pltpu.PrefetchScalarGridSpec(
+            num_scalar_prefetch=1,
+            grid=(2, steps),
+            in_specs=in_specs,
+            out_specs=pl.BlockSpec((rows, width), out_at),
+        ),
+        out_shape=jax.ShapeDtypeStruct(shape, jnp.float32),
+        input_output_aliases=aliases,
+        cost_estimate=pl.CostEstimate(flops=0, bytes_accessed=12 * mine.size, transcendentals=0),
+        name="settle",
+    )(*operands)
+
+
 def row_block(rows, width):
     return pl.BlockSpec((rows, width), lambda at, *_: (at, 0))
 
@@ -617,24 +831,45 @@
     half = 2 * width
     heads_width = w_out.shape[0] // 2
     hidden = w_up.shape[1] // 2
-    blocks = [2 * row, 2 * row + 1, 2 * (1 - row), 2 * (1 - row) + 1]
+    place = jnp.stack([col, row, slab, core]).astype(jnp.int32)
+    row_table = jnp.reshape(row, (1,)).astype(jnp.int32)
+    down_dims = ((0,), (0,))
+    across = ((1,), (1,))
 
     def part(values, at, size, axis):
         return lax.dynamic_slice_in_dim(values, at * size, size, axis)
 
-    def other_half(send, axis):
-        by_row = swap_row(send)
+    def exchange(stack):
+        return lax.all_to_all(stack, "col", 0, 0, tiled=True)
+
+    def to_all(block):
+        return exchange(jnp.broadcast_to(block[None], (cols,) + block.shape))
+
+    done = ()
+
+    def step(run, *inputs):
+        nonlocal done
+        inputs, _ = lax.optimization_barrier((inputs, done))
+        result = run(*inputs)
+        done = result
+        return result
+
+    tokens_near = to_all(tokens)
+
+    def ready(master, axis):
+        whole, send = step(lambda weight: cast_weight(place, weight, axis), master)
+        return whole, swap_row(send)
+
+    qkv_whole, qkv_row = ready(w_qkv, 0)
+    up_whole, up_row = ready(w_up, 0)
+    down_whole, down_row = ready(w_down, 1)
+    out_whole, out_row = ready(w_out, 1)
+
+    def fill(whole, by_row, axis):
         by_x = swap_x(by_row)
-        return pair(slab, by_row, by_x, axis)
-
-    def whole_weight(master, axis):
-        send = bf16(part(master, slab, width, axis))
-        return jnp.concatenate([bf16(master), other_half(send, axis)], axis=axis)
-
-    up_full = whole_weight(part(w_up, core, hidden, 1), 0)
-    qkv_full = whole_weight(part(w_qkv, core, 3 * heads_width, 1), 0)
-    down_full = whole_weight(part(w_down, core, hidden, 0), 1)
-    out_full = whole_weight(part(w_out, core, heads_width, 0), 1)
+        start = whole.shape[axis] // 2
+        whole = lax.dynamic_update_slice_in_dim(whole, by_row, start, axis)
+        return lax.dynamic_update_slice_in_dim(whole, by_x, start + by_row.shape[axis], axis)
 
     tables = jnp.concatenate([parent, depth], axis=0)
     tables = jnp.stack([tables, swap_core(tables)])
@@ -648,108 +883,118 @@
     positions = (levels * SEG + (token % SEG).astype(jnp.float32)[None, :]).reshape(2 * count)
     rotary = rotary_tables(positions)
 
-    whole = f32(gather_line(tokens, blocks, col))
-    gain_here = jnp.concatenate([part(ln_gain, at, width, 0) for at in blocks])
-    bias_here = jnp.concatenate([part(ln_bias, at, width, 0) for at in blocks])
-    mean = jnp.mean(whole, axis=1, keepdims=True)
-    centred = whole - mean
-    inv_scale = lax.rsqrt(jnp.mean(centred * centred, axis=1, keepdims=True) + norm_epsilon)
-    normed = bf16(centred * inv_scale * gain_here + bias_here)
-    normed = jnp.concatenate([normed, swap_core(normed)], axis=0)
-    grad = gather_line(cotangent, blocks, col)
-    grad = jnp.concatenate([grad, swap_core(grad)], axis=0)
-
-    mixed = matmul(normed, qkv_full) + part(b_qkv, core, 3 * heads_width, 0)
-    query, keyval = split_heads(mixed, rotary)
+    grad_near = to_all(after(cotangent, tokens_near))
+    normed, normed_plain, normal, inv_scale = step(
+        lambda mine, theirs: gathered(place, mine, theirs, (ln_gain, ln_bias)),
+        tokens_near,
+        swap_core(tokens_near),
+    )
+    normed_own = normed[:, :half]
+
+    qkv_full = fill(qkv_whole, qkv_row, 0)
+    mixed = step(
+        lambda left, right: matmul(left, right) + part(b_qkv, core, 3 * heads_width, 0), normed, qkv_full
+    )
+    query, keyval = step(lambda values: split_heads(values, rotary), mixed)
     trunk = lax.ppermute(keyval, "row", [(0, 1)])
-    hidden_up = matmul(normed, up_full) + part(b_up, core, hidden, 0)
     root = math.sqrt(2.0 / math.pi)
-    squared = hidden_up * hidden_up
-    bend = jnp.tanh(root * (hidden_up + 0.044715 * squared * hidden_up))
-    activated = bf16(0.5 * hidden_up * (1.0 + bend))
-    slope = bf16(
-        0.5 * (1.0 + bend)
-        + 0.5 * hidden_up * (1.0 - bend * bend) * root * (1.0 + 3.0 * 0.044715 * squared)
-    )
-
-    def reduced(left, right, name):
-        sent = swap_row(bf16(left()))
-        both = bf16(right() + f32(sent))
-        return bf16(f32(both) + f32(swap_x(both)))
-
-    down_dims = ((0,), (0,))
-    across = ((1,), (1,))
-    grad_own, grad_other = grad[:, :half], grad[:, half:]
-    normed_own, normed_other = normed[:, :half], normed[:, half:]
-    cut = hidden // 4
-    down_first = reduced(
-        lambda: matmul(activated[:, :cut], grad_other, down_dims),
-        lambda: matmul(activated[:, :cut], grad_own, down_dims),
-        "down_first",
-    )
-    down_last = reduced(
-        lambda: matmul(activated[:, cut:], grad_other, down_dims),
-        lambda: matmul(activated[:, cut:], grad_own, down_dims),
-        "down_last",
-    )
-    down_sum = jnp.concatenate([down_first, down_last], axis=0)
-    down_grad = f32(pair(core, down_sum, swap_core(down_sum), 0))
-
-    act_grad = matmul(grad, down_full, across)
-    up_grad = bf16(act_grad * f32(slope))
-    up_sum = reduced(
-        lambda: matmul(normed_other, up_grad, down_dims),
-        lambda: matmul(normed_own, up_grad, down_dims),
-        "up",
-    )
-    up_weight_grad = f32(pair(core, up_sum, swap_core(up_sum), 1))
-
-    out_heads = bf16(matmul(grad, out_full, across))
-    row_table = jnp.reshape(row, (1,)).astype(jnp.int32)
-    attended, query_grad, own_grad, trunk_grad = tree_attention(
-        parents, row_table, query, keyval, trunk, out_heads
+
+    def feed(left, right):
+        hidden_up = matmul(left, right) + part(b_up, core, hidden, 0)
+        squared = hidden_up * hidden_up
+        bend = jnp.tanh(root * (hidden_up + 0.044715 * squared * hidden_up))
+        return bf16(0.5 * hidden_up * (1.0 + bend)), bf16(
+            0.5 * (1.0 + bend)
+            + 0.5 * hidden_up * (1.0 - bend * bend) * root * (1.0 + 3.0 * 0.044715 * squared)
+        )
+
+    up_full = fill(up_whole, up_row, 0)
+    activated, slope = step(feed, normed, up_full)
+    down_full = fill(down_whole, down_row, 1)
+    out_full = fill(out_whole, out_row, 1)
+
+    grad, grad_plain = step(
+        lambda mine, theirs: gathered(place, mine, theirs), grad_near, swap_core(grad_near)
+    )
+    grad_own = grad[:, :half]
+
+    def cut(values, at):
+        size = values.shape[1] // 2
+        return values[:, at * size : (at + 1) * size]
+
+    def leaving(left, right):
+        return step(lambda a, b: bf16(matmul(a, b, down_dims)), left, right)
+
+    def staying(left, right, sent):
+        return step(lambda a, b, c: bf16(matmul(a, b, down_dims) + f32(c)), left, right, sent)
+
+    def crossed(both, arrived):
+        mine = step(lambda a, b: bf16(f32(a) + f32(b)), both, arrived)
+        return mine, swap_core(mine)
+
+    def settled(pieces, shape, axis, offset, dest):
+        operands = pieces if dest is None else pieces + (dest,)
+        return step(
+            lambda mine, theirs, *rest: settle(place, mine, theirs, shape, axis, offset, *rest), *operands
+        )
+
+    down_sent_a = swap_row(leaving(cut(activated, 0), grad_plain))
+    down_sent_b = swap_row(leaving(cut(activated, 1), grad_plain))
+    out_heads = step(lambda a, b: bf16(matmul(a, b, across)), grad, out_full)
+    attended, query_grad, own_grad, trunk_grad = step(
+        lambda *operands: tree_attention(parents, row_table, *operands), query, keyval, trunk, out_heads
     )
     trunk_sent = lax.ppermute(trunk_grad, "row", [(1, 0)])
-    out_sum = reduced(
-        lambda: matmul(attended, grad_other, down_dims),
-        lambda: matmul(attended, grad_own, down_dims),
-        "out",
-    )
-    out_grad = f32(pair(core, out_sum, swap_core(out_sum), 0))
-    mixed_grad = join_heads(row_table, query_grad, own_grad, trunk_sent, rotary)
-    qkv_sum = reduced(
-        lambda: matmul(normed_other, mixed_grad, down_dims),
-        lambda: matmul(normed_own, mixed_grad, down_dims),
-        "qkv",
-    )
-    qkv_weight_grad = f32(pair(core, qkv_sum, swap_core(qkv_sum), 1))
-
-    def spread(terms):
-        mine = terms[:count] + f32(swap_core(bf16(terms[count:])))
-        mine = bf16(mine)
-        ordered = pair(row, mine[:, :half], mine[:, half:], 1)
-        stacked = jnp.stack([ordered[:, at * width : (at + 1) * width] for at in range(cols)])
-        swapped = lax.all_to_all(stacked, "col", 0, 0, tiled=True)
-        return jnp.sum(f32(swapped), axis=0)
-
-    branch = spread(matmul(attended, out_full) + matmul(activated, down_full))
-    output = bf16(f32(tokens) + branch + b_res)
-
-    norm_grad = spread(
-        matmul(mixed_grad, qkv_full, across) + matmul(up_grad, up_full, across)
-    )
-    normal = (f32(tokens) - mean) * inv_scale
+    down_both_a = staying(cut(activated, 0), grad_own, down_sent_a)
+    down_cross_a = swap_x(down_both_a)
+    up_grad = step(lambda a, b, c: bf16(matmul(a, b, across) * f32(c)), grad, down_full, slope)
+    up_sent_a = swap_row(leaving(cut(normed_plain, 0), up_grad))
+    down_both_b = staying(cut(activated, 1), grad_own, down_sent_b)
+    down_cross_b = swap_x(down_both_b)
+    up_sent_b = swap_row(leaving(cut(normed_plain, 1), up_grad))
+    out_sent = swap_row(leaving(attended, grad_plain))
+    down_a = crossed(down_both_a, down_cross_a)
+    branch_terms = step(
+        lambda a, b, c, d: matmul(a, b) + matmul(c, d), attended, out_full, activated, down_full
+    )
+    branch_near = swap_core(step(bf16, branch_terms[count:]))
+    mixed_grad = step(
+        lambda *operands: join_heads(row_table, *operands, rotary), query_grad, own_grad, trunk_sent
+    )
+    qkv_sent_a = swap_row(leaving(cut(normed_plain, 0), mixed_grad))
+    qkv_sent_b = swap_row(leaving(cut(normed_plain, 1), mixed_grad))
+    branch_parts = exchange(step(lambda a, b: stacked(place, a, b, cols), branch_terms, branch_near))
+    down_b = crossed(down_both_b, down_cross_b)
+    norm_terms = step(
+        lambda a, b, c, d: matmul(a, b, across) + matmul(c, d, across),
+        mixed_grad, qkv_full, up_grad, up_full,
+    )
+    norm_near = swap_core(step(bf16, norm_terms[count:]))
+    up_both_a = staying(cut(normed_own, 0), up_grad, up_sent_a)
+    up_cross_a = swap_x(up_both_a)
+    norm_parts = exchange(step(lambda a, b: stacked(place, a, b, cols), norm_terms, norm_near))
+    down_grad = settled(down_a, w_down.shape, 0, 0, None)
+    down_grad = settled(down_b, w_down.shape, 0, down_both_a.shape[0], down_grad)
+    output = step(
+        lambda parts, block: bf16(f32(block) + jnp.sum(f32(parts), axis=0) + b_res), branch_parts, tokens
+    )
+    up_both_b = staying(cut(normed_own, 1), up_grad, up_sent_b)
+    up_cross_b = swap_x(up_both_b)
+    norm_grad = step(lambda parts: jnp.sum(f32(parts), axis=0), norm_parts)
     scaled = norm_grad * part(ln_gain, col, width, 0)
     sums = jnp.stack([jnp.sum(scaled, axis=1), jnp.sum(scaled * normal, axis=1)])
-    shifted = [
-        lax.ppermute(sums, "col", [(at, (at + hop) % cols) for at in range(cols)])
-        for hop in range(1, cols)
-    ]
-    sums = functools.reduce(jnp.add, shifted, sums) / (cols * width)
-    tokens_grad = inv_scale * (
-        scaled - sums[0][:, None] - normal * sums[1][:, None]
-    ) + f32(cotangent)
-
+    for bit in (1, 2):
+        sums = sums + lax.ppermute(sums, "col", [(at, at ^ bit) for at in range(cols)])
+    up_a = crossed(up_both_a, up_cross_a)
+    out_both = staying(attended, grad_own, out_sent)
+    out_cross = swap_x(out_both)
+    sums = sums / (cols * width)
+    tokens_grad = step(
+        lambda sums, values: inv_scale
+        * (values - sums[0][:, None] - normal * sums[1][:, None])
+        + f32(cotangent),
+        sums, scaled,
+    )
     small = jnp.concatenate(
         [
             jnp.sum(f32(up_grad), axis=0),
@@ -759,27 +1004,45 @@
             jnp.sum(norm_grad, axis=0),
         ]
     ).reshape(-1, 128)
+    shared_at = (hidden + 3 * heads_width) // 128
+    small_other = swap_core(small)
+    shared = (small + small_other)[shared_at:]
+    res_at = width // 128
+    ends = shared[res_at:][None]
+    for bit in (1, 2):
+        ends = pair((col // bit) % 2, ends, lax.ppermute(ends, "col", [(at, at ^ bit) for at in range(cols)]), 0)
+    small = jnp.concatenate(
+        [
+            pair(core, small[: hidden // 128], small_other[: hidden // 128], 0),
+            pair(core, small[hidden // 128 : shared_at], small_other[hidden // 128 : shared_at], 0),
+            shared[:res_at],
+            ends.reshape(-1, 128),
+        ]
+    )
+    up_grad_weight = settled(up_a, w_up.shape, 1, 0, None)
+    qkv_both_a = staying(cut(normed_own, 0), mixed_grad, qkv_sent_a)
+    qkv_cross_a = swap_x(qkv_both_a)
+    up_b = crossed(up_both_b, up_cross_b)
     small = small + swap_row(small)
-    small = small + swap_x(small)
-    small, small_other = small.reshape(-1), swap_core(small).reshape(-1)
-    bounds = [0, hidden, hidden + 3 * heads_width]
-    up_bias_grad = pair(core, small[: bounds[1]], small_other[: bounds[1]], 0)
-    qkv_bias_grad = pair(
-        core, small[bounds[1] : bounds[2]], small_other[bounds[1] : bounds[2]], 0
-    )
-    shared = (small + small_other)[bounds[2] :].reshape(3, width)
-    res_bias_grad = shared[0]
-    norm_sums = shared[1:].reshape(-1, 128)
-    arrived = [norm_sums] + [
-        lax.ppermute(norm_sums, "col", [(at, (at + hop) % cols) for at in range(cols)])
-        for hop in range(1, cols)
-    ]
-    arrived = arrived[::-1]
-    arrived = jnp.stack(arrived + arrived[:-1])
-    arrived = lax.dynamic_slice_in_dim(arrived, cols - 1 - col, cols, 0)
-    arrived = arrived.reshape(cols, 2, width)
-    gain_grad = arrived[:, 0].reshape(-1)
-    shift_grad = arrived[:, 1].reshape(-1)
+    qkv_both_b = staying(cut(normed_own, 1), mixed_grad, qkv_sent_b)
+    qkv_cross_b = swap_x(qkv_both_b)
+    out_mine = crossed(out_both, out_cross)
+    up_weight_grad = settled(up_b, w_up.shape, 1, up_both_a.shape[0], up_grad_weight)
+    out_grad = settled(out_mine, w_out.shape, 0, 0, None)
+    qkv_a = crossed(qkv_both_a, qkv_cross_a)
+    qkv_weight_grad = settled(qkv_a, w_qkv.shape, 1, 0, None)
+    small = step(jnp.add, small, swap_x(small))
+    qkv_b = crossed(qkv_both_b, qkv_cross_b)
+    qkv_weight_grad = settled(qkv_b, w_qkv.shape, 1, qkv_both_a.shape[0], qkv_weight_grad)
+
+    bounds = [0, 2 * hidden // 128, (2 * hidden + 6 * heads_width) // 128]
+    bounds.append(bounds[-1] + res_at)
+    up_bias_grad = small[: bounds[1]].reshape(-1)
+    qkv_bias_grad = small[bounds[1] : bounds[2]].reshape(-1)
+    res_bias_grad = small[bounds[2] : bounds[3]].reshape(-1)
+    ends = small[bounds[3] :].reshape(cols, 2, width)
+    gain_grad = ends[:, 0].reshape(-1)
+    shift_grad = ends[:, 1].reshape(-1)
     return (
         output,
         tokens_grad,

time: 575 us -> 507 us (0.88)
  Pallas kernels: 28.3 us -> 106 us
  other arithmetic: 87.3 us -> 25.2 us
  waiting for transfers between devices: 220 us -> 182 us
  starting transfers between devices: 81.5 us -> 58.3 us
  matrix products: 95.7 us -> 80.3 us
  local copies, waits for them, and re-layouts: 53.8 us -> 45.5 us
    pallas_call x0 -> x15, Pallas kernels: none -> 77.4 us  [the longest x7 33.7 us: settle(): pl.pallas_call(settle_kernel, grid_spec=pltpu.PrefetchScalarGridSpec(num_...]
    ppermute x18 -> x4, waiting for transfers between devices: 44.3 us -> 4.75 us  [the longest x2 2.95 us: paired_device(): lax.ppermute(sums, 'col', [(at, at ^ bit) for at in range(cols)])]
    all_to_all x2 -> x4, waiting for transfers between devices: 10.7 us -> 46.4 us  [exchange(): return lax.all_to_all(stack, 'col', 0, 0, tiled=True)]
    ppermute x18 -> x4, starting transfers between devices: 36.7 us -> 5 us  [the longest x2 4.7 us: paired_device(): lax.ppermute(ends, 'col', [(at, at ^ bit) for at in range(cols)])]
    ppermute x10 -> x12, waiting for transfers between devices: 78.2 us -> 48.4 us  [swap_x(): return lax.ppermute(values, 'dp', SWAP_X)]
    ppermute x1, waiting for transfers between devices: 1.07 us -> 24.8 us  [paired_device(): trunk_sent = lax.ppermute(trunk_grad, 'row', [(1, 0)])]
    ppermute x10 -> x12, waiting for transfers between devices: 76.6 us -> 56.1 us  [swap_row(): return lax.ppermute(values, 'row', SWAP_ROW)]
    convert_element_type x4 -> x0, other arithmetic: 20.2 us -> none  [f32(): return values.astype(jnp.float32)]
  transfers between devices with their start and end apart: 52 -> 47, of which waited for: 24 -> 19; matrix products, arithmetic and copies ran while one was open for 37% -> 25% of each run, Pallas kernels for 4% -> 20%
where the time goes in v2:
time: 507 us; the launch traced here: 499 us
  waiting for transfers between devices  182 us (36%)
  Pallas kernels  106 us (21%)
  matrix products  80.3 us (16%)
  starting transfers between devices  58.3 us (11%)
  local copies, waits for them, and re-layouts  45.5 us (9%)
  other arithmetic  25.2 us (5%)
    dot_general x22, matrix products, matmul(): lax.dot_general(left, right, (dims, ((), ())), preferred_element_type=jnp...  80.3 us
    ppermute x12, waiting for transfers between devices, swap_row(): return lax.ppermute(values, 'row', SWAP_ROW)  56.1 us
    ppermute x12, waiting for transfers between devices, swap_x(): return lax.ppermute(values, 'dp', SWAP_X)  48.4 us
    all_to_all x4, waiting for transfers between devices, exchange(): return lax.all_to_all(stack, 'col', 0, 0, tiled=True)  46.4 us
    pallas_call x7, Pallas kernels, settle(): pl.pallas_call(settle_kernel, grid_spec=pltpu.PrefetchScalarGridSpec(num_...  33.7 us
    ppermute x1, waiting for transfers between devices, paired_device(): trunk_sent = lax.ppermute(trunk_grad, 'row', [(1, 0)])  24.8 us
    all_to_all x4, starting transfers between devices, exchange(): return lax.all_to_all(stack, 'col', 0, 0, tiled=True)  20.1 us
    pallas_call x1, Pallas kernels, tree_attention(): pl.pallas_call(tree_kernel, grid_spec=pltpu.PrefetchScalarGridSpec(num_sc...  18.4 us
  transfers between devices with their start and end apart: 47, of which 19 were waited for; matrix products, arithmetic and copies ran while one was open for 25% of the time, Pallas kernels for 20%

profile of v2, /device:TPU:0, one launch (start us, length us, event | category | flops | bytes accessed | tf_op | source)
XLA Modules:
  0.0 499.2 jit_solution(12621931945628116268)
XLA Ops:
  3.2 6.3 %all-to-all-start = ((bf16[4,512,512]{2,1,0:T(8,128)(2,1)}), bf16[4,512,512]{2,1,0:T(8,128)(2,1)S(1)}, u32[]{:S(2)}, u32[]{:S(2)}) async-start(bf16[4,512,512]{2,1,0:T(8,128)(2,1)} %broadcast_in_dim.81), calls=%async_computation | async-start | bytes 4194304 | tf_op jit(solution)/shard_map/all_to_all | solution.py:843
  15.1 5.3 %cast_weight.5 = (bf16[2048,1024]{1,0:T(8,128)(2,1)}, bf16[512,1024]{1,0:T(8,128)(2,1)}) custom-call(s32[4]{0:T(128)} %pad_add_fusion.1.place_ref, f32[1024,2048]{1,0:T(8,128)} %master_ref.1), custom_call_target="tpu_custom_call" | custom-call | flops 1048576 | bytes 7340032 | tf_op jit(solution)/shard_map/cast_weight/pallas_call | solution.py:667
  21.9 5.2 %cast_weight.6 = (bf16[1024,2048]{1,0:T(8,128)(2,1)}, bf16[1024,512]{1,0:T(8,128)(2,1)}) custom-call(s32[4]{0:T(128)} %pad_add_fusion.1.place_ref, f32[2048,1024]{1,0:T(8,128)} %master_ref.2), custom_call_target="tpu_custom_call" | custom-call | flops 1048576 | bytes 7340032 | tf_op jit(solution)/shard_map/cast_weight/pallas_call | solution.py:667
  29.2 28.6 %all-to-all-done.mine_ref = bf16[4,512,512]{2,1,0:T(8,128)(2,1)S(1)} async-done(((bf16[4,512,512]{2,1,0:T(8,128)(2,1)}), bf16[4,512,512]{2,1,0:T(8,128)(2,1)S(1)}, u32[]{:S(2)}, u32[]{:S(2)}) %all-to-all-start) | async-done | bytes 2097184 | tf_op jit(solution)/shard_map/all_to_all | solution.py:843
  70.7 15.4 %collective-permute-done.2 = bf16[512,768]{1,0:T(8,128)(2,1)} collective-permute-done((bf16[512,768]{1,0:T(8,128)(2,1)}, bf16[512,768]{1,0:T(8,128)(2,1)}, u32[]{:S(2)}, u32[]{:S(2)}) %collective-permute-start.2) | collective-permute-done | bytes 786464 | tf_op jit(solution)/shard_map/ppermute | solution.py:335
  100.5 6.1 %collective-permute-done.3 = bf16[512,768]{1,0:T(8,128)(2,1)S(1)} collective-permute-done((bf16[512,768]{1,0:T(8,128)(2,1)}, bf16[512,768]{1,0:T(8,128)(2,1)S(1)}, u32[]{:S(2)}, u32[]{:S(2)}) %collective-permute-start.3) | collective-permute-done | bytes 786464 | tf_op jit(solution)/shard_map/ppermute | solution.py:339
  107.7 21.5 %collective-permute-done.7 = bf16[512,1024]{1,0:T(8,128)(2,1)S(1)} collective-permute-done((bf16[512,1024]{1,0:T(8,128)(2,1)}, bf16[512,1024]{1,0:T(8,128)(2,1)S(1)}, u32[]{:S(2)}, u32[]{:S(2)}) %collective-permute-start.7) | collective-permute-done | bytes 1048608 | tf_op jit(solution)/shard_map/ppermute | solution.py:339
  130.2 20.6 %collective-permute-done.11 = bf16[1024,512]{1,0:T(8,128)(2,1)S(1)} collective-permute-done((bf16[1024,512]{1,0:T(8,128)(2,1)}, bf16[1024,512]{1,0:T(8,128)(2,1)S(1)}, u32[]{:S(2)}, u32[]{:S(2)}) %collective-permute-start.11) | collective-permute-done | bytes 1048608 | tf_op jit(solution)/shard_map/ppermute | solution.py:339
  151.8 8.6 %norm_blocks.1 = (bf16[2,512,2048]{2,1,0:T(8,128)(2,1)}, bf16[2,512,1024]{2,1,0:T(8,128)(2,1)}, f32[512,512]{1,0:T(8,128)}, f32[512,1]{1,0:T(8,128)}) custom-call(s32[4]{0:T(128)} %pad_add_fusion.1.place_ref, f32[4,512]{1,0:T(4,128)} %reshape.190.gain_ref, f32[4,512]{1,0:T(4,128)} %reshape.191.bias_ref, bf16[4,512,512]{2,1,0:T(8,128)(2,1)} %copy-done.5, ...), custom_call_target="tpu_custom_call" | custom-call | flops 10485760 | bytes 13107200 | tf_op jit(solution)/shard_map/norm_blocks/pallas_call | solution.py:580
  160.4 8.2 %convolution_add_fusion.2.mixed_ref = f32[1024,768]{1,0:T(8,128)} fusion(bf16[1024,2048]{1,0:T(8,128)(2,1)} %bitcast.83, bf16[2048,768]{1,0:T(8,128)(2,1)} %constant_dynamic-update-slice_fusion.11, f32[768]{0:T(1024)S(1)} %dynamic_slice.15), kind=kOutput, calls=%fused_computation.21 | convolution fusion | flops 3222011904 | bytes 10488832 | tf_op jit(solution)/shard_map/dot_general | solution.py:331
  182.8 10.1 %add_convert_fusion = (bf16[1024,1024]{1,0:T(8,128)(2,1)}, bf16[1024,1024]{1,0:T(8,128)(2,1)S(1)}) fusion(f32[1024]{0:T(1024)S(1)} %dynamic-slice-done, bf16[1024,2048]{1,0:T(8,128)(2,1)S(1)} %bitcast.84, bf16[2048,1024]{1,0:T(8,128)(2,1)} %constant_dynamic-update-slice_fusion.9), kind=kOutput, calls=%fused_computation.9 | convolution fusion | flops 4315938816 | bytes 12587008 | tf_op jit(solution)/shard_map/dot_general | solution.py:331
  196.2 6.2 %join_blocks.1 = (bf16[2,512,2048]{2,1,0:T(8,128)(2,1)}, bf16[2,512,1024]{2,1,0:T(8,128)(2,1)}) custom-call(s32[4]{0:T(128)} %pad_add_fusion.1.place_ref, bf16[4,512,512]{2,1,0:T(8,128)(2,1)} %all-to-all-done.1.mine_ref, bf16[4,512,512]{2,1,0:T(8,128)(2,1)} %copy-done.29), custom_call_target="tpu_custom_call" | custom-call | flops 10485760 | bytes 13107200 | tf_op jit(solution)/shard_map/join_blocks/pallas_call | solution.py:580
  214.3 18.4 %tree_attention.1 = (bf16[1024,256]{1,0:T(8,128)(2,1)}, f32[1024,256]{1,0:T(8,128)}, f32[1024,512]{1,0:T(8,128)}, bf16[1024,512]{1,0:T(8,128)(2,1)}) custom-call(s32[2,4]{1,0:T(2,128)} %bitcast.105, s32[1]{0:T(128)} %bitcast.1.row_ref, bf16[1024,256]{1,0:T(8,128)(2,1)} %get-tuple-element.176.query_ref, bf16[1024,512]{1,0:T(8,128)(2,1)} %get-tuple-element.177.keyval_ref, ...), custom_call_target="tpu_custom_call" | custom-call | flops 9663676416 | bytes 5242880 | tf_op jit(solution)/shard_map/tree_attention/pallas_call | solution.py:777
  239.1 7.4 %convert_reduce_fusion.2 = (f32[1024]{0:T(1024)S(1)}, bf16[1024,1024]{1,0:T(8,128)(2,1)S(1)}) fusion(bf16[1024,1024]{1,0:T(8,128)(2,1)S(1)} %copy-done.58, bf16[1024,2048]{1,0:T(8,128)(2,1)S(1)} %bitcast.88, bf16[1024,2048]{1,0:T(8,128)(2,1)} %constant_dynamic-update-slice_fusion.5), kind=kOutput, calls=%fused_computation.6 | convolution fusion | flops 4300209152 | bytes 12587008 | tf_op jit(solution)/shard_map/dot_general | solution.py:331
  248.8 7.5 %collective-permute-done.14 = bf16[512,1024]{1,0:T(8,128)(2,1)} collective-permute-done((bf16[512,1024]{1,0:T(8,128)(2,1)}, bf16[512,1024]{1,0:T(8,128)(2,1)}, u32[]{:S(2)}, u32[]{:S(2)}) %collective-permute-start.14) | collective-permute-done | bytes 1048608 | tf_op jit(solution)/shard_map/ppermute | solution.py:335
  279.2 24.8 %collective-permute-done.16.sent_ref = bf16[1024,512]{1,0:T(8,128)(2,1)S(1)} collective-permute-done((bf16[1024,512]{1,0:T(8,128)(2,1)S(1)}, bf16[1024,512]{1,0:T(8,128)(2,1)S(1)}, u32[]{:S(2)}, u32[]{:S(2)}) %collective-permute-start.16) | collective-permute-done | bytes 1048608 | tf_op jit(solution)/shard_map/ppermute | solution.py:947
  305.0 5.2 %join_heads.1 = bf16[1024,768]{1,0:T(8,128)(2,1)} custom-call(s32[1]{0:T(128)} %bitcast.1.row_ref, f32[1024,256]{1,0:T(8,128)} %get-tuple-element.206.dq_ref, f32[1024,512]{1,0:T(8,128)} %get-tuple-element.207.dkv_ref, bf16[1024,512]{1,0:T(8,128)(2,1)} %copy-done.44, f32[1024,128]{1,0:T(8,128)} %get-tuple-element.295.cos_ref, ...), custom_call_target="tpu_custom_call" | custom-call | flops 15728640 | bytes 6291456 | tf_op jit(solution)/shard_map/join_heads/pallas_call | solution.py:756
  315.6 5.3 %stack_blocks.2 = bf16[4,512,512]{2,1,0:T(8,128)(2,1)} custom-call(s32[4]{0:T(128)} %pad_add_fusion.1.place_ref, f32[1024,2048]{1,0:T(8,128)} %copy-done, bf16[512,2048]{1,0:T(8,128)(2,1)} %collective-permute-done.15.arrived_ref), custom_call_target="tpu_custom_call" | custom-call | flops 1048576 | bytes 8388608 | tf_op jit(solution)/shard_map/stack_blocks/pallas_call | solution.py:610
  328.8 6.5 %fusion.37 = f32[1024,2048]{1,0:T(8,128)S(1)} fusion(bf16[1024,1024]{1,0:T(8,128)(2,1)S(1)} %copy-done.7, bf16[2048,1024]{1,0:T(8,128)(2,1)} %constant_dynamic-update-slice_fusion.9), kind=kOutput, calls=%fused_computation.124 | convolution fusion | flops 4294967296 | bytes 14680064 | tf_op jit(solution)/shard_map/dot_general | solution.py:331
  345.3 19.5 %collective-permute-done.21 = bf16[512,1024]{1,0:T(8,128)(2,1)S(1)} collective-permute-done((bf16[512,1024]{1,0:T(8,128)(2,1)S(1)}, bf16[512,1024]{1,0:T(8,128)(2,1)S(1)}, u32[]{:S(2)}, u32[]{:S(2)}) %collective-permute-start.21) | collective-permute-done | bytes 1048608 | tf_op jit(solution)/shard_map/ppermute | solution.py:335
  367.0 5.3 %stack_blocks.3 = bf16[4,512,512]{2,1,0:T(8,128)(2,1)} custom-call(s32[4]{0:T(128)} %pad_add_fusion.1.place_ref, f32[1024,2048]{1,0:T(8,128)} %copy-done.2, bf16[512,2048]{1,0:T(8,128)(2,1)} %collective-permute-done.20.arrived_ref), custom_call_target="tpu_custom_call" | custom-call | flops 1048576 | bytes 8388608 | tf_op jit(solution)/shard_map/stack_blocks/pallas_call | solution.py:610
  399.7 5.6 %collective-permute-done.22 = bf16[512,1024]{1,0:T(8,128)(2,1)} collective-permute-done((bf16[512,1024]{1,0:T(8,128)(2,1)}, bf16[512,1024]{1,0:T(8,128)(2,1)}, u32[]{:S(2)}, u32[]{:S(2)}) %collective-permute-start.22) | collective-permute-done | bytes 1048608 | tf_op jit(solution)/shard_map/ppermute | solution.py:335
  409.9 16.3 %all-to-all-done.3 = bf16[4,512,512]{2,1,0:T(8,128)(2,1)} async-done(((bf16[4,512,512]{2,1,0:T(8,128)(2,1)}), bf16[4,512,512]{2,1,0:T(8,128)(2,1)}, u32[]{:S(2)}, u32[]{:S(2)}) %all-to-all-start.3) | async-done | bytes 2097184 | tf_op jit(solution)/shard_map/all_to_all | solution.py:843
  441.1 5.3 %settle.9.refs_0_ = f32[1024,2048]{1,0:T(8,128)} custom-call(s32[4]{0:T(128)} %pad_add_fusion.1.place_ref, bf16[512,1024]{1,0:T(8,128)(2,1)} %copy-done.17, bf16[512,1024]{1,0:T(8,128)(2,1)} %copy-done.43), custom_call_target="tpu_custom_call" | custom-call | bytes 6291456 | tf_op jit(solution)/shard_map/settle/pallas_call | solution.py:717
  (305 shorter events, 228.2 us)
Async XLA Ops:
  3.2 54.5 %all-to-all-start = ((bf16[4,512,512]{2,1,0:T(8,128)(2,1)}), bf16[4,512,512]{2,1,0:T(8,128)(2,1)S(1)}, u32[]{:S(2)}, u32[]{:S(2)}) async-start(bf16[4,512,512]{2,1,0:T(8,128)(2,1)} %broadcast_in_dim.81), calls=%async_computation | async-start | bytes 4194304 | tf_op jit(solution)/shard_map/all_to_all | solution.py:843
  20.4 66.8 %collective-permute-start.6 = (bf16[512,1024]{1,0:T(8,128)(2,1)}, bf16[512,1024]{1,0:T(8,128)(2,1)}, u32[]{:S(2)}, u32[]{:S(2)}) collective-permute-start(bf16[512,1024]{1,0:T(8,128)(2,1)} %get-tuple-element.146), channel_id=1, source_target_pairs={{0,4},{4,0},{1,5},{5,1},{2,6},{6,2},{3,7},{7,3},{8,12},{12,8},{9,1... | collective-permute-start | bytes 3145736 | tf_op jit(solution)/shard_map/ppermute | solution.py:335
  27.1 61.0 %collective-permute-start.10 = (bf16[1024,512]{1,0:T(8,128)(2,1)}, bf16[1024,512]{1,0:T(8,128)(2,1)}, u32[]{:S(2)}, u32[]{:S(2)}) collective-permute-start(bf16[1024,512]{1,0:T(8,128)(2,1)} %get-tuple-element.149), channel_id=1, source_target_pairs={{0,4},{4,0},{1,5},{5,1},{2,6},{6,2},{3,7},{7,3},{8,12},{12,8},{9,1... | collective-permute-start | bytes 3145736 | tf_op jit(solution)/shard_map/ppermute | solution.py:335
  27.6 58.4 %collective-permute-start.2 = (bf16[512,768]{1,0:T(8,128)(2,1)}, bf16[512,768]{1,0:T(8,128)(2,1)}, u32[]{:S(2)}, u32[]{:S(2)}) collective-permute-start(bf16[512,768]{1,0:T(8,128)(2,1)} %get-tuple-element.143), channel_id=1, source_target_pairs={{0,4},{4,0},{1,5},{5,1},{2,6},{6,2},{3,7},{7,3},{8,12},{12,8},{9,1... | collective-permute-start | bytes 2359304 | tf_op jit(solution)/shard_map/ppermute | solution.py:335
  59.4 119.7 %all-to-all-start.1 = ((bf16[4,512,512]{2,1,0:T(8,128)(2,1)}), bf16[4,512,512]{2,1,0:T(8,128)(2,1)}, u32[]{:S(2)}, u32[]{:S(2)}) async-start(bf16[4,512,512]{2,1,0:T(8,128)(2,1)} %broadcast_in_dim.92), calls=%async_computation.1 | async-start | bytes 4194304 | tf_op jit(solution)/shard_map/all_to_all | solution.py:843
  64.0 87.8 %collective-permute-start.1 = (bf16[4,512,512]{2,1,0:T(8,128)(2,1)S(1)}, bf16[4,512,512]{2,1,0:T(8,128)(2,1)}, u32[]{:S(2)}, u32[]{:S(2)}) collective-permute-start(bf16[4,512,512]{2,1,0:T(8,128)(2,1)S(1)} %all-to-all-done.mine_ref), channel_id=1, source_target_pairs={{0,8},{8,0},{16,24},{24,16},{1,9},{9,1},{17,25},{25,17},{2,10},{10... | collective-permute-start | bytes 6291464 | tf_op jit(solution)/shard_map/ppermute | solution.py:343
  87.2 41.9 %collective-permute-start.7 = (bf16[512,1024]{1,0:T(8,128)(2,1)}, bf16[512,1024]{1,0:T(8,128)(2,1)S(1)}, u32[]{:S(2)}, u32[]{:S(2)}) collective-permute-start(bf16[512,1024]{1,0:T(8,128)(2,1)} %collective-permute-done.6), channel_id=1, source_target_pairs={{0,16},{16,0},{8,24},{24,8},{1,17},{17,1},{9,25},{25,9},{2,18},{18... | collective-permute-start | bytes 3145736 | tf_op jit(solution)/shard_map/ppermute | solution.py:339
  88.2 62.6 %collective-permute-start.11 = (bf16[1024,512]{1,0:T(8,128)(2,1)}, bf16[1024,512]{1,0:T(8,128)(2,1)S(1)}, u32[]{:S(2)}, u32[]{:S(2)}) collective-permute-start(bf16[1024,512]{1,0:T(8,128)(2,1)} %collective-permute-done.10), channel_id=1, source_target_pairs={{0,16},{16,0},{8,24},{24,8},{1,17},{17,1},{9,25},{25,9},{2,18},{18... | collective-permute-start | bytes 3145736 | tf_op jit(solution)/shard_map/ppermute | solution.py:339
  93.1 86.0 %collective-permute-start.9 = (bf16[256,512]{1,0:T(8,128)(2,1)S(1)}, bf16[256,512]{1,0:T(8,128)(2,1)S(1)}, u32[]{:S(2)}, u32[]{:S(2)}) collective-permute-start(bf16[256,512]{1,0:T(8,128)(2,1)S(1)} %collective-permute-done.8), channel_id=1, source_target_pairs={{0,16},{16,0},{8,24},{24,8},{1,17},{17,1},{9,25},{25,9},{2,18},{18... | collective-permute-start | bytes 786440 | tf_op jit(solution)/shard_map/ppermute | solution.py:339
  173.7 40.6 %collective-permute-start.4 = (bf16[1024,512]{1,0:T(8,128)(2,1)}, bf16[1024,512]{1,0:T(8,128)(2,1)}, u32[]{:S(2)}, u32[]{:S(2)}) collective-permute-start(bf16[1024,512]{1,0:T(8,128)(2,1)} %get-tuple-element.177.keyval_ref), channel_id=1, source_target_pairs={{0,4},{1,5},{2,6},{3,7},{8,12},{9,13},{10,14},{11,15},{16,20},{17,... | collective-permute-start | bytes 3145736 | tf_op jit(solution)/shard_map/ppermute | solution.py:899
  207.9 26.3 %collective-permute-start.12 = (bf16[512,1024]{1,0:T(8,128)(2,1)}, bf16[512,1024]{1,0:T(8,128)(2,1)}, u32[]{:S(2)}, u32[]{:S(2)}) collective-permute-start(bf16[512,1024]{1,0:T(8,128)(2,1)} %convolution_convert_fusion.3), channel_id=1, source_target_pairs={{0,4},{4,0},{1,5},{5,1},{2,6},{6,2},{3,7},{7,3},{8,12},{12,8},{9,1... | collective-permute-start | bytes 3145736 | tf_op jit(solution)/shard_map/ppermute | solution.py:335
  210.2 46.1 %collective-permute-start.14 = (bf16[512,1024]{1,0:T(8,128)(2,1)}, bf16[512,1024]{1,0:T(8,128)(2,1)}, u32[]{:S(2)}, u32[]{:S(2)}) collective-permute-start(bf16[512,1024]{1,0:T(8,128)(2,1)} %convolution_convert_fusion.2), channel_id=1, source_target_pairs={{0,4},{4,0},{1,5},{5,1},{2,6},{6,2},{3,7},{7,3},{8,12},{12,8},{9,1... | collective-permute-start | bytes 3145736 | tf_op jit(solution)/shard_map/ppermute | solution.py:335
  276.6 39.1 %collective-permute-start.15 = (bf16[512,2048]{1,0:T(8,128)(2,1)}, bf16[512,2048]{1,0:T(8,128)(2,1)}, u32[]{:S(2)}, u32[]{:S(2)}) collective-permute-start(bf16[512,2048]{1,0:T(8,128)(2,1)} %slice.122), channel_id=1, source_target_pairs={{0,8},{8,0},{16,24},{24,16},{1,9},{9,1},{17,25},{25,17},{2,10},{10... | collective-permute-start | bytes 6291464 | tf_op jit(solution)/shard_map/ppermute | solution.py:343
  276.6 27.5 %collective-permute-start.16 = (bf16[1024,512]{1,0:T(8,128)(2,1)S(1)}, bf16[1024,512]{1,0:T(8,128)(2,1)S(1)}, u32[]{:S(2)}, u32[]{:S(2)}) collective-permute-start(bf16[1024,512]{1,0:T(8,128)(2,1)S(1)} %copy-done.57), channel_id=1, source_target_pairs={{4,0},{5,1},{6,2},{7,3},{12,8},{13,9},{14,10},{15,11},{20,16},{21,... | collective-permute-start | bytes 3145736 | tf_op jit(solution)/shard_map/ppermute | solution.py:947
  278.0 47.7 %collective-permute-start.17 = (bf16[512,1024]{1,0:T(8,128)(2,1)}, bf16[512,1024]{1,0:T(8,128)(2,1)}, u32[]{:S(2)}, u32[]{:S(2)}) collective-permute-start(bf16[512,1024]{1,0:T(8,128)(2,1)} %add_convert_fusion.7), channel_id=1, source_target_pairs={{0,16},{16,0},{8,24},{24,8},{1,17},{17,1},{9,25},{25,9},{2,18},{18... | collective-permute-start | bytes 3145736 | tf_op jit(solution)/shard_map/ppermute | solution.py:339
  320.9 53.0 %all-to-all-start.2 = ((bf16[4,512,512]{2,1,0:T(8,128)(2,1)}), bf16[4,512,512]{2,1,0:T(8,128)(2,1)}, u32[]{:S(2)}, u32[]{:S(2)}) async-start(bf16[4,512,512]{2,1,0:T(8,128)(2,1)} %stack_blocks.2), calls=%async_computation.2 | async-start | bytes 4194304 | tf_op jit(solution)/shard_map/all_to_all | solution.py:843
  339.1 27.9 %collective-permute-start.20 = (bf16[512,2048]{1,0:T(8,128)(2,1)S(1)}, bf16[512,2048]{1,0:T(8,128)(2,1)}, u32[]{:S(2)}, u32[]{:S(2)}) collective-permute-start(bf16[512,2048]{1,0:T(8,128)(2,1)S(1)} %slice.123), channel_id=1, source_target_pairs={{0,8},{8,0},{16,24},{24,16},{1,9},{9,1},{17,25},{25,17},{2,10},{10... | collective-permute-start | bytes 6291464 | tf_op jit(solution)/shard_map/ppermute | solution.py:343
  373.9 52.3 %all-to-all-start.3 = ((bf16[4,512,512]{2,1,0:T(8,128)(2,1)}), bf16[4,512,512]{2,1,0:T(8,128)(2,1)}, u32[]{:S(2)}, u32[]{:S(2)}) async-start(bf16[4,512,512]{2,1,0:T(8,128)(2,1)} %stack_blocks.3), calls=%async_computation.3 | async-start | bytes 4194304 | tf_op jit(solution)/shard_map/all_to_all | solution.py:843
  379.2 52.6 %collective-permute-start.25 = (bf16[256,1024]{1,0:T(8,128)(2,1)}, bf16[256,1024]{1,0:T(8,128)(2,1)}, u32[]{:S(2)}, u32[]{:S(2)}) collective-permute-start(bf16[256,1024]{1,0:T(8,128)(2,1)} %convolution_convert_fusion.6), channel_id=1, source_target_pairs={{0,4},{4,0},{1,5},{5,1},{2,6},{6,2},{3,7},{7,3},{8,12},{12,8},{9,1... | collective-permute-start | bytes 1572872 | tf_op jit(solution)/shard_map/ppermute | solution.py:335
  381.2 74.3 %collective-permute-start.27 = (bf16[512,768]{1,0:T(8,128)(2,1)}, bf16[512,768]{1,0:T(8,128)(2,1)}, u32[]{:S(2)}, u32[]{:S(2)}) collective-permute-start(bf16[512,768]{1,0:T(8,128)(2,1)} %convolution_convert_fusion.4), channel_id=1, source_target_pairs={{0,4},{4,0},{1,5},{5,1},{2,6},{6,2},{3,7},{7,3},{8,12},{12,8},{9,1... | collective-permute-start | bytes 2359304 | tf_op jit(solution)/shard_map/ppermute | solution.py:335
  383.0 66.3 %collective-permute-start.29 = (bf16[512,768]{1,0:T(8,128)(2,1)}, bf16[512,768]{1,0:T(8,128)(2,1)}, u32[]{:S(2)}, u32[]{:S(2)}) collective-permute-start(bf16[512,768]{1,0:T(8,128)(2,1)} %convolution_convert_fusion.5), channel_id=1, source_target_pairs={{0,4},{4,0},{1,5},{5,1},{2,6},{6,2},{3,7},{7,3},{8,12},{12,8},{9,1... | collective-permute-start | bytes 2359304 | tf_op jit(solution)/shard_map/ppermute | solution.py:335
  390.2 39.0 %collective-permute-start.26 = (bf16[512,1024]{1,0:T(8,128)(2,1)}, bf16[512,1024]{1,0:T(8,128)(2,1)}, u32[]{:S(2)}, u32[]{:S(2)}) collective-permute-start(bf16[512,1024]{1,0:T(8,128)(2,1)} %add_convert_fusion.4), channel_id=1, source_target_pairs={{0,16},{16,0},{8,24},{24,8},{1,17},{17,1},{9,25},{25,9},{2,18},{18... | collective-permute-start | bytes 3145736 | tf_op jit(solution)/shard_map/ppermute | solution.py:339
  408.8 44.8 %collective-permute-start.28 = (bf16[512,1024]{1,0:T(8,128)(2,1)}, bf16[512,1024]{1,0:T(8,128)(2,1)}, u32[]{:S(2)}, u32[]{:S(2)}) collective-permute-start(bf16[512,1024]{1,0:T(8,128)(2,1)} %add_convert_fusion.3), channel_id=1, source_target_pairs={{0,16},{16,0},{8,24},{24,8},{1,17},{17,1},{9,25},{25,9},{2,18},{18... | collective-permute-start | bytes 3145736 | tf_op jit(solution)/shard_map/ppermute | solution.py:339
  463.5 26.8 %collective-permute-start.31 = (bf16[512,768]{1,0:T(8,128)(2,1)S(1)}, bf16[512,768]{1,0:T(8,128)(2,1)S(1)}, u32[]{:S(2)}, u32[]{:S(2)}) collective-permute-start(bf16[512,768]{1,0:T(8,128)(2,1)S(1)} %add_convert_fusion.11), channel_id=1, source_target_pairs={{0,16},{16,0},{8,24},{24,8},{1,17},{17,1},{9,25},{25,9},{2,18},{18... | collective-permute-start | bytes 2359304 | tf_op jit(solution)/shard_map/ppermute | solution.py:339
  (85 other events, 700.9 us)

commit v3 on v2

--- a/solution.py
+++ b/solution.py
@@ -583,9 +583,7 @@
             num_scalar_prefetch=1, grid=(count // rows,), in_specs=in_specs, out_specs=out_specs
         ),
         out_shape=out_shape,
-        cost_estimate=pl.CostEstimate(
-            flops=40 * count * width, bytes_accessed=50 * count * width, transcendentals=0
-        ),
+        cost_estimate=pl.CostEstimate(flops=1, bytes_accessed=1, transcendentals=0),
         name="join_blocks" if norm is None else "norm_blocks",
     )(place, *operands)
     return [values.reshape(2 * count, -1) for values in results[:2]] + list(results[2:])
@@ -616,7 +614,7 @@
             out_specs=pl.BlockSpec((blocks, rows, width), lambda at, *_: (0, at, 0)),
         ),
         out_shape=jax.ShapeDtypeStruct((blocks, count, width), jnp.bfloat16),
-        cost_estimate=pl.CostEstimate(flops=count * full, bytes_accessed=8 * count * full, transcendentals=0),
+        cost_estimate=pl.CostEstimate(flops=1, bytes_accessed=1, transcendentals=0),
         name="stack_blocks",
     )(place, terms, arrived)
 
@@ -673,7 +671,7 @@
             jax.ShapeDtypeStruct(whole, jnp.bfloat16),
             jax.ShapeDtypeStruct(send, jnp.bfloat16),
         ],
-        cost_estimate=pl.CostEstimate(flops=height * width, bytes_accessed=7 * height * width, transcendentals=0),
+        cost_estimate=pl.CostEstimate(flops=1, bytes_accessed=1, transcendentals=0),
         name="cast_weight",
     )(place, master)
 
@@ -724,7 +722,7 @@
         ),
         out_shape=jax.ShapeDtypeStruct(shape, jnp.float32),
         input_output_aliases=aliases,
-        cost_estimate=pl.CostEstimate(flops=0, bytes_accessed=12 * mine.size, transcendentals=0),
+        cost_estimate=pl.CostEstimate(flops=1, bytes_accessed=1, transcendentals=0),
         name="settle",
     )(*operands)
 
@@ -745,7 +743,7 @@
             jax.ShapeDtypeStruct((count, width // 3), jnp.bfloat16),
             jax.ShapeDtypeStruct((count, 2 * width // 3), jnp.bfloat16),
         ],
-        cost_estimate=pl.CostEstimate(flops=20 * count * width, bytes_accessed=8 * count * width, transcendentals=0),
+        cost_estimate=pl.CostEstimate(flops=1, bytes_accessed=1, transcendentals=0),
         name="split_heads",
     )(mixed, *tables)
 
@@ -763,7 +761,7 @@
             out_specs=row_block(rows, 3 * half),
         ),
         out_shape=jax.ShapeDtypeStruct((count, 3 * half), jnp.bfloat16),
-        cost_estimate=pl.CostEstimate(flops=60 * count * half, bytes_accessed=24 * count * half, transcendentals=0),
+        cost_estimate=pl.CostEstimate(flops=1, bytes_accessed=1, transcendentals=0),
         name="join_heads",
     )(row, dq, dkv, sent, *tables)
 
@@ -800,9 +798,7 @@
             jax.ShapeDtypeStruct((count, 2 * half), jnp.float32),
             jax.ShapeDtypeStruct((trees * keys, 2 * half), jnp.bfloat16),
         ],
-        cost_estimate=pl.CostEstimate(
-            flops=12 * pairs * half, bytes_accessed=20 * count * half, transcendentals=pairs
-        ),
+        cost_estimate=pl.CostEstimate(flops=1, bytes_accessed=1, transcendentals=0),
         name="tree_attention",
     )(parents, row, query, keyval, trunk, grad)
 
@@ -854,19 +850,17 @@
         done = result
         return result
 
+    def wait(value):
+        return step(lambda arrived: arrived, value)
+
     tokens_near = to_all(tokens)
+    grad_near = lax.all_gather(cotangent, "col", axis=0)
 
     def ready(master, axis):
         whole, send = step(lambda weight: cast_weight(place, weight, axis), master)
         return whole, swap_row(send)
 
-    qkv_whole, qkv_row = ready(w_qkv, 0)
-    up_whole, up_row = ready(w_up, 0)
-    down_whole, down_row = ready(w_down, 1)
-    out_whole, out_row = ready(w_out, 1)
-
-    def fill(whole, by_row, axis):
-        by_x = swap_x(by_row)
+    def fill(whole, by_row, by_x, axis):
         start = whole.shape[axis] // 2
         whole = lax.dynamic_update_slice_in_dim(whole, by_row, start, axis)
         return lax.dynamic_update_slice_in_dim(whole, by_x, start + by_row.shape[axis], axis)
@@ -883,15 +877,26 @@
     positions = (levels * SEG + (token % SEG).astype(jnp.float32)[None, :]).reshape(2 * count)
     rotary = rotary_tables(positions)
 
-    grad_near = to_all(after(cotangent, tokens_near))
+    qkv_whole, qkv_row = ready(w_qkv, 0)
+    up_whole, up_row = ready(w_up, 0)
+    qkv_row = wait(qkv_row)
+    qkv_x = swap_x(qkv_row)
+    out_whole, out_row = ready(w_out, 1)
+    down_whole, down_row = ready(w_down, 1)
+    rotary = step(lambda *tables: tables, *rotary)
+    up_row = wait(up_row)
+    up_x = swap_x(up_row)
+    qkv_x = wait(qkv_x)
+    tokens_near = wait(tokens_near)
+    tokens_far = swap_core(tokens_near)
+    out_row = wait(out_row)
+    out_x = swap_x(out_row)
     normed, normed_plain, normal, inv_scale = step(
-        lambda mine, theirs: gathered(place, mine, theirs, (ln_gain, ln_bias)),
-        tokens_near,
-        swap_core(tokens_near),
+        lambda mine, theirs: gathered(place, mine, theirs, (ln_gain, ln_bias)), tokens_near, tokens_far
     )
     normed_own = normed[:, :half]
-
-    qkv_full = fill(qkv_whole, qkv_row, 0)
+    grad_far = swap_core(grad_near)
+    qkv_full = step(lambda *parts: fill(*parts, 0), qkv_whole, qkv_row, qkv_x)
     mixed = step(
         lambda left, right: matmul(left, right) + part(b_qkv, core, 3 * heads_width, 0), normed, qkv_full
     )
@@ -908,14 +913,11 @@
             + 0.5 * hidden_up * (1.0 - bend * bend) * root * (1.0 + 3.0 * 0.044715 * squared)
         )
 
-    up_full = fill(up_whole, up_row, 0)
+    up_full = step(lambda *parts: fill(*parts, 0), up_whole, up_row, up_x)
     activated, slope = step(feed, normed, up_full)
-    down_full = fill(down_whole, down_row, 1)
-    out_full = fill(out_whole, out_row, 1)
-
-    grad, grad_plain = step(
-        lambda mine, theirs: gathered(place, mine, theirs), grad_near, swap_core(grad_near)
-    )
+    down_row = wait(down_row)
+    down_x = swap_x(down_row)
+    grad, grad_plain = step(lambda mine, theirs: gathered(place, mine, theirs), grad_near, grad_far)
     grad_own = grad[:, :half]
 
     def cut(values, at):
@@ -940,6 +942,7 @@
 
     down_sent_a = swap_row(leaving(cut(activated, 0), grad_plain))
     down_sent_b = swap_row(leaving(cut(activated, 1), grad_plain))
+    out_full = step(lambda *parts: fill(*parts, 1), out_whole, out_row, out_x)
     out_heads = step(lambda a, b: bf16(matmul(a, b, across)), grad, out_full)
     attended, query_grad, own_grad, trunk_grad = step(
         lambda *operands: tree_attention(parents, row_table, *operands), query, keyval, trunk, out_heads
@@ -947,93 +950,118 @@
     trunk_sent = lax.ppermute(trunk_grad, "row", [(1, 0)])
     down_both_a = staying(cut(activated, 0), grad_own, down_sent_a)
     down_cross_a = swap_x(down_both_a)
+    down_full = step(lambda *parts: fill(*parts, 1), down_whole, down_row, down_x)
     up_grad = step(lambda a, b, c: bf16(matmul(a, b, across) * f32(c)), grad, down_full, slope)
     up_sent_a = swap_row(leaving(cut(normed_plain, 0), up_grad))
     down_both_b = staying(cut(activated, 1), grad_own, down_sent_b)
     down_cross_b = swap_x(down_both_b)
     up_sent_b = swap_row(leaving(cut(normed_plain, 1), up_grad))
-    out_sent = swap_row(leaving(attended, grad_plain))
     down_a = crossed(down_both_a, down_cross_a)
     branch_terms = step(
         lambda a, b, c, d: matmul(a, b) + matmul(c, d), attended, out_full, activated, down_full
     )
-    branch_near = swap_core(step(bf16, branch_terms[count:]))
+    down_grad = settled(down_a, w_down.shape, 0, 0, None)
     mixed_grad = step(
         lambda *operands: join_heads(row_table, *operands, rotary), query_grad, own_grad, trunk_sent
     )
     qkv_sent_a = swap_row(leaving(cut(normed_plain, 0), mixed_grad))
+    down_b = crossed(down_both_b, down_cross_b)
     qkv_sent_b = swap_row(leaving(cut(normed_plain, 1), mixed_grad))
-    branch_parts = exchange(step(lambda a, b: stacked(place, a, b, cols), branch_terms, branch_near))
-    down_b = crossed(down_both_b, down_cross_b)
+    down_grad = settled(down_b, w_down.shape, 0, down_both_a.shape[0], down_grad)
+    branch_near = swap_core(step(bf16, branch_terms[count:]))
+    up_both_a = staying(cut(normed_own, 0), up_grad, up_sent_a)
+    up_cross_a = swap_x(up_both_a)
     norm_terms = step(
         lambda a, b, c, d: matmul(a, b, across) + matmul(c, d, across),
         mixed_grad, qkv_full, up_grad, up_full,
     )
+    branch_parts = exchange(step(lambda a, b: stacked(place, a, b, cols), branch_terms, branch_near))
     norm_near = swap_core(step(bf16, norm_terms[count:]))
-    up_both_a = staying(cut(normed_own, 0), up_grad, up_sent_a)
-    up_cross_a = swap_x(up_both_a)
+    up_both_b = staying(cut(normed_own, 1), up_grad, up_sent_b)
+    up_cross_b = swap_x(up_both_b)
+    up_a = crossed(up_both_a, up_cross_a)
+    qkv_both_a = staying(cut(normed_own, 0), mixed_grad, qkv_sent_a)
+    qkv_cross_a = swap_x(qkv_both_a)
     norm_parts = exchange(step(lambda a, b: stacked(place, a, b, cols), norm_terms, norm_near))
-    down_grad = settled(down_a, w_down.shape, 0, 0, None)
-    down_grad = settled(down_b, w_down.shape, 0, down_both_a.shape[0], down_grad)
+    out_sent = swap_row(leaving(attended, grad_plain))
+    up_weight_grad = settled(up_a, w_up.shape, 1, 0, None)
+    up_b = crossed(up_both_b, up_cross_b)
     output = step(
         lambda parts, block: bf16(f32(block) + jnp.sum(f32(parts), axis=0) + b_res), branch_parts, tokens
     )
-    up_both_b = staying(cut(normed_own, 1), up_grad, up_sent_b)
-    up_cross_b = swap_x(up_both_b)
-    norm_grad = step(lambda parts: jnp.sum(f32(parts), axis=0), norm_parts)
-    scaled = norm_grad * part(ln_gain, col, width, 0)
-    sums = jnp.stack([jnp.sum(scaled, axis=1), jnp.sum(scaled * normal, axis=1)])
-    for bit in (1, 2):
-        sums = sums + lax.ppermute(sums, "col", [(at, at ^ bit) for at in range(cols)])
-    up_a = crossed(up_both_a, up_cross_a)
-    out_both = staying(attended, grad_own, out_sent)
-    out_cross = swap_x(out_both)
-    sums = sums / (cols * width)
-    tokens_grad = step(
-        lambda sums, values: inv_scale
-        * (values - sums[0][:, None] - normal * sums[1][:, None])
-        + f32(cotangent),
-        sums, scaled,
-    )
+    qkv_both_b = staying(cut(normed_own, 1), mixed_grad, qkv_sent_b)
+    qkv_cross_b = swap_x(qkv_both_b)
+    up_weight_grad = settled(up_b, w_up.shape, 1, up_both_a.shape[0], up_weight_grad)
+    gain_here = part(ln_gain, col, width, 0)
+
+    def norm_sums(parts):
+        total = jnp.sum(f32(parts), axis=0)
+        scaled = total * gain_here
+        return (
+            total,
+            jnp.stack([jnp.sum(scaled, axis=1), jnp.sum(scaled * normal, axis=1)]),
+            jnp.sum(total * normal, axis=0),
+            jnp.sum(total, axis=0),
+        )
+
+    norm_grad, sums, gain_sum, shift_sum = step(norm_sums, norm_parts)
+
+    def line_step(values, bit):
+        return lax.ppermute(values, "col", [(at, at ^ bit) for at in range(cols)])
+
     small = jnp.concatenate(
         [
             jnp.sum(f32(up_grad), axis=0),
             jnp.sum(f32(mixed_grad), axis=0),
             jnp.sum(f32(cotangent), axis=0),
-            jnp.sum(norm_grad * normal, axis=0),
-            jnp.sum(norm_grad, axis=0),
+            gain_sum,
+            shift_sum,
         ]
     ).reshape(-1, 128)
     shared_at = (hidden + 3 * heads_width) // 128
+    res_at = width // 128
+    sums_next = line_step(sums, 1)
     small_other = swap_core(small)
-    shared = (small + small_other)[shared_at:]
-    res_at = width // 128
+    qkv_a = crossed(qkv_both_a, qkv_cross_a)
+    sums, shared = step(
+        lambda sums, arrived, small, other: (sums + arrived, (small + other)[shared_at:]),
+        sums, sums_next, small, small_other,
+    )
+    sums_next = line_step(sums, 2)
     ends = shared[res_at:][None]
-    for bit in (1, 2):
-        ends = pair((col // bit) % 2, ends, lax.ppermute(ends, "col", [(at, at ^ bit) for at in range(cols)]), 0)
-    small = jnp.concatenate(
-        [
-            pair(core, small[: hidden // 128], small_other[: hidden // 128], 0),
-            pair(core, small[hidden // 128 : shared_at], small_other[hidden // 128 : shared_at], 0),
-            shared[:res_at],
-            ends.reshape(-1, 128),
-        ]
-    )
-    up_grad_weight = settled(up_a, w_up.shape, 1, 0, None)
-    qkv_both_a = staying(cut(normed_own, 0), mixed_grad, qkv_sent_a)
-    qkv_cross_a = swap_x(qkv_both_a)
-    up_b = crossed(up_both_b, up_cross_b)
-    small = small + swap_row(small)
-    qkv_both_b = staying(cut(normed_own, 1), mixed_grad, qkv_sent_b)
-    qkv_cross_b = swap_x(qkv_both_b)
+    ends_next = line_step(ends, 1)
+    out_both = staying(attended, grad_own, out_sent)
+    out_cross = swap_x(out_both)
+    ends = step(lambda ends, arrived: pair(col % 2, ends, arrived, 0), ends, ends_next)
+    ends_next = line_step(ends, 2)
+    qkv_weight_grad = settled(qkv_a, w_qkv.shape, 1, 0, None)
+    sums = (sums + sums_next) / (cols * width)
+    tokens_grad = step(
+        lambda sums, total: inv_scale
+        * (total * gain_here - sums[0][:, None] - normal * sums[1][:, None])
+        + f32(cotangent),
+        sums, norm_grad,
+    )
+
+    def gather_small(small, other, shared, ends, arrived):
+        return jnp.concatenate(
+            [
+                pair(core, small[: hidden // 128], other[: hidden // 128], 0),
+                pair(core, small[hidden // 128 : shared_at], other[hidden // 128 : shared_at], 0),
+                shared[:res_at],
+                pair(col // 2, ends, arrived, 0).reshape(-1, 128),
+            ]
+        )
+
+    small = step(gather_small, small, small_other, shared, ends, ends_next)
+    small_next = swap_row(small)
+    qkv_b = crossed(qkv_both_b, qkv_cross_b)
+    small = step(jnp.add, small, small_next)
+    small_next = swap_x(small)
     out_mine = crossed(out_both, out_cross)
-    up_weight_grad = settled(up_b, w_up.shape, 1, up_both_a.shape[0], up_grad_weight)
+    qkv_weight_grad = settled(qkv_b, w_qkv.shape, 1, qkv_both_a.shape[0], qkv_weight_grad)
     out_grad = settled(out_mine, w_out.shape, 0, 0, None)
-    qkv_a = crossed(qkv_both_a, qkv_cross_a)
-    qkv_weight_grad = settled(qkv_a, w_qkv.shape, 1, 0, None)
-    small = step(jnp.add, small, swap_x(small))
-    qkv_b = crossed(qkv_both_b, qkv_cross_b)
-    qkv_weight_grad = settled(qkv_b, w_qkv.shape, 1, qkv_both_a.shape[0], qkv_weight_grad)
+    small = step(jnp.add, small, small_next)
 
     bounds = [0, 2 * hidden // 128, (2 * hidden + 6 * heads_width) // 128]
     bounds.append(bounds[-1] + res_at)

time: 507 us -> 464 us (0.915)
  waiting for transfers between devices: 182 us -> 131 us
  between operations: 1.83 us -> 15.3 us
  local copies, waits for them, and re-layouts: 45.5 us -> 34.6 us
  matrix products: 80.3 us -> 86.2 us
    ppermute x12, waiting for transfers between devices: 48.4 us -> 22.9 us  [swap_x(): return lax.ppermute(values, 'dp', SWAP_X)]
    ppermute x1, waiting for transfers between devices: 24.8 us -> 0.01 us  [paired_device(): trunk_sent = lax.ppermute(trunk_grad, 'row', [(1, 0)])]
    unnamed x123 -> x113, local copies, waits for them, and re-layouts: 16.6 us -> 2.69 us
    ppermute x12, waiting for transfers between devices: 56.1 us -> 67.5 us  [swap_row(): return lax.ppermute(values, 'row', SWAP_ROW)]
    all_to_all x4 -> x3, waiting for transfers between devices: 46.4 us -> 39.2 us  [exchange(): return lax.all_to_all(stack, 'col', 0, 0, tiled=True)]
    dot_general x22, matrix products: 80.3 us -> 86.2 us  [matmul(): lax.dot_general(left, right, (dims, ((), ())), preferred_element_type=jnp...]
    all_to_all x4 -> x3, starting transfers between devices: 20.1 us -> 15.9 us  [exchange(): return lax.all_to_all(stack, 'col', 0, 0, tiled=True)]
  transfers between devices with their start and end apart: 47 -> 47, of which waited for: 19 -> 14; matrix products, arithmetic and copies ran while one was open for 25% -> 30% of each run, Pallas kernels for 20% -> 22%
where the time goes in v3:
time: 464 us; the launch traced here: 456 us
  waiting for transfers between devices  131 us (28%)
  Pallas kernels  106 us (23%)
  matrix products  86.2 us (19%)
  starting transfers between devices  58.8 us (13%)
  local copies, waits for them, and re-layouts  34.6 us (7%)
  other arithmetic  23.7 us (5%)
  between operations  15.3 us (3%)
    dot_general x22, matrix products, matmul(): lax.dot_general(left, right, (dims, ((), ())), preferred_element_type=jnp...  86.2 us
    ppermute x12, waiting for transfers between devices, swap_row(): return lax.ppermute(values, 'row', SWAP_ROW)  67.5 us
    all_to_all x3, waiting for transfers between devices, exchange(): return lax.all_to_all(stack, 'col', 0, 0, tiled=True)  39.2 us
    pallas_call x7, Pallas kernels, settle(): pl.pallas_call(settle_kernel, grid_spec=pltpu.PrefetchScalarGridSpec(num_...  33.7 us
    ppermute x12, waiting for transfers between devices, swap_x(): return lax.ppermute(values, 'dp', SWAP_X)  22.9 us
    pallas_call x1, Pallas kernels, tree_attention(): pl.pallas_call(tree_kernel, grid_spec=pltpu.PrefetchScalarGridSpec(num_sc...  18.6 us
    pallas_call x4, Pallas kernels, cast_weight(): pl.pallas_call(cast_rows_kernel if axis == 0 else cast_cols_kernel, grid_...  18.4 us
    ppermute x12, starting transfers between devices, swap_row(): return lax.ppermute(values, 'row', SWAP_ROW)  16.3 us
  transfers between devices with their start and end apart: 47, of which 14 were waited for; matrix products, arithmetic and copies ran while one was open for 30% of the time, Pallas kernels for 22%

profile of v3, /device:TPU:0, one launch (start us, length us, event | category | flops | bytes accessed | tf_op | source)
XLA Modules:
  0.0 456.0 jit_solution(16687534210750771663)
XLA Ops:
  9.7 6.3 %all-to-all-start = ((bf16[4,512,512]{2,1,0:T(8,128)(2,1)}), bf16[4,512,512]{2,1,0:T(8,128)(2,1)S(1)}, u32[]{:S(2)}, u32[]{:S(2)}) async-start(bf16[4,512,512]{2,1,0:T(8,128)(2,1)} %broadcast_in_dim.76), calls=%async_computation | async-start | bytes 4194304 | tf_op jit(solution)/shard_map/all_to_all | solution.py:839
  23.4 5.3 %cast_weight.5 = (bf16[2048,1024]{1,0:T(8,128)(2,1)}, bf16[512,1024]{1,0:T(8,128)(2,1)}) custom-call(s32[4]{0:T(128)} %pad_add_fusion.1.place_ref, f32[1024,2048]{1,0:T(8,128)} %master_ref.1), custom_call_target="tpu_custom_call" | custom-call | flops 1 | bytes 1 | tf_op jit(solution)/shard_map/cast_weight/pallas_call | solution.py:665
  29.2 13.2 %collective-permute-done.1 = bf16[512,768]{1,0:T(8,128)(2,1)} collective-permute-done((bf16[512,768]{1,0:T(8,128)(2,1)}, bf16[512,768]{1,0:T(8,128)(2,1)}, u32[]{:S(2)}, u32[]{:S(2)}) %collective-permute-start.1) | collective-permute-done | bytes 786464 | tf_op jit(solution)/shard_map/ppermute | solution.py:335
  50.1 5.3 %cast_weight.7 = (bf16[1024,2048]{1,0:T(8,128)(2,1)}, bf16[1024,512]{1,0:T(8,128)(2,1)}) custom-call(s32[4]{0:T(128)} %pad_add_fusion.1.place_ref, f32[2048,1024]{1,0:T(8,128)} %master_ref.3), custom_call_target="tpu_custom_call" | custom-call | flops 1 | bytes 1 | tf_op jit(solution)/shard_map/cast_weight/pallas_call | solution.py:665
  55.4 8.0 %collective-permute-done.3 = bf16[512,1024]{1,0:T(8,128)(2,1)S(1)} collective-permute-done((bf16[512,1024]{1,0:T(8,128)(2,1)}, bf16[512,1024]{1,0:T(8,128)(2,1)S(1)}, u32[]{:S(2)}, u32[]{:S(2)}) %collective-permute-start.3) | collective-permute-done | bytes 1048608 | tf_op jit(solution)/shard_map/ppermute | solution.py:335
  63.4 34.6 %all-to-all-done.mine_ref = bf16[4,512,512]{2,1,0:T(8,128)(2,1)S(1)} async-done(((bf16[4,512,512]{2,1,0:T(8,128)(2,1)}), bf16[4,512,512]{2,1,0:T(8,128)(2,1)S(1)}, u32[]{:S(2)}, u32[]{:S(2)}) %all-to-all-start) | async-done | bytes 2097184 | tf_op jit(solution)/shard_map/all_to_all | solution.py:839
  107.4 8.6 %norm_blocks.1 = (bf16[2,512,2048]{2,1,0:T(8,128)(2,1)}, bf16[2,512,1024]{2,1,0:T(8,128)(2,1)}, f32[512,512]{1,0:T(8,128)}, f32[512,1]{1,0:T(8,128)}) custom-call(s32[4]{0:T(128)} %pad_add_fusion.1.place_ref, f32[4,512]{1,0:T(4,128)} %reshape.187.gain_ref, f32[4,512]{1,0:T(4,128)} %reshape.188.bias_ref, bf16[4,512,512]{2,1,0:T(8,128)(2,1)} %copy-done.3, ...), custom_call_target="tpu_custom_call" | custom-call | flops 1 | bytes 1 | tf_op jit(solution)/shard_map/norm_blocks/pallas_call | solution.py:580
  120.2 8.2 %convolution_add_fusion.2.mixed_ref = f32[1024,768]{1,0:T(8,128)} fusion(bf16[1024,2048]{1,0:T(8,128)(2,1)} %bitcast.83, bf16[2048,768]{1,0:T(8,128)(2,1)} %constant_dynamic-update-slice_fusion.11, f32[768]{0:T(1024)S(1)} %dynamic_slice.17), kind=kOutput, calls=%fused_computation.21 | convolution fusion | flops 3222011904 | bytes 10488832 | tf_op jit(solution)/shard_map/dot_general | solution.py:331
  143.5 10.1 %add_convert_fusion = (bf16[1024,1024]{1,0:T(8,128)(2,1)}, bf16[1024,1024]{1,0:T(8,128)(2,1)S(1)}) fusion(f32[1024]{0:T(1024)S(1)} %dynamic-slice-done, bf16[1024,2048]{1,0:T(8,128)(2,1)S(1)} %bitcast.84, bf16[2048,1024]{1,0:T(8,128)(2,1)} %constant_dynamic-update-slice_fusion.9), kind=kOutput, calls=%fused_computation.9 | convolution fusion | flops 4315938816 | bytes 12587008 | tf_op jit(solution)/shard_map/dot_general | solution.py:331
  155.3 6.2 %join_blocks.1 = (bf16[2,512,2048]{2,1,0:T(8,128)(2,1)}, bf16[2,512,1024]{2,1,0:T(8,128)(2,1)}) custom-call(s32[4]{0:T(128)} %pad_add_fusion.1.place_ref, bf16[4,512,512]{2,1,0:T(8,128)(2,1)} %bitcast.81, bf16[4,512,512]{2,1,0:T(8,128)(2,1)} %collective-permute-done.7.theirs_ref), custom_call_target="tpu_custom_call" | custom-call | flops 1 | bytes 1 | tf_op jit(solution)/shard_map/join_blocks/pallas_call | solution.py:580
  176.1 18.6 %tree_attention.1 = (bf16[1024,256]{1,0:T(8,128)(2,1)}, f32[1024,256]{1,0:T(8,128)}, f32[1024,512]{1,0:T(8,128)}, bf16[1024,512]{1,0:T(8,128)(2,1)}) custom-call(s32[2,4]{1,0:T(2,128)} %bitcast.100, s32[1]{0:T(128)} %bitcast.1.row_ref, bf16[1024,256]{1,0:T(8,128)(2,1)} %get-tuple-element.226.query_ref, bf16[1024,512]{1,0:T(8,128)(2,1)} %get-tuple-element.227.keyval_ref, ...), custom_call_target="tpu_custom_call" | custom-call | flops 1 | bytes 1 | tf_op jit(solution)/shard_map/tree_attention/pallas_call | solution.py:775
  205.7 7.2 %convert_reduce_fusion.2 = (f32[1024]{0:T(1024)S(1)}, bf16[1024,1024]{1,0:T(8,128)(2,1)S(1)}) fusion(bf16[1024,1024]{1,0:T(8,128)(2,1)S(1)} %copy-done.53, bf16[1024,2048]{1,0:T(8,128)(2,1)S(1)} %bitcast.88, bf16[1024,2048]{1,0:T(8,128)(2,1)} %constant_dynamic-update-slice_fusion.5), kind=kOutput, calls=%fused_computation.6 | convolution fusion | flops 4300209152 | bytes 12587008 | tf_op jit(solution)/shard_map/dot_general | solution.py:331
  235.4 5.2 %settle.7.refs_0_ = f32[2048,1024]{1,0:T(8,128)} custom-call(s32[4]{0:T(128)} %pad_add_fusion.1.place_ref, bf16[512,1024]{1,0:T(8,128)(2,1)} %copy-done.19, bf16[512,1024]{1,0:T(8,128)(2,1)} %collective-permute-done.17.theirs_ref), custom_call_target="tpu_custom_call" | custom-call | flops 1 | bytes 1 | tf_op jit(solution)/shard_map/settle/pallas_call | solution.py:715
  240.6 5.4 %join_heads.1 = bf16[1024,768]{1,0:T(8,128)(2,1)} custom-call(s32[1]{0:T(128)} %bitcast.1.row_ref, f32[1024,256]{1,0:T(8,128)} %get-tuple-element.258.dq_ref, f32[1024,512]{1,0:T(8,128)} %get-tuple-element.259.dkv_ref, bf16[1024,512]{1,0:T(8,128)(2,1)} %collective-permute-done.16.sent_ref, f32[1024,128]{1,0:T(8,128)} %get-tuple-element.187.cos_ref, ...), custom_call_target="tpu_custom_call" | custom-call | flops 1 | bytes 1 | tf_op jit(solution)/shard_map/join_heads/pallas_call | solution.py:754
  262.6 5.2 %settle.8 = f32[2048,1024]{1,0:T(8,128)} custom-call(s32[4]{0:T(128)} %pad_add_fusion.1.place_ref, bf16[512,1024]{1,0:T(8,128)(2,1)} %copy-done.21, bf16[512,1024]{1,0:T(8,128)(2,1)} %collective-permute-done.18.theirs_ref, f32[2048,1024]{1,0:T(8,128)} %settle.7.refs_0_), custom_call_target="tpu_custom_call", output_to_operand_aliasing={{}: (3, {})} | custom-call | flops 1 | bytes 1 | tf_op jit(solution)/shard_map/settle/pallas_call | solution.py:715
  267.8 11.1 %collective-permute-done.20 = bf16[512,1024]{1,0:T(8,128)(2,1)} collective-permute-done((bf16[512,1024]{1,0:T(8,128)(2,1)}, bf16[512,1024]{1,0:T(8,128)(2,1)}, u32[]{:S(2)}, u32[]{:S(2)}) %collective-permute-start.20) | collective-permute-done | bytes 1048608 | tf_op jit(solution)/shard_map/ppermute | solution.py:335
  286.9 6.9 %convolution_add_fusion.1.terms_ref = f32[1024,2048]{1,0:T(8,128)} fusion(f32[1024,2048]{1,0:T(8,128)S(1)} %fusion.36, bf16[1024,1024]{1,0:T(8,128)(2,1)S(1)} %copy-done.5, bf16[2048,1024]{1,0:T(8,128)(2,1)S(1)} %copy-done.51), kind=kOutput, calls=%fused_computation.11 | convolution fusion | flops 4297064448 | bytes 23068672 | tf_op jit(solution)/shard_map/dot_general | solution.py:331
  293.8 5.3 %stack_blocks.2 = bf16[4,512,512]{2,1,0:T(8,128)(2,1)} custom-call(s32[4]{0:T(128)} %pad_add_fusion.1.place_ref, f32[1024,2048]{1,0:T(8,128)} %convolution_add_fusion.terms_ref, bf16[512,2048]{1,0:T(8,128)(2,1)} %collective-permute-done.19.arrived_ref), custom_call_target="tpu_custom_call" | custom-call | flops 1 | bytes 1 | tf_op jit(solution)/shard_map/stack_blocks/pallas_call | solution.py:608
  310.0 19.9 %collective-permute-done.21 = bf16[512,1024]{1,0:T(8,128)(2,1)S(1)} collective-permute-done((bf16[512,1024]{1,0:T(8,128)(2,1)}, bf16[512,1024]{1,0:T(8,128)(2,1)S(1)}, u32[]{:S(2)}, u32[]{:S(2)}) %collective-permute-start.21) | collective-permute-done | bytes 1048608 | tf_op jit(solution)/shard_map/ppermute | solution.py:335
  335.0 10.3 %collective-permute-done.26 = bf16[512,768]{1,0:T(8,128)(2,1)S(1)} collective-permute-done((bf16[512,768]{1,0:T(8,128)(2,1)S(1)}, bf16[512,768]{1,0:T(8,128)(2,1)S(1)}, u32[]{:S(2)}, u32[]{:S(2)}) %collective-permute-start.26) | collective-permute-done | bytes 786464 | tf_op jit(solution)/shard_map/ppermute | solution.py:335
  347.2 5.3 %stack_blocks.3 = bf16[4,512,512]{2,1,0:T(8,128)(2,1)} custom-call(s32[4]{0:T(128)} %pad_add_fusion.1.place_ref, f32[1024,2048]{1,0:T(8,128)} %convolution_add_fusion.1.terms_ref, bf16[512,2048]{1,0:T(8,128)(2,1)} %collective-permute-done.25.arrived_ref), custom_call_target="tpu_custom_call" | custom-call | flops 1 | bytes 1 | tf_op jit(solution)/shard_map/stack_blocks/pallas_call | solution.py:608
  364.3 5.3 %settle.9.refs_0_ = f32[1024,2048]{1,0:T(8,128)} custom-call(s32[4]{0:T(128)} %pad_add_fusion.1.place_ref, bf16[512,1024]{1,0:T(8,128)(2,1)} %add_convert_fusion.2.mine_ref, bf16[512,1024]{1,0:T(8,128)(2,1)} %collective-permute-done.24.theirs_ref), custom_call_target="tpu_custom_call" | custom-call | flops 1 | bytes 1 | tf_op jit(solution)/shard_map/settle/pallas_call | solution.py:715
  369.7 13.9 %collective-permute-done.22 = bf16[512,1024]{1,0:T(8,128)(2,1)} collective-permute-done((bf16[512,1024]{1,0:T(8,128)(2,1)}, bf16[512,1024]{1,0:T(8,128)(2,1)}, u32[]{:S(2)}, u32[]{:S(2)}) %collective-permute-start.22) | collective-permute-done | bytes 1048608 | tf_op jit(solution)/shard_map/ppermute | solution.py:339
  395.0 5.2 %settle.10 = f32[1024,2048]{1,0:T(8,128)} custom-call(s32[4]{0:T(128)} %pad_add_fusion.1.place_ref, bf16[512,1024]{1,0:T(8,128)(2,1)} %copy-done.20, bf16[512,1024]{1,0:T(8,128)(2,1)} %collective-permute-done.27.theirs_ref, f32[1024,2048]{1,0:T(8,128)} %settle.9.refs_0_), custom_call_target="tpu_custom_call", output_to_operand_aliasing={{}: (3, {})} | custom-call | flops 1 | bytes 1 | tf_op jit(solution)/shard_map/settle/pallas_call | solution.py:715
  (297 shorter events, 210.1 us)
Async XLA Ops:
  9.7 88.2 %all-to-all-start = ((bf16[4,512,512]{2,1,0:T(8,128)(2,1)}), bf16[4,512,512]{2,1,0:T(8,128)(2,1)S(1)}, u32[]{:S(2)}, u32[]{:S(2)}) async-start(bf16[4,512,512]{2,1,0:T(8,128)(2,1)} %broadcast_in_dim.76), calls=%async_computation | async-start | bytes 4194304 | tf_op jit(solution)/shard_map/all_to_all | solution.py:839
  16.0 87.5 %all-gather.3.cloned.1.call-start = ((), (), s32[]{:S(2)}) async-start(), calls=%async_computation.3 | async-start | bytes 2621440 | tf_op jit(solution)/shard_map/all_gather | solution.py:857
  28.7 34.7 %collective-permute-start.3 = (bf16[512,1024]{1,0:T(8,128)(2,1)}, bf16[512,1024]{1,0:T(8,128)(2,1)S(1)}, u32[]{:S(2)}, u32[]{:S(2)}) collective-permute-start(bf16[512,1024]{1,0:T(8,128)(2,1)} %get-tuple-element.179), channel_id=1, source_target_pairs={{0,4},{4,0},{1,5},{5,1},{2,6},{6,2},{3,7},{7,3},{8,12},{12,8},{9,1... | collective-permute-start | bytes 3145736 | tf_op jit(solution)/shard_map/ppermute | solution.py:335
  101.3 52.3 %collective-permute-start.8 = (bf16[1024,512]{1,0:T(8,128)(2,1)}, bf16[1024,512]{1,0:T(8,128)(2,1)}, u32[]{:S(2)}, u32[]{:S(2)}) collective-permute-start(bf16[1024,512]{1,0:T(8,128)(2,1)} %get-tuple-element.186), channel_id=1, source_target_pairs={{0,4},{4,0},{1,5},{5,1},{2,6},{6,2},{3,7},{7,3},{8,12},{12,8},{9,1... | collective-permute-start | bytes 3145736 | tf_op jit(solution)/shard_map/ppermute | solution.py:335
  102.0 37.5 %collective-permute-start.9 = (bf16[512,1024]{1,0:T(8,128)(2,1)S(1)}, bf16[512,1024]{1,0:T(8,128)(2,1)}, u32[]{:S(2)}, u32[]{:S(2)}) collective-permute-start(bf16[512,1024]{1,0:T(8,128)(2,1)S(1)} %collective-permute-done.3), channel_id=1, source_target_pairs={{0,16},{16,0},{8,24},{24,8},{1,17},{17,1},{9,25},{25,9},{2,18},{18... | collective-permute-start | bytes 3145736 | tf_op jit(solution)/shard_map/ppermute | solution.py:339
  103.5 51.8 %collective-permute-start.7 = (bf16[4,512,512]{2,1,0:T(8,128)(2,1)}, bf16[4,512,512]{2,1,0:T(8,128)(2,1)}, u32[]{:S(2)}, u32[]{:S(2)}) collective-permute-start(bf16[4,512,512]{2,1,0:T(8,128)(2,1)} %bitcast.80), channel_id=1, source_target_pairs={{0,8},{8,0},{16,24},{24,16},{1,9},{9,1},{17,25},{25,17},{2,10},{10... | collective-permute-start | bytes 6291464 | tf_op jit(solution)/shard_map/ppermute | solution.py:343
  128.4 43.2 %collective-permute-start.10 = (bf16[256,512]{1,0:T(8,128)(2,1)S(1)}, bf16[256,512]{1,0:T(8,128)(2,1)}, u32[]{:S(2)}, u32[]{:S(2)}) collective-permute-start(bf16[256,512]{1,0:T(8,128)(2,1)S(1)} %collective-permute-done.5), channel_id=1, source_target_pairs={{0,16},{16,0},{8,24},{24,8},{1,17},{17,1},{9,25},{25,9},{2,18},{18... | collective-permute-start | bytes 786440 | tf_op jit(solution)/shard_map/ppermute | solution.py:339
  134.9 41.2 %collective-permute-start.6 = (bf16[1024,512]{1,0:T(8,128)(2,1)}, bf16[1024,512]{1,0:T(8,128)(2,1)}, u32[]{:S(2)}, u32[]{:S(2)}) collective-permute-start(bf16[1024,512]{1,0:T(8,128)(2,1)} %get-tuple-element.227.keyval_ref), channel_id=1, source_target_pairs={{0,4},{1,5},{2,6},{3,7},{8,12},{9,13},{10,14},{11,15},{16,20},{17,... | collective-permute-start | bytes 3145736 | tf_op jit(solution)/shard_map/ppermute | solution.py:904
  153.6 47.5 %collective-permute-start.11 = (bf16[1024,512]{1,0:T(8,128)(2,1)}, bf16[1024,512]{1,0:T(8,128)(2,1)}, u32[]{:S(2)}, u32[]{:S(2)}) collective-permute-start(bf16[1024,512]{1,0:T(8,128)(2,1)} %collective-permute-done.8), channel_id=1, source_target_pairs={{0,16},{16,0},{8,24},{24,8},{1,17},{17,1},{9,25},{25,9},{2,18},{18... | collective-permute-start | bytes 3145736 | tf_op jit(solution)/shard_map/ppermute | solution.py:339
  165.8 30.2 %collective-permute-start.12 = (bf16[512,1024]{1,0:T(8,128)(2,1)}, bf16[512,1024]{1,0:T(8,128)(2,1)}, u32[]{:S(2)}, u32[]{:S(2)}) collective-permute-start(bf16[512,1024]{1,0:T(8,128)(2,1)} %convolution_convert_fusion.3), channel_id=1, source_target_pairs={{0,4},{4,0},{1,5},{5,1},{2,6},{6,2},{3,7},{7,3},{8,12},{12,8},{9,1... | collective-permute-start | bytes 3145736 | tf_op jit(solution)/shard_map/ppermute | solution.py:335
  169.6 45.6 %collective-permute-start.14 = (bf16[512,1024]{1,0:T(8,128)(2,1)}, bf16[512,1024]{1,0:T(8,128)(2,1)}, u32[]{:S(2)}, u32[]{:S(2)}) collective-permute-start(bf16[512,1024]{1,0:T(8,128)(2,1)} %convolution_convert_fusion.2), channel_id=1, source_target_pairs={{0,4},{4,0},{1,5},{5,1},{2,6},{6,2},{3,7},{7,3},{8,12},{12,8},{9,1... | collective-permute-start | bytes 3145736 | tf_op jit(solution)/shard_map/ppermute | solution.py:335
  194.7 45.9 %collective-permute-start.16 = (bf16[1024,512]{1,0:T(8,128)(2,1)}, bf16[1024,512]{1,0:T(8,128)(2,1)}, u32[]{:S(2)}, u32[]{:S(2)}) collective-permute-start(bf16[1024,512]{1,0:T(8,128)(2,1)} %get-tuple-element.233), channel_id=1, source_target_pairs={{4,0},{5,1},{6,2},{7,3},{12,8},{13,9},{14,10},{15,11},{20,16},{21,... | collective-permute-start | bytes 3145736 | tf_op jit(solution)/shard_map/ppermute | solution.py:950
  199.6 26.1 %collective-permute-start.13 = (bf16[512,1024]{1,0:T(8,128)(2,1)S(1)}, bf16[512,1024]{1,0:T(8,128)(2,1)S(1)}, u32[]{:S(2)}, u32[]{:S(2)}) collective-permute-start(bf16[512,1024]{1,0:T(8,128)(2,1)S(1)} %add_convert_fusion.8), channel_id=1, source_target_pairs={{0,16},{16,0},{8,24},{24,8},{1,17},{17,1},{9,25},{25,9},{2,18},{18... | collective-permute-start | bytes 3145736 | tf_op jit(solution)/shard_map/ppermute | solution.py:339
  219.4 29.6 %collective-permute-start.15 = (bf16[512,1024]{1,0:T(8,128)(2,1)}, bf16[512,1024]{1,0:T(8,128)(2,1)}, u32[]{:S(2)}, u32[]{:S(2)}) collective-permute-start(bf16[512,1024]{1,0:T(8,128)(2,1)} %add_convert_fusion.7), channel_id=1, source_target_pairs={{0,16},{16,0},{8,24},{24,8},{1,17},{17,1},{9,25},{25,9},{2,18},{18... | collective-permute-start | bytes 3145736 | tf_op jit(solution)/shard_map/ppermute | solution.py:339
  251.5 27.4 %collective-permute-start.20 = (bf16[512,1024]{1,0:T(8,128)(2,1)}, bf16[512,1024]{1,0:T(8,128)(2,1)}, u32[]{:S(2)}, u32[]{:S(2)}) collective-permute-start(bf16[512,1024]{1,0:T(8,128)(2,1)} %convolution_convert_fusion.1), channel_id=1, source_target_pairs={{0,4},{4,0},{1,5},{5,1},{2,6},{6,2},{3,7},{7,3},{8,12},{12,8},{9,1... | collective-permute-start | bytes 3145736 | tf_op jit(solution)/shard_map/ppermute | solution.py:335
  267.8 26.0 %collective-permute-start.19 = (bf16[512,2048]{1,0:T(8,128)(2,1)}, bf16[512,2048]{1,0:T(8,128)(2,1)}, u32[]{:S(2)}, u32[]{:S(2)}) collective-permute-start(bf16[512,2048]{1,0:T(8,128)(2,1)} %slice.122), channel_id=1, source_target_pairs={{0,8},{8,0},{16,24},{24,16},{1,9},{9,1},{17,25},{25,17},{2,10},{10... | collective-permute-start | bytes 6291464 | tf_op jit(solution)/shard_map/ppermute | solution.py:343
  299.1 53.5 %all-to-all-start.1 = ((bf16[4,512,512]{2,1,0:T(8,128)(2,1)}), bf16[4,512,512]{2,1,0:T(8,128)(2,1)}, u32[]{:S(2)}, u32[]{:S(2)}) async-start(bf16[4,512,512]{2,1,0:T(8,128)(2,1)} %stack_blocks.2), calls=%async_computation.1 | async-start | bytes 4194304 | tf_op jit(solution)/shard_map/all_to_all | solution.py:839
  303.6 26.3 %collective-permute-start.21 = (bf16[512,1024]{1,0:T(8,128)(2,1)}, bf16[512,1024]{1,0:T(8,128)(2,1)S(1)}, u32[]{:S(2)}, u32[]{:S(2)}) collective-permute-start(bf16[512,1024]{1,0:T(8,128)(2,1)} %convolution_convert_fusion), channel_id=1, source_target_pairs={{0,4},{4,0},{1,5},{5,1},{2,6},{6,2},{3,7},{7,3},{8,12},{12,8},{9,1... | collective-permute-start | bytes 3145736 | tf_op jit(solution)/shard_map/ppermute | solution.py:335
  307.9 39.3 %collective-permute-start.25 = (bf16[512,2048]{1,0:T(8,128)(2,1)S(1)}, bf16[512,2048]{1,0:T(8,128)(2,1)}, u32[]{:S(2)}, u32[]{:S(2)}) collective-permute-start(bf16[512,2048]{1,0:T(8,128)(2,1)S(1)} %slice.125), channel_id=1, source_target_pairs={{0,8},{8,0},{16,24},{24,16},{1,9},{9,1},{17,25},{25,17},{2,10},{10... | collective-permute-start | bytes 6291464 | tf_op jit(solution)/shard_map/ppermute | solution.py:343
  309.5 35.8 %collective-permute-start.26 = (bf16[512,768]{1,0:T(8,128)(2,1)S(1)}, bf16[512,768]{1,0:T(8,128)(2,1)S(1)}, u32[]{:S(2)}, u32[]{:S(2)}) collective-permute-start(bf16[512,768]{1,0:T(8,128)(2,1)S(1)} %convolution_convert_fusion.5), channel_id=1, source_target_pairs={{0,4},{4,0},{1,5},{5,1},{2,6},{6,2},{3,7},{7,3},{8,12},{12,8},{9,1... | collective-permute-start | bytes 2359304 | tf_op jit(solution)/shard_map/ppermute | solution.py:335
  352.5 52.3 %all-to-all-start.2 = ((bf16[4,512,512]{2,1,0:T(8,128)(2,1)}), bf16[4,512,512]{2,1,0:T(8,128)(2,1)}, u32[]{:S(2)}, u32[]{:S(2)}) async-start(bf16[4,512,512]{2,1,0:T(8,128)(2,1)} %stack_blocks.3), calls=%async_computation.2 | async-start | bytes 4194304 | tf_op jit(solution)/shard_map/all_to_all | solution.py:839
  357.7 25.9 %collective-permute-start.22 = (bf16[512,1024]{1,0:T(8,128)(2,1)}, bf16[512,1024]{1,0:T(8,128)(2,1)}, u32[]{:S(2)}, u32[]{:S(2)}) collective-permute-start(bf16[512,1024]{1,0:T(8,128)(2,1)} %add_convert_fusion.3), channel_id=1, source_target_pairs={{0,16},{16,0},{8,24},{24,8},{1,17},{17,1},{9,25},{25,9},{2,18},{18... | collective-permute-start | bytes 3145736 | tf_op jit(solution)/shard_map/ppermute | solution.py:339
  359.6 31.8 %collective-permute-start.28 = (bf16[512,768]{1,0:T(8,128)(2,1)}, bf16[512,768]{1,0:T(8,128)(2,1)}, u32[]{:S(2)}, u32[]{:S(2)}) collective-permute-start(bf16[512,768]{1,0:T(8,128)(2,1)} %convolution_convert_fusion.4), channel_id=1, source_target_pairs={{0,4},{4,0},{1,5},{5,1},{2,6},{6,2},{3,7},{7,3},{8,12},{12,8},{9,1... | collective-permute-start | bytes 2359304 | tf_op jit(solution)/shard_map/ppermute | solution.py:335
  394.5 32.3 %collective-permute-start.36 = (bf16[512,768]{1,0:T(8,128)(2,1)}, bf16[512,768]{1,0:T(8,128)(2,1)}, u32[]{:S(2)}, u32[]{:S(2)}) collective-permute-start(bf16[512,768]{1,0:T(8,128)(2,1)} %add_convert_fusion.11), channel_id=1, source_target_pairs={{0,16},{16,0},{8,24},{24,8},{1,17},{17,1},{9,25},{25,9},{2,18},{18... | collective-permute-start | bytes 2359304 | tf_op jit(solution)/shard_map/ppermute | solution.py:339
  (78 other events, 822.7 us)
Sparse Core Ops, SparseCore 0:
  23.4 74.0 all-gather.2

commit v4 on v3

--- a/solution.py
+++ b/solution.py
@@ -559,7 +559,7 @@
 
 def gathered(place, mine, theirs, norm=None):
     blocks, count, width = mine.shape
-    rows = SEG // 2
+    rows = SEG if norm is None else SEG // 2
     full = blocks * width
     in_specs = [pl.BlockSpec((blocks, rows, width), lambda at, *_: (0, at, 0))] * 2
     out_specs = [pair_rows(rows, full), pair_rows(rows, full // 2)]
@@ -603,7 +603,7 @@
 
 def stacked(place, terms, arrived, blocks):
     count, full = arrived.shape
-    rows = SEG // 2
+    rows = SEG
     width = full // blocks
     return pl.pallas_call(
         stack_kernel,
@@ -638,7 +638,7 @@
 
 def cast_weight(place, master, axis):
     height, width = master.shape
-    rows = SEG
+    rows = min(2 * SEG, master.shape[0] // 4)
     if axis == 0:
         width = width // 2
         steps = height // rows
@@ -676,36 +676,29 @@
     )(place, master)
 
 
-def settle_kernel(place_ref, mine_ref, theirs_ref, *refs):
+def settle_kernel(axis, place_ref, mine_ref, theirs_ref, *refs):
     out_ref = refs[-1]
-
-    @pl.when(pl.program_id(0) == 0)
-    def _():
-        out_ref[...] = f32(mine_ref[...])
-
-    @pl.when(pl.program_id(0) == 1)
-    def _():
-        out_ref[...] = f32(theirs_ref[...])
+    mine, theirs = f32(mine_ref[...]), f32(theirs_ref[...])
+    if axis == 0:
+        out_ref[place_ref[3]] = mine
+        out_ref[1 - place_ref[3]] = theirs
+    else:
+        width = mine.shape[1]
+        first = place_ref[3] == 0
+        out_ref[:, :width] = jnp.where(first, mine, theirs)
+        out_ref[:, width:] = jnp.where(first, theirs, mine)
 
 
 def settle(place, mine, theirs, shape, axis, offset, dest=None):
-    rows, width = SEG, mine.shape[1]
-    steps = mine.shape[0] // rows
-    first = offset // rows
-    per_core = shape[0] // 2 // rows
-
-    def whose(turn, place_ref):
-        return place_ref[3] + turn - 2 * place_ref[3] * turn
-
-    def out_at(turn, at, place_ref):
-        if axis == 0:
-            return (whose(turn, place_ref) * per_core + first + at, 0)
-        return (first + at, whose(turn, place_ref))
-
-    in_specs = [
-        pl.BlockSpec((rows, width), lambda turn, at, place_ref: (jnp.where(turn == 0, at, steps - 1), 0)),
-        pl.BlockSpec((rows, width), lambda turn, at, place_ref: (jnp.where(turn == 0, 0, at), 0)),
-    ]
+    rows, width = mine.shape
+    at = offset // rows
+    whole = pl.BlockSpec((rows, width), lambda *_: (0, 0))
+    if axis == 0:
+        shape = (2, shape[0] // 2, width)
+        out_spec = pl.BlockSpec((2, rows, width), lambda *_: (0, at, 0))
+    else:
+        out_spec = pl.BlockSpec((rows, 2 * width), lambda *_: (at, 0))
+    in_specs = [whole, whole]
     operands = [place, mine, theirs]
     aliases = {}
     if dest is not None:
@@ -713,12 +706,9 @@
         operands.append(dest)
         aliases = {3: 0}
     return pl.pallas_call(
-        settle_kernel,
+        functools.partial(settle_kernel, axis),
         grid_spec=pltpu.PrefetchScalarGridSpec(
-            num_scalar_prefetch=1,
-            grid=(2, steps),
-            in_specs=in_specs,
-            out_specs=pl.BlockSpec((rows, width), out_at),
+            num_scalar_prefetch=1, grid=(1,), in_specs=in_specs, out_specs=out_spec
         ),
         out_shape=jax.ShapeDtypeStruct(shape, jnp.float32),
         input_output_aliases=aliases,
@@ -733,7 +723,7 @@
 
 def split_heads(mixed, tables):
     count, width = mixed.shape
-    rows = SEG
+    rows = 2 * SEG
     return pl.pallas_call(
         split_kernel,
         grid=(count // rows,),
@@ -750,7 +740,7 @@
 
 def join_heads(row, dq, dkv, sent, tables):
     count, half = dq.shape
-    rows = SEG
+    rows = 2 * SEG
     return pl.pallas_call(
         join_kernel,
         grid_spec=pltpu.PrefetchScalarGridSpec(
@@ -853,8 +843,7 @@
     def wait(value):
         return step(lambda arrived: arrived, value)
 
-    tokens_near = to_all(tokens)
-    grad_near = lax.all_gather(cotangent, "col", axis=0)
+    tokens_near = lax.all_gather(tokens, "col", axis=0)
 
     def ready(master, axis):
         whole, send = step(lambda weight: cast_weight(place, weight, axis), master)
@@ -889,6 +878,7 @@
     qkv_x = wait(qkv_x)
     tokens_near = wait(tokens_near)
     tokens_far = swap_core(tokens_near)
+    grad_near = to_all(after(cotangent, tokens_near))
     out_row = wait(out_row)
     out_x = swap_x(out_row)
     normed, normed_plain, normal, inv_scale = step(
@@ -960,37 +950,36 @@
     branch_terms = step(
         lambda a, b, c, d: matmul(a, b) + matmul(c, d), attended, out_full, activated, down_full
     )
-    down_grad = settled(down_a, w_down.shape, 0, 0, None)
+    branch_near = swap_core(step(bf16, branch_terms[count:]))
     mixed_grad = step(
         lambda *operands: join_heads(row_table, *operands, rotary), query_grad, own_grad, trunk_sent
     )
     qkv_sent_a = swap_row(leaving(cut(normed_plain, 0), mixed_grad))
     down_b = crossed(down_both_b, down_cross_b)
     qkv_sent_b = swap_row(leaving(cut(normed_plain, 1), mixed_grad))
-    down_grad = settled(down_b, w_down.shape, 0, down_both_a.shape[0], down_grad)
-    branch_near = swap_core(step(bf16, branch_terms[count:]))
-    up_both_a = staying(cut(normed_own, 0), up_grad, up_sent_a)
-    up_cross_a = swap_x(up_both_a)
     norm_terms = step(
         lambda a, b, c, d: matmul(a, b, across) + matmul(c, d, across),
         mixed_grad, qkv_full, up_grad, up_full,
     )
-    branch_parts = exchange(step(lambda a, b: stacked(place, a, b, cols), branch_terms, branch_near))
+    branch = lax.psum_scatter(
+        step(lambda a, b: stacked(place, a, b, cols), branch_terms, branch_near), "col", tiled=False
+    )
+    up_both_a = staying(cut(normed_own, 0), up_grad, up_sent_a)
+    up_cross_a = swap_x(up_both_a)
     norm_near = swap_core(step(bf16, norm_terms[count:]))
+    down_grad = settled(down_a, w_down.shape, 0, 0, None)
+    norm_parts = exchange(step(lambda a, b: stacked(place, a, b, cols), norm_terms, norm_near))
     up_both_b = staying(cut(normed_own, 1), up_grad, up_sent_b)
     up_cross_b = swap_x(up_both_b)
+    down_grad = settled(down_b, w_down.shape, 0, down_both_a.shape[0], down_grad)
     up_a = crossed(up_both_a, up_cross_a)
     qkv_both_a = staying(cut(normed_own, 0), mixed_grad, qkv_sent_a)
     qkv_cross_a = swap_x(qkv_both_a)
-    norm_parts = exchange(step(lambda a, b: stacked(place, a, b, cols), norm_terms, norm_near))
     out_sent = swap_row(leaving(attended, grad_plain))
-    up_weight_grad = settled(up_a, w_up.shape, 1, 0, None)
     up_b = crossed(up_both_b, up_cross_b)
-    output = step(
-        lambda parts, block: bf16(f32(block) + jnp.sum(f32(parts), axis=0) + b_res), branch_parts, tokens
-    )
     qkv_both_b = staying(cut(normed_own, 1), mixed_grad, qkv_sent_b)
     qkv_cross_b = swap_x(qkv_both_b)
+    up_weight_grad = settled(up_a, w_up.shape, 1, 0, None)
     up_weight_grad = settled(up_b, w_up.shape, 1, up_both_a.shape[0], up_weight_grad)
     gain_here = part(ln_gain, col, width, 0)
 
@@ -1053,6 +1042,7 @@
             ]
         )
 
+    output = step(lambda parts, block: bf16(f32(block) + f32(parts) + b_res), branch, tokens)
     small = step(gather_small, small, small_other, shared, ends, ends_next)
     small_next = swap_row(small)
     qkv_b = crossed(qkv_both_b, qkv_cross_b)
@@ -1076,10 +1066,10 @@
         tokens_grad,
         qkv_weight_grad,
         qkv_bias_grad,
-        out_grad,
+        out_grad.reshape(w_out.shape),
         up_weight_grad,
         up_bias_grad,
-        down_grad,
+        down_grad.reshape(w_down.shape),
         res_bias_grad,
         gain_grad,
         shift_grad,

time: 464 us -> 413 us (0.89)
  waiting for transfers between devices: 131 us -> 74.2 us
  Pallas kernels: 106 us -> 97.8 us
  local copies, waits for them, and re-layouts: 34.6 us -> 39.5 us
    ppermute x12, waiting for transfers between devices: 67.5 us -> 33 us  [swap_row(): return lax.ppermute(values, 'row', SWAP_ROW)]
    ppermute x12, waiting for transfers between devices: 22.9 us -> 8.17 us  [swap_x(): return lax.ppermute(values, 'dp', SWAP_X)]
    all_to_all x3 -> x2, waiting for transfers between devices: 39.2 us -> 28.7 us  [exchange(): return lax.all_to_all(stack, 'col', 0, 0, tiled=True)]
    ppermute x12, starting transfers between devices: 16.3 us -> 26.4 us  [swap_row(): return lax.ppermute(values, 'row', SWAP_ROW)]
    all_to_all x3 -> x2, starting transfers between devices: 15.9 us -> 8.78 us  [exchange(): return lax.all_to_all(stack, 'col', 0, 0, tiled=True)]
    unnamed x113 -> x109, local copies, waits for them, and re-layouts: 2.69 us -> 9.58 us
    convert_element_type x8, other arithmetic: 10.7 us -> 16.8 us  [bf16(): return values.astype(jnp.bfloat16)]
  transfers between devices with their start and end apart: 47 -> 47, of which waited for: 14 -> 13; matrix products, arithmetic and copies ran while one was open for 30% -> 35% of each run, Pallas kernels for 22% -> 24%
where the time goes in v4:
time: 413 us; the launch traced here: 405 us
  Pallas kernels  97.8 us (24%)
  matrix products  90.7 us (22%)
  waiting for transfers between devices  74.2 us (18%)
  starting transfers between devices  61.3 us (15%)
  local copies, waits for them, and re-layouts  39.5 us (10%)
  other arithmetic  26.5 us (6%)
  between operations  15.1 us (4%)
    dot_general x22, matrix products, matmul(): lax.dot_general(left, right, (dims, ((), ())), preferred_element_type=jnp...  90.7 us
    ppermute x12, waiting for transfers between devices, swap_row(): return lax.ppermute(values, 'row', SWAP_ROW)  33 us
    pallas_call x7, Pallas kernels, settle(): pl.pallas_call(functools.partial(settle_kernel, axis), grid_spec=pltpu.Pr...  29.9 us
    all_to_all x2, waiting for transfers between devices, exchange(): return lax.all_to_all(stack, 'col', 0, 0, tiled=True)  28.7 us
    ppermute x12, starting transfers between devices, swap_row(): return lax.ppermute(values, 'row', SWAP_ROW)  26.4 us
    pallas_call x1, Pallas kernels, tree_attention(): pl.pallas_call(tree_kernel, grid_spec=pltpu.PrefetchScalarGridSpec(num_sc...  18 us
    pallas_call x4, Pallas kernels, cast_weight(): pl.pallas_call(cast_rows_kernel if axis == 0 else cast_cols_kernel, grid_...  17.4 us
    convert_element_type x8, other arithmetic, bf16(): return values.astype(jnp.bfloat16)  16.8 us
  transfers between devices with their start and end apart: 47, of which 13 were waited for; matrix products, arithmetic and copies ran while one was open for 35% of the time, Pallas kernels for 24%

profile of v4, /device:TPU:0, one launch (start us, length us, event | category | flops | bytes accessed | tf_op | source)
XLA Modules:
  0.0 405.2 jit_solution(6273183133538011242)
XLA Ops:
  8.6 5.0 %cast_weight.4 = (bf16[2048,768]{1,0:T(8,128)(2,1)}, bf16[512,768]{1,0:T(8,128)(2,1)}) custom-call(s32[4]{0:T(128)} %pad_add_fusion.1.place_ref, f32[1024,1536]{1,0:T(8,128)} %master_ref), custom_call_target="tpu_custom_call" | custom-call | flops 1 | bytes 1 | tf_op jit(solution)/shard_map/cast_weight/pallas_call | solution.py:665
  16.7 5.3 %cast_weight.5 = (bf16[2048,1024]{1,0:T(8,128)(2,1)}, bf16[512,1024]{1,0:T(8,128)(2,1)}) custom-call(s32[4]{0:T(128)} %pad_add_fusion.1.place_ref, f32[1024,2048]{1,0:T(8,128)} %master_ref.1), custom_call_target="tpu_custom_call" | custom-call | flops 1 | bytes 1 | tf_op jit(solution)/shard_map/cast_weight/pallas_call | solution.py:665
  22.1 13.1 %collective-permute-done.1 = bf16[512,768]{1,0:T(8,128)(2,1)S(1)} collective-permute-done((bf16[512,768]{1,0:T(8,128)(2,1)}, bf16[512,768]{1,0:T(8,128)(2,1)S(1)}, u32[]{:S(2)}, u32[]{:S(2)}) %collective-permute-start.1) | collective-permute-done | bytes 786464 | tf_op jit(solution)/shard_map/ppermute | solution.py:335
  47.6 9.2 %collective-permute-done.3 = bf16[512,1024]{1,0:T(8,128)(2,1)S(1)} collective-permute-done((bf16[512,1024]{1,0:T(8,128)(2,1)}, bf16[512,1024]{1,0:T(8,128)(2,1)S(1)}, u32[]{:S(2)}, u32[]{:S(2)}) %collective-permute-start.3) | collective-permute-done | bytes 1048608 | tf_op jit(solution)/shard_map/ppermute | solution.py:335
  73.3 8.6 %norm_blocks.1 = (bf16[2,512,2048]{2,1,0:T(8,128)(2,1)}, bf16[2,512,1024]{2,1,0:T(8,128)(2,1)}, f32[512,512]{1,0:T(8,128)}, f32[512,1]{1,0:T(8,128)}) custom-call(s32[4]{0:T(128)} %pad_add_fusion.1.place_ref, f32[4,512]{1,0:T(4,128)} %reshape.193.gain_ref, f32[4,512]{1,0:T(4,128)} %reshape.194.bias_ref, bf16[4,512,512]{2,1,0:T(8,128)(2,1)} %bitcast.85, ...), custom_call_target="tpu_custom_call" | custom-call | flops 1 | bytes 1 | tf_op jit(solution)/shard_map/norm_blocks/pallas_call | solution.py:580
  86.1 8.2 %convolution_add_fusion.2.mixed_ref = f32[1024,768]{1,0:T(8,128)} fusion(bf16[1024,2048]{1,0:T(8,128)(2,1)} %bitcast.88, bf16[2048,768]{1,0:T(8,128)(2,1)} %constant_dynamic-update-slice_fusion.11, f32[768]{0:T(1024)S(1)} %dynamic_slice.17), kind=kOutput, calls=%fused_computation.20 | convolution fusion | flops 3222011904 | bytes 10488832 | tf_op jit(solution)/shard_map/dot_general | solution.py:331
  100.0 4.6 %collective-permute-start.6 = (bf16[1024,512]{1,0:T(8,128)(2,1)}, bf16[1024,512]{1,0:T(8,128)(2,1)}, u32[]{:S(2)}, u32[]{:S(2)}) collective-permute-start(bf16[1024,512]{1,0:T(8,128)(2,1)} %get-tuple-element.229.keyval_ref), channel_id=1, source_target_pairs={{0,4},{1,5},{2,6},{3,7},{8,12},{9,13},{10,14},{11,15},{16,20},{17,... | collective-permute-start | bytes 3145736 | tf_op jit(solution)/shard_map/ppermute | solution.py:894
  106.9 5.7 %all-to-all-done.mine_ref = bf16[4,512,512]{2,1,0:T(8,128)(2,1)S(1)} async-done(((bf16[4,512,512]{2,1,0:T(8,128)(2,1)}), bf16[4,512,512]{2,1,0:T(8,128)(2,1)S(1)}, u32[]{:S(2)}, u32[]{:S(2)}) %all-to-all-start) | async-done | bytes 2097184 | tf_op jit(solution)/shard_map/all_to_all | solution.py:829
  115.6 11.6 %add_convert_fusion = (bf16[1024,1024]{1,0:T(8,128)(2,1)}, bf16[1024,1024]{1,0:T(8,128)(2,1)S(1)}) fusion(f32[1024]{0:T(1024)S(1)} %dynamic-slice-done, bf16[1024,2048]{1,0:T(8,128)(2,1)} %bitcast.89, bf16[2048,1024]{1,0:T(8,128)(2,1)} %constant_dynamic-update-slice_fusion.9), kind=kOutput, calls=%fused_computation.8 | convolution fusion | flops 4315938816 | bytes 12587008 | tf_op jit(solution)/shard_map/dot_general | solution.py:331
  130.7 5.8 %join_blocks.1 = (bf16[2,512,2048]{2,1,0:T(8,128)(2,1)}, bf16[2,512,1024]{2,1,0:T(8,128)(2,1)}) custom-call(s32[4]{0:T(128)} %pad_add_fusion.1.place_ref, bf16[4,512,512]{2,1,0:T(8,128)(2,1)} %copy-done.7, bf16[4,512,512]{2,1,0:T(8,128)(2,1)} %collective-permute-done.7.theirs_ref), custom_call_target="tpu_custom_call" | custom-call | flops 1 | bytes 1 | tf_op jit(solution)/shard_map/join_blocks/pallas_call | solution.py:580
  152.6 18.0 %tree_attention.1 = (bf16[1024,256]{1,0:T(8,128)(2,1)}, f32[1024,256]{1,0:T(8,128)}, f32[1024,512]{1,0:T(8,128)}, bf16[1024,512]{1,0:T(8,128)(2,1)}) custom-call(s32[2,4]{1,0:T(2,128)} %bitcast.106, s32[1]{0:T(128)} %bitcast.1.row_ref, bf16[1024,256]{1,0:T(8,128)(2,1)} %get-tuple-element.228.query_ref, bf16[1024,512]{1,0:T(8,128)(2,1)} %get-tuple-element.229.keyval_ref, ...), custom_call_target="tpu_custom_call" | custom-call | flops 1 | bytes 1 | tf_op jit(solution)/shard_map/tree_attention/pallas_call | solution.py:765
  181.2 7.3 %convert_reduce_fusion.2 = (f32[1024]{0:T(1024)S(1)}, bf16[1024,1024]{1,0:T(8,128)(2,1)S(1)}) fusion(bf16[1024,1024]{1,0:T(8,128)(2,1)S(1)} %copy-done.51, bf16[1024,2048]{1,0:T(8,128)(2,1)S(1)} %bitcast.93, bf16[1024,2048]{1,0:T(8,128)(2,1)} %constant_dynamic-update-slice_fusion.5), kind=kOutput, calls=%fused_computation.6 | convolution fusion | flops 4300209152 | bytes 12587008 | tf_op jit(solution)/shard_map/dot_general | solution.py:331
  214.1 4.5 %join_heads.1 = bf16[1024,768]{1,0:T(8,128)(2,1)} custom-call(s32[1]{0:T(128)} %bitcast.1.row_ref, f32[1024,256]{1,0:T(8,128)} %get-tuple-element.259.dq_ref, f32[1024,512]{1,0:T(8,128)} %get-tuple-element.260.dkv_ref, bf16[1024,512]{1,0:T(8,128)(2,1)} %collective-permute-done.16.sent_ref, f32[1024,128]{1,0:T(8,128)} %get-tuple-element.188.cos_ref, ...), custom_call_target="tpu_custom_call" | custom-call | flops 1 | bytes 1 | tf_op jit(solution)/shard_map/join_heads/pallas_call | solution.py:744
  227.4 5.7 %fusion.36 = f32[1024,2048]{1,0:T(8,128)} fusion(bf16[1024,768]{1,0:T(8,128)(2,1)S(1)} %copy-done.9, bf16[2048,768]{1,0:T(8,128)(2,1)S(1)} %copy-done.50), kind=kOutput, calls=%fused_computation.121 | convolution fusion | flops 3221225472 | bytes 13107200 | tf_op jit(solution)/shard_map/dot_general | solution.py:331
  233.1 7.0 %convolution_add_fusion.1.terms_ref = f32[1024,2048]{1,0:T(8,128)S(1)} fusion(f32[1024,2048]{1,0:T(8,128)} %fusion.36, bf16[1024,1024]{1,0:T(8,128)(2,1)S(1)} %copy-done.6, bf16[2048,1024]{1,0:T(8,128)(2,1)S(1)} %copy-done.49), kind=kOutput, calls=%fused_computation.10 | convolution fusion | flops 4297064448 | bytes 23068672 | tf_op jit(solution)/shard_map/dot_general | solution.py:331
  245.2 4.6 %stack_blocks.2 = bf16[4,512,512]{2,1,0:T(8,128)(2,1)} custom-call(s32[4]{0:T(128)} %pad_add_fusion.1.place_ref, f32[1024,2048]{1,0:T(8,128)} %copy-done, bf16[512,2048]{1,0:T(8,128)(2,1)} %collective-permute-done.15.arrived_ref), custom_call_target="tpu_custom_call" | custom-call | flops 1 | bytes 1 | tf_op jit(solution)/shard_map/stack_blocks/pallas_call | solution.py:608
  249.8 4.5 %add_convert_fusion.4 = bf16[512,1024]{1,0:T(8,128)(2,1)} fusion(bf16[512,1024]{1,0:T(8,128)(2,1)} %collective-permute-done.18, bf16[1024,512]{1,0:T(8,128)(2,1)} %get-tuple-element.290, bf16[1024,1024]{1,0:T(8,128)(2,1)} %copy-done.5), kind=kOutput, calls=%fused_computation.15 | convolution fusion | flops 1075314688 | bytes 5242880 | tf_op jit(solution)/shard_map/dot_general | solution.py:331
  264.8 4.6 %stack_blocks.3 = bf16[4,512,512]{2,1,0:T(8,128)(2,1)} custom-call(s32[4]{0:T(128)} %pad_add_fusion.1.place_ref, f32[1024,2048]{1,0:T(8,128)} %copy-done.2, bf16[512,2048]{1,0:T(8,128)(2,1)} %collective-permute-done.19.arrived_ref), custom_call_target="tpu_custom_call" | custom-call | flops 1 | bytes 1 | tf_op jit(solution)/shard_map/stack_blocks/pallas_call | solution.py:608
  277.8 4.8 %collective-permute-done.21 = bf16[512,1024]{1,0:T(8,128)(2,1)} collective-permute-done((bf16[512,1024]{1,0:T(8,128)(2,1)}, bf16[512,1024]{1,0:T(8,128)(2,1)}, u32[]{:S(2)}, u32[]{:S(2)}) %collective-permute-start.21) | collective-permute-done | bytes 1048608 | tf_op jit(solution)/shard_map/ppermute | solution.py:335
  304.1 8.0 %collective-permute-done.22 = bf16[512,1024]{1,0:T(8,128)(2,1)} collective-permute-done((bf16[512,1024]{1,0:T(8,128)(2,1)}, bf16[512,1024]{1,0:T(8,128)(2,1)}, u32[]{:S(2)}, u32[]{:S(2)}) %collective-permute-start.22) | collective-permute-done | bytes 1048608 | tf_op jit(solution)/shard_map/ppermute | solution.py:339
  322.7 4.7 %settle.9.refs_0_ = f32[1024,2048]{1,0:T(8,128)} custom-call(s32[4]{0:T(128)} %pad_add_fusion.1.place_ref, bf16[512,1024]{1,0:T(8,128)(2,1)} %add_convert_fusion.2.mine_ref, bf16[512,1024]{1,0:T(8,128)(2,1)} %collective-permute-done.27.theirs_ref), custom_call_target="tpu_custom_call" | custom-call | flops 1 | bytes 1 | tf_op jit(solution)/shard_map/settle/pallas_call | solution.py:708
  327.5 4.7 %settle.10 = f32[1024,2048]{1,0:T(8,128)} custom-call(s32[4]{0:T(128)} %pad_add_fusion.1.place_ref, bf16[512,1024]{1,0:T(8,128)(2,1)} %add_convert_fusion.1.mine_ref, bf16[512,1024]{1,0:T(8,128)(2,1)} %collective-permute-done.26.theirs_ref, f32[1024,2048]{1,0:T(8,128)} %settle.9.refs_0_), custom_call_target="tpu_custom_call", output_to_operand_aliasing={{}: (3, {})} | custom-call | flops 1 | bytes 1 | tf_op jit(solution)/shard_map/settle/pallas_call | solution.py:708
  332.2 23.1 %all-to-all-done.1 = bf16[4,512,512]{2,1,0:T(8,128)(2,1)} async-done(((bf16[4,512,512]{2,1,0:T(8,128)(2,1)}), bf16[4,512,512]{2,1,0:T(8,128)(2,1)}, u32[]{:S(2)}, u32[]{:S(2)}) %all-to-all-start.1) | async-done | bytes 2097184 | tf_op jit(solution)/shard_map/all_to_all | solution.py:829
  376.5 5.1 %collective-permute-start.40 = (f32[64,128]{1,0:T(8,128)S(1)}, f32[64,128]{1,0:T(8,128)S(1)}, u32[]{:S(2)}, u32[]{:S(2)}) collective-permute-start(f32[64,128]{1,0:T(8,128)S(1)} %pad_maximum_fusion), channel_id=1, source_target_pairs={{0,4},{4,0},{1,5},{5,1},{2,6},{6,2},{3,7},{7,3},{8,12},{12,8},{9,1... | collective-permute-start | bytes 98312 | tf_op jit(solution)/shard_map/ppermute | solution.py:335
  (293 shorter events, 206.2 us)
Async XLA Ops:
  7.2 50.8 %all-gather.3.cloned.1.call-start = ((), (), s32[]{:S(2)}) async-start(), calls=%async_computation.4 | async-start | bytes 2621440 | tf_op jit(solution)/shard_map/all_gather | solution.py:846
  22.0 34.8 %collective-permute-start.3 = (bf16[512,1024]{1,0:T(8,128)(2,1)}, bf16[512,1024]{1,0:T(8,128)(2,1)S(1)}, u32[]{:S(2)}, u32[]{:S(2)}) collective-permute-start(bf16[512,1024]{1,0:T(8,128)(2,1)} %get-tuple-element.180), channel_id=1, source_target_pairs={{0,4},{4,0},{1,5},{5,1},{2,6},{6,2},{3,7},{7,3},{8,12},{12,8},{9,1... | collective-permute-start | bytes 3145736 | tf_op jit(solution)/shard_map/ppermute | solution.py:335
  59.5 53.0 %all-to-all-start = ((bf16[4,512,512]{2,1,0:T(8,128)(2,1)}), bf16[4,512,512]{2,1,0:T(8,128)(2,1)S(1)}, u32[]{:S(2)}, u32[]{:S(2)}) async-start(bf16[4,512,512]{2,1,0:T(8,128)(2,1)} %broadcast_in_dim.86), calls=%async_computation | async-start | bytes 4194304 | tf_op jit(solution)/shard_map/all_to_all | solution.py:829
  67.2 60.0 %collective-permute-start.8 = (bf16[1024,512]{1,0:T(8,128)(2,1)}, bf16[1024,512]{1,0:T(8,128)(2,1)}, u32[]{:S(2)}, u32[]{:S(2)}) collective-permute-start(bf16[1024,512]{1,0:T(8,128)(2,1)} %get-tuple-element.187), channel_id=1, source_target_pairs={{0,4},{4,0},{1,5},{5,1},{2,6},{6,2},{3,7},{7,3},{8,12},{12,8},{9,1... | collective-permute-start | bytes 3145736 | tf_op jit(solution)/shard_map/ppermute | solution.py:335
  67.7 36.9 %collective-permute-start.9 = (bf16[512,1024]{1,0:T(8,128)(2,1)}, bf16[512,1024]{1,0:T(8,128)(2,1)}, u32[]{:S(2)}, u32[]{:S(2)}) collective-permute-start(bf16[512,1024]{1,0:T(8,128)(2,1)} %copy-done.34), channel_id=1, source_target_pairs={{0,16},{16,0},{8,24},{24,8},{1,17},{17,1},{9,25},{25,9},{2,18},{18... | collective-permute-start | bytes 3145736 | tf_op jit(solution)/shard_map/ppermute | solution.py:339
  94.4 55.1 %collective-permute-start.10 = (bf16[256,512]{1,0:T(8,128)(2,1)S(1)}, bf16[256,512]{1,0:T(8,128)(2,1)}, u32[]{:S(2)}, u32[]{:S(2)}) collective-permute-start(bf16[256,512]{1,0:T(8,128)(2,1)S(1)} %collective-permute-done.5), channel_id=1, source_target_pairs={{0,16},{16,0},{8,24},{24,8},{1,17},{17,1},{9,25},{25,9},{2,18},{18... | collective-permute-start | bytes 786440 | tf_op jit(solution)/shard_map/ppermute | solution.py:339
  100.0 52.5 %collective-permute-start.6 = (bf16[1024,512]{1,0:T(8,128)(2,1)}, bf16[1024,512]{1,0:T(8,128)(2,1)}, u32[]{:S(2)}, u32[]{:S(2)}) collective-permute-start(bf16[1024,512]{1,0:T(8,128)(2,1)} %get-tuple-element.229.keyval_ref), channel_id=1, source_target_pairs={{0,4},{1,5},{2,6},{3,7},{8,12},{9,13},{10,14},{11,15},{16,20},{17,... | collective-permute-start | bytes 3145736 | tf_op jit(solution)/shard_map/ppermute | solution.py:894
  140.6 31.5 %collective-permute-start.12 = (bf16[512,1024]{1,0:T(8,128)(2,1)}, bf16[512,1024]{1,0:T(8,128)(2,1)}, u32[]{:S(2)}, u32[]{:S(2)}) collective-permute-start(bf16[512,1024]{1,0:T(8,128)(2,1)} %convolution_convert_fusion.3), channel_id=1, source_target_pairs={{0,4},{4,0},{1,5},{5,1},{2,6},{6,2},{3,7},{7,3},{8,12},{12,8},{9,1... | collective-permute-start | bytes 3145736 | tf_op jit(solution)/shard_map/ppermute | solution.py:335
  143.7 33.0 %collective-permute-start.11 = (bf16[1024,512]{1,0:T(8,128)(2,1)}, bf16[1024,512]{1,0:T(8,128)(2,1)}, u32[]{:S(2)}, u32[]{:S(2)}) collective-permute-start(bf16[1024,512]{1,0:T(8,128)(2,1)} %collective-permute-done.8), channel_id=1, source_target_pairs={{0,16},{16,0},{8,24},{24,8},{1,17},{17,1},{9,25},{25,9},{2,18},{18... | collective-permute-start | bytes 3145736 | tf_op jit(solution)/shard_map/ppermute | solution.py:339
  148.9 45.5 %collective-permute-start.14 = (bf16[512,1024]{1,0:T(8,128)(2,1)}, bf16[512,1024]{1,0:T(8,128)(2,1)}, u32[]{:S(2)}, u32[]{:S(2)}) collective-permute-start(bf16[512,1024]{1,0:T(8,128)(2,1)} %convolution_convert_fusion.2), channel_id=1, source_target_pairs={{0,4},{4,0},{1,5},{5,1},{2,6},{6,2},{3,7},{7,3},{8,12},{12,8},{9,1... | collective-permute-start | bytes 3145736 | tf_op jit(solution)/shard_map/ppermute | solution.py:335
  170.6 43.5 %collective-permute-start.16 = (bf16[1024,512]{1,0:T(8,128)(2,1)}, bf16[1024,512]{1,0:T(8,128)(2,1)}, u32[]{:S(2)}, u32[]{:S(2)}) collective-permute-start(bf16[1024,512]{1,0:T(8,128)(2,1)} %get-tuple-element.235), channel_id=1, source_target_pairs={{4,0},{5,1},{6,2},{7,3},{12,8},{13,9},{14,10},{15,11},{20,16},{21,... | collective-permute-start | bytes 3145736 | tf_op jit(solution)/shard_map/ppermute | solution.py:940
  175.7 25.6 %collective-permute-start.13 = (bf16[512,1024]{1,0:T(8,128)(2,1)S(1)}, bf16[512,1024]{1,0:T(8,128)(2,1)S(1)}, u32[]{:S(2)}, u32[]{:S(2)}) collective-permute-start(bf16[512,1024]{1,0:T(8,128)(2,1)S(1)} %add_convert_fusion.8), channel_id=1, source_target_pairs={{0,16},{16,0},{8,24},{24,8},{1,17},{17,1},{9,25},{25,9},{2,18},{18... | collective-permute-start | bytes 3145736 | tf_op jit(solution)/shard_map/ppermute | solution.py:339
  190.8 59.0 %collective-permute-start.18 = (bf16[512,1024]{1,0:T(8,128)(2,1)}, bf16[512,1024]{1,0:T(8,128)(2,1)}, u32[]{:S(2)}, u32[]{:S(2)}) collective-permute-start(bf16[512,1024]{1,0:T(8,128)(2,1)} %convolution_convert_fusion.1), channel_id=1, source_target_pairs={{0,4},{4,0},{1,5},{5,1},{2,6},{6,2},{3,7},{7,3},{8,12},{12,8},{9,1... | collective-permute-start | bytes 3145736 | tf_op jit(solution)/shard_map/ppermute | solution.py:335
  214.1 31.1 %collective-permute-start.15 = (bf16[512,2048]{1,0:T(8,128)(2,1)}, bf16[512,2048]{1,0:T(8,128)(2,1)}, u32[]{:S(2)}, u32[]{:S(2)}) collective-permute-start(bf16[512,2048]{1,0:T(8,128)(2,1)} %slice.122), channel_id=1, source_target_pairs={{0,8},{8,0},{16,24},{24,16},{1,9},{9,1},{17,25},{25,17},{2,10},{10... | collective-permute-start | bytes 6291464 | tf_op jit(solution)/shard_map/ppermute | solution.py:343
  254.8 27.8 %collective-permute-start.21 = (bf16[512,1024]{1,0:T(8,128)(2,1)}, bf16[512,1024]{1,0:T(8,128)(2,1)}, u32[]{:S(2)}, u32[]{:S(2)}) collective-permute-start(bf16[512,1024]{1,0:T(8,128)(2,1)} %convolution_convert_fusion), channel_id=1, source_target_pairs={{0,4},{4,0},{1,5},{5,1},{2,6},{6,2},{3,7},{7,3},{8,12},{12,8},{9,1... | collective-permute-start | bytes 3145736 | tf_op jit(solution)/shard_map/ppermute | solution.py:335
  258.3 32.0 %collective-permute-start.25 = (bf16[512,1024]{1,0:T(8,128)(2,1)}, bf16[512,1024]{1,0:T(8,128)(2,1)}, u32[]{:S(2)}, u32[]{:S(2)}) collective-permute-start(bf16[512,1024]{1,0:T(8,128)(2,1)} %add_convert_fusion.5.mine_ref), channel_id=1, source_target_pairs={{0,8},{8,0},{16,24},{24,16},{1,9},{9,1},{17,25},{25,17},{2,10},{10... | collective-permute-start | bytes 3145736 | tf_op jit(solution)/shard_map/ppermute | solution.py:343
  258.5 36.3 %collective-permute-start.24 = (bf16[512,1024]{1,0:T(8,128)(2,1)}, bf16[512,1024]{1,0:T(8,128)(2,1)}, u32[]{:S(2)}, u32[]{:S(2)}) collective-permute-start(bf16[512,1024]{1,0:T(8,128)(2,1)} %add_convert_fusion.4), channel_id=1, source_target_pairs={{0,16},{16,0},{8,24},{24,8},{1,17},{17,1},{9,25},{25,9},{2,18},{18... | collective-permute-start | bytes 3145736 | tf_op jit(solution)/shard_map/ppermute | solution.py:339
  269.4 85.8 %all-to-all-start.1 = ((bf16[4,512,512]{2,1,0:T(8,128)(2,1)}), bf16[4,512,512]{2,1,0:T(8,128)(2,1)}, u32[]{:S(2)}, u32[]{:S(2)}) async-start(bf16[4,512,512]{2,1,0:T(8,128)(2,1)} %stack_blocks.3), calls=%async_computation.2 | async-start | bytes 4194304 | tf_op jit(solution)/shard_map/all_to_all | solution.py:829
  273.9 100.5 %reduce-scatter.2.cloned.1.call-start = ((), (), s32[]{:S(2)}) async-start(), calls=%async_computation.3 | async-start | bytes 2621440 | tf_op jit(solution)/shard_map/reduce_scatter | solution.py:964
  274.2 25.2 %collective-permute-start.23 = (bf16[512,768]{1,0:T(8,128)(2,1)}, bf16[512,768]{1,0:T(8,128)(2,1)}, u32[]{:S(2)}, u32[]{:S(2)}) collective-permute-start(bf16[512,768]{1,0:T(8,128)(2,1)} %convolution_convert_fusion.5), channel_id=1, source_target_pairs={{0,4},{4,0},{1,5},{5,1},{2,6},{6,2},{3,7},{7,3},{8,12},{12,8},{9,1... | collective-permute-start | bytes 2359304 | tf_op jit(solution)/shard_map/ppermute | solution.py:335
  288.3 29.6 %collective-permute-start.28 = (bf16[512,768]{1,0:T(8,128)(2,1)}, bf16[512,768]{1,0:T(8,128)(2,1)}, u32[]{:S(2)}, u32[]{:S(2)}) collective-permute-start(bf16[512,768]{1,0:T(8,128)(2,1)} %convolution_convert_fusion.4), channel_id=1, source_target_pairs={{0,4},{4,0},{1,5},{5,1},{2,6},{6,2},{3,7},{7,3},{8,12},{12,8},{9,1... | collective-permute-start | bytes 2359304 | tf_op jit(solution)/shard_map/ppermute | solution.py:335
  315.8 46.3 %collective-permute-start.35 = (bf16[256,1024]{1,0:T(8,128)(2,1)}, bf16[256,1024]{1,0:T(8,128)(2,1)}, u32[]{:S(2)}, u32[]{:S(2)}) collective-permute-start(bf16[256,1024]{1,0:T(8,128)(2,1)} %convolution_convert_fusion.6), channel_id=1, source_target_pairs={{0,4},{4,0},{1,5},{5,1},{2,6},{6,2},{3,7},{7,3},{8,12},{12,8},{9,1... | collective-permute-start | bytes 1572872 | tf_op jit(solution)/shard_map/ppermute | solution.py:335
  317.3 41.1 %collective-permute-start.31 = (bf16[512,768]{1,0:T(8,128)(2,1)}, bf16[512,768]{1,0:T(8,128)(2,1)}, u32[]{:S(2)}, u32[]{:S(2)}) collective-permute-start(bf16[512,768]{1,0:T(8,128)(2,1)} %add_convert_fusion.12), channel_id=1, source_target_pairs={{0,16},{16,0},{8,24},{24,8},{1,17},{17,1},{9,25},{25,9},{2,18},{18... | collective-permute-start | bytes 2359304 | tf_op jit(solution)/shard_map/ppermute | solution.py:339
  321.2 60.4 %collective-permute-start.36 = (bf16[512,768]{1,0:T(8,128)(2,1)}, bf16[512,768]{1,0:T(8,128)(2,1)}, u32[]{:S(2)}, u32[]{:S(2)}) collective-permute-start(bf16[512,768]{1,0:T(8,128)(2,1)} %add_convert_fusion.11), channel_id=1, source_target_pairs={{0,16},{16,0},{8,24},{24,8},{1,17},{17,1},{9,25},{25,9},{2,18},{18... | collective-permute-start | bytes 2359304 | tf_op jit(solution)/shard_map/ppermute | solution.py:339
  (76 other events, 609.5 us)
Sparse Core Ops, SparseCore 0:
  9.6 48.3 all-gather.2
  290.4 64.2 reduce-scatter.1
